TPU v7x, 32 devices: a whole 2x2x4 slice. The times are simulated.
32 devices in a mesh: clip: 2 (over y), wide: 8 (over z, core), tp: 2 (over x).
Axes of the slice: x: 2, y: 2, z: 4, core: 2. Of those that a mesh axis runs over, the one named last changes fastest.
Arguments:
- frames_a: bfloat16 [4, 16, 256, 1024], P('clip', 'wide'), may hold values from -6 to 6
- frames_b: bfloat16 [4, 16, 64, 1024], P('clip', 'wide'), may hold values from -6 to 6
- actions_a: int32 [4, 16], P('clip', 'wide'), may hold values from 0 to 7
- actions_b: int32 [4, 16], P('clip', 'wide'), may hold values from 0 to 7
- action_table: bfloat16 [8, 1024], replicated, may hold values from -3 to 3
- gain_space: float32 [1024], replicated, may hold values from 0.5 to 1.5
- space_qkv: bfloat16 [3, 1024, 1024], P(None, None, 'tp'), may hold values from -0.1875 to 0.1875
- space_out: bfloat16 [1024, 1024], P('tp'), may hold values from -0.5 to 0.5
- gain_time: float32 [1024], replicated, may hold values from 0.5 to 1.5
- time_qkv: bfloat16 [3, 1024, 1024], P(None, None, 'tp'), may hold values from -0.1875 to 0.1875
- time_out: bfloat16 [1024, 1024], P('tp'), may hold values from -0.25 to 0.25
- gain_ffn: float32 [1024], replicated, may hold values from 0.5 to 1.5
- ffn_up: bfloat16 [1024, 4096], P(None, 'tp'), may hold values from -0.1875 to 0.1875
- ffn_down: bfloat16 [4096, 1024], P('tp'), may hold values from -0.09375 to 0.09375
- cot_a: bfloat16 [4, 16, 256, 1024], P('clip', 'wide'), may hold values from -6 to 6
- cot_b: bfloat16 [4, 16, 64, 1024], P('clip', 'wide'), may hold values from -6 to 6
Outputs:
- out_a: bfloat16 [4, 16, 256, 1024], P('clip', 'wide')
- out_b: bfloat16 [4, 16, 64, 1024], P('clip', 'wide')
- d_frames_a: bfloat16 [4, 16, 256, 1024], P('clip', 'wide')
- d_frames_b: bfloat16 [4, 16, 64, 1024], P('clip', 'wide')
- d_action_table: float32 [8, 1024], P(None, 'wide')
- d_gain_space: float32 [1024], P('wide')
- d_space_qkv: float32 [3, 1024, 1024], P(None, 'wide', 'tp')
- d_space_out: float32 [1024, 1024], P('tp', 'wide')
- d_gain_time: float32 [1024], P('wide')
- d_time_qkv: float32 [3, 1024, 1024], P(None, 'wide', 'tp')
- d_time_out: float32 [1024, 1024], P('tp', 'wide')
- d_gain_ffn: float32 [1024], P('wide')
- d_ffn_up: float32 [1024, 4096], P('wide', 'tp')
- d_ffn_down: float32 [4096, 1024], P('tp', 'wide')
All inputs are finite; a program needn't handle non-finite values.
Results may differ from a plain program's by a relative error of at most 0.03.
Values may be sent and summed in bfloat16 or wider, within the bound.
No kernel may reach another device: no remote copies, remote signals or barrier semaphores. Data moves between devices by JAX's collectives and lax.ppermute only.
A program may use at most 192 MiB of HBM per device.

v0:
```python
from functools import partial

import jax
import jax.numpy as jnp
from jax import lax
from jax.sharding import PartitionSpec as P

HEAD = 64


def layer_norm(values, gain_vec):
    centered = values - jnp.mean(values, -1, keepdims=True)
    spread = jnp.mean(centered * centered, -1, keepdims=True)
    return centered * lax.rsqrt(spread + 1e-05) * gain_vec


def causal_mask(length):
    return lax.broadcasted_iota(jnp.int32, (length, length), 0) >= lax.broadcasted_iota(
        jnp.int32, (length, length), 1
    )


def score_block(query, keys, causal):
    scores = jnp.einsum(
        "nqphe,nkphe->nphqk", query, keys, preferred_element_type=jnp.float32
    ) * query.shape[-1] ** (-0.5)
    if causal:
        scores = jnp.where(causal_mask(keys.shape[1]), scores, -1e30)
    return scores


def attend(query, keys, values, causal):
    scores = score_block(query, keys, causal)
    largest = jnp.max(scores, -1, keepdims=True)
    shifted = jnp.exp(scores - largest)
    totals = jnp.sum(shifted, -1, keepdims=True)
    soft_low = (shifted / totals).astype(jnp.bfloat16)
    head_out = jnp.einsum(
        "nphqk,nkphe->nqphe", soft_low, values, preferred_element_type=jnp.float32
    )
    return (head_out.astype(jnp.bfloat16), largest + jnp.log(totals))


def attend_back(query, keys, values, log_total, d_out, causal):
    scale_factor = query.shape[-1] ** (-0.5)
    weights_soft = jnp.exp(score_block(query, keys, causal) - log_total)
    d_soft = jnp.einsum("nqphe,nkphe->nphqk", d_out, values, preferred_element_type=jnp.float32)
    row_dot = jnp.sum(weights_soft * d_soft, -1, keepdims=True)
    d_scores = (weights_soft * (d_soft - row_dot)).astype(jnp.bfloat16)
    d_query = (
        jnp.einsum("nphqk,nkphe->nqphe", d_scores, keys, preferred_element_type=jnp.float32)
        * scale_factor
    ).astype(jnp.bfloat16)
    d_keys = (
        jnp.einsum("nphqk,nqphe->nkphe", d_scores, query, preferred_element_type=jnp.float32)
        * scale_factor
    ).astype(jnp.bfloat16)
    d_values = jnp.einsum(
        "nphqk,nqphe->nkphe",
        weights_soft.astype(jnp.bfloat16),
        d_out,
        preferred_element_type=jnp.float32,
    ).astype(jnp.bfloat16)
    return (d_query, d_keys, d_values)


def attention_forward(residual, gain_vec, weight_qkv, weight_out, causal):
    normed = layer_norm(residual, gain_vec).astype(jnp.bfloat16)
    projected = jnp.einsum(
        "nlpd,tde->tnlpe", normed, weight_qkv, preferred_element_type=jnp.float32
    ).astype(jnp.bfloat16)
    split_heads = projected.reshape(projected.shape[:4] + (projected.shape[4] // HEAD, HEAD))
    head_out, log_total = attend(split_heads[0], split_heads[1], split_heads[2], causal)
    flat_heads = head_out.reshape(normed.shape[:3] + (-1,))
    branch_part = jnp.einsum(
        "nlpe,ed->nlpd", flat_heads, weight_out, preferred_element_type=jnp.float32
    )
    return (branch_part, (normed, split_heads, flat_heads, log_total))


def attention_backward(d_branch, kept, weight_qkv, weight_out, causal):
    normed, split_heads, flat_heads, log_total = kept
    grad_out = jnp.einsum("nlpe,nlpd->ed", flat_heads, d_branch, preferred_element_type=jnp.float32)
    d_flat = jnp.einsum(
        "nlpd,ed->nlpe", d_branch, weight_out, preferred_element_type=jnp.float32
    ).astype(jnp.bfloat16)
    d_query, d_keys, d_values = attend_back(
        split_heads[0],
        split_heads[1],
        split_heads[2],
        log_total,
        d_flat.reshape(split_heads.shape[1:]),
        causal,
    )
    d_projected = jnp.stack([d_query, d_keys, d_values]).reshape(split_heads.shape[:4] + (-1,))
    grad_qkv = jnp.einsum(
        "nlpd,tnlpe->tde", normed, d_projected, preferred_element_type=jnp.float32
    )
    d_normed = jnp.einsum(
        "tnlpe,tde->nlpd", d_projected, weight_qkv, preferred_element_type=jnp.float32
    )
    return (d_normed, grad_qkv, grad_out)


def settle(partials, residuals):
    sums = (
        lax.psum(partials[0].astype(jnp.bfloat16), "tp").astype(jnp.float32),
        lax.psum(partials[1].astype(jnp.bfloat16), "tp").astype(jnp.float32),
    )
    return tuple(
        ((residual + summed).astype(jnp.bfloat16) for residual, summed in zip(residuals, sums))
    )


def per_device(
    frames_a,
    frames_b,
    actions_a,
    actions_b,
    action_table,
    gain_space,
    space_qkv,
    space_out,
    gain_time,
    time_qkv,
    time_out,
    gain_ffn,
    ffn_up,
    ffn_down,
    cot_a,
    cot_b,
):
    model_width = frames_a.shape[-1]
    table_wide = action_table.astype(jnp.float32)
    action_codes = lax.broadcasted_iota(jnp.int32, (1, 1, action_table.shape[0]), 2)
    one_hots = [
        (actions[:, :, None] == action_codes).astype(jnp.float32)
        for actions in (actions_a, actions_b)
    ]
    starts = [
        frames.astype(jnp.float32) + jnp.einsum("cfa,ad->cfd", one_hot, table_wide)[:, :, None, :]
        for frames, one_hot in zip((frames_a, frames_b), one_hots)
    ]
    space_fwd = [
        attention_forward(
            begun.reshape((-1, begun.shape[2], 1, model_width)),
            gain_space,
            space_qkv,
            space_out,
            False,
        )
        for begun in starts
    ]
    middles = settle(
        (space_fwd[0][0].reshape(starts[0].shape), space_fwd[1][0].reshape(starts[1].shape)), starts
    )
    on_grid = (
        lax.all_to_all(middles[0], "wide", split_axis=2, concat_axis=1, tiled=True),
        lax.all_to_all(middles[1], "wide", split_axis=2, concat_axis=1, tiled=True),
    )
    grid_wide = [placed.astype(jnp.float32) for placed in on_grid]
    time_fwd = [
        attention_forward(placed, gain_time, time_qkv, time_out, True) for placed in grid_wide
    ]
    latest = settle((time_fwd[0][0], time_fwd[1][0]), grid_wide)
    on_frames = (
        lax.all_to_all(latest[0], "wide", split_axis=1, concat_axis=2, tiled=True),
        lax.all_to_all(latest[1], "wide", split_axis=1, concat_axis=2, tiled=True),
    )
    count_first = on_frames[0].size // model_width
    late_rows = jnp.concatenate(
        [on_frames[0].reshape(-1, model_width), on_frames[1].reshape(-1, model_width)]
    ).astype(jnp.float32)
    normed_ffn = layer_norm(late_rows, gain_ffn).astype(jnp.bfloat16)
    hidden = jnp.dot(normed_ffn, ffn_up, preferred_element_type=jnp.float32)
    gelu_low = jax.nn.gelu(hidden, approximate=True).astype(jnp.bfloat16)
    ffn_part = jnp.dot(gelu_low, ffn_down, preferred_element_type=jnp.float32)
    results = settle(
        (
            ffn_part[:count_first].reshape(on_frames[0].shape),
            ffn_part[count_first:].reshape(on_frames[1].shape),
        ),
        (
            late_rows[:count_first].reshape(on_frames[0].shape),
            late_rows[count_first:].reshape(on_frames[1].shape),
        ),
    )
    cot_rows = jnp.concatenate([cot_a.reshape(-1, model_width), cot_b.reshape(-1, model_width)])
    grad_down = jnp.einsum("rf,rd->fd", gelu_low, cot_rows, preferred_element_type=jnp.float32)
    d_gelu = jnp.einsum("rd,fd->rf", cot_rows, ffn_down, preferred_element_type=jnp.float32)
    _, gelu_pull = jax.vjp(partial(jax.nn.gelu, approximate=True), hidden)
    d_hidden = gelu_pull(d_gelu)[0].astype(jnp.bfloat16)
    grad_up = jnp.einsum("rd,rf->df", normed_ffn, d_hidden, preferred_element_type=jnp.float32)
    d_normed_ffn = lax.psum(
        jnp.einsum("rf,df->rd", d_hidden, ffn_up, preferred_element_type=jnp.float32).astype(
            jnp.bfloat16
        ),
        "tp",
    ).astype(jnp.float32)
    _, norm_pull = jax.vjp(layer_norm, late_rows, gain_ffn)
    d_rows, grad_gain_ffn = norm_pull(d_normed_ffn)
    d_late = (cot_rows.astype(jnp.float32) + d_rows).astype(jnp.bfloat16)
    d_grid = (
        lax.all_to_all(
            d_late[:count_first].reshape(on_frames[0].shape),
            "wide",
            split_axis=2,
            concat_axis=1,
            tiled=True,
        ),
        lax.all_to_all(
            d_late[count_first:].reshape(on_frames[1].shape),
            "wide",
            split_axis=2,
            concat_axis=1,
            tiled=True,
        ),
    )
    time_pieces = [
        attention_backward(d_branch, kept[1], time_qkv, time_out, True)
        for d_branch, kept in zip(d_grid, time_fwd)
    ]
    d_time_normed = (
        lax.psum(time_pieces[0][0].astype(jnp.bfloat16), "tp").astype(jnp.float32),
        lax.psum(time_pieces[1][0].astype(jnp.bfloat16), "tp").astype(jnp.float32),
    )
    d_middle = []
    grad_gain_time = jnp.zeros_like(gain_time)
    for placed, d_norm_part, d_branch in zip(grid_wide, d_time_normed, d_grid):
        _, norm_pull = jax.vjp(layer_norm, placed, gain_time)
        d_residual, d_gain = norm_pull(d_norm_part)
        d_middle.append((d_branch.astype(jnp.float32) + d_residual).astype(jnp.bfloat16))
        grad_gain_time = grad_gain_time + d_gain
    d_frames = (
        lax.all_to_all(d_middle[0], "wide", split_axis=1, concat_axis=2, tiled=True),
        lax.all_to_all(d_middle[1], "wide", split_axis=1, concat_axis=2, tiled=True),
    )
    space_pieces = [
        attention_backward(d_branch.reshape(kept[1][0].shape), kept[1], space_qkv, space_out, False)
        for d_branch, kept in zip(d_frames, space_fwd)
    ]
    d_space_normed = (
        lax.psum(space_pieces[0][0].astype(jnp.bfloat16), "tp").astype(jnp.float32),
        lax.psum(space_pieces[1][0].astype(jnp.bfloat16), "tp").astype(jnp.float32),
    )
    d_inputs = []
    grad_gain_space = jnp.zeros_like(gain_space)
    grad_table = jnp.zeros(action_table.shape, jnp.float32)
    for begun, d_norm_part, d_branch, one_hot in zip(starts, d_space_normed, d_frames, one_hots):
        _, norm_pull = jax.vjp(layer_norm, begun, gain_space)
        d_residual, d_gain = norm_pull(d_norm_part.reshape(begun.shape))
        d_begun = d_branch.astype(jnp.float32) + d_residual
        d_inputs.append(d_begun.astype(jnp.bfloat16))
        grad_gain_space = grad_gain_space + d_gain
        grad_table = grad_table + jnp.einsum("cfa,cfd->ad", one_hot, jnp.sum(d_begun, 2))
    grad_space_qkv = space_pieces[0][1] + space_pieces[1][1]
    grad_space_out = space_pieces[0][2] + space_pieces[1][2]
    grad_time_qkv = time_pieces[0][1] + time_pieces[1][1]
    grad_time_out = time_pieces[0][2] + time_pieces[1][2]
    shares = (
        lax.psum_scatter(
            grad_space_qkv.astype(jnp.bfloat16), "wide", scatter_dimension=1, tiled=True
        ).astype(jnp.float32),
        lax.psum_scatter(
            grad_space_out.astype(jnp.bfloat16), "wide", scatter_dimension=1, tiled=True
        ).astype(jnp.float32),
        lax.psum_scatter(
            grad_time_qkv.astype(jnp.bfloat16), "wide", scatter_dimension=1, tiled=True
        ).astype(jnp.float32),
        lax.psum_scatter(
            grad_time_out.astype(jnp.bfloat16), "wide", scatter_dimension=1, tiled=True
        ).astype(jnp.float32),
        lax.psum_scatter(
            grad_up.astype(jnp.bfloat16), "wide", scatter_dimension=0, tiled=True
        ).astype(jnp.float32),
        lax.psum_scatter(
            grad_down.astype(jnp.bfloat16), "wide", scatter_dimension=1, tiled=True
        ).astype(jnp.float32),
        lax.psum_scatter(
            grad_gain_space.astype(jnp.bfloat16), "wide", scatter_dimension=0, tiled=True
        ).astype(jnp.float32),
        lax.psum_scatter(
            grad_gain_time.astype(jnp.bfloat16), "wide", scatter_dimension=0, tiled=True
        ).astype(jnp.float32),
        lax.psum_scatter(
            grad_gain_ffn.astype(jnp.bfloat16), "wide", scatter_dimension=0, tiled=True
        ).astype(jnp.float32),
        lax.psum_scatter(
            grad_table.astype(jnp.bfloat16), "wide", scatter_dimension=1, tiled=True
        ).astype(jnp.float32),
    )
    summed_grads = (
        lax.psum(shares[0].astype(jnp.bfloat16), "clip").astype(jnp.float32),
        lax.psum(shares[1].astype(jnp.bfloat16), "clip").astype(jnp.float32),
        lax.psum(shares[2].astype(jnp.bfloat16), "clip").astype(jnp.float32),
        lax.psum(shares[3].astype(jnp.bfloat16), "clip").astype(jnp.float32),
        lax.psum(shares[4].astype(jnp.bfloat16), "clip").astype(jnp.float32),
        lax.psum(shares[5].astype(jnp.bfloat16), "clip").astype(jnp.float32),
        lax.psum(shares[6].astype(jnp.bfloat16), "clip").astype(jnp.float32),
        lax.psum(shares[7].astype(jnp.bfloat16), "clip").astype(jnp.float32),
        lax.psum(shares[8].astype(jnp.bfloat16), "clip").astype(jnp.float32),
        lax.psum(shares[9].astype(jnp.bfloat16), "clip").astype(jnp.float32),
    )
    return (
        results[0],
        results[1],
        d_inputs[0],
        d_inputs[1],
        summed_grads[9],
        summed_grads[6],
        summed_grads[0],
        summed_grads[1],
        summed_grads[7],
        summed_grads[2],
        summed_grads[3],
        summed_grads[8],
        summed_grads[4],
        summed_grads[5],
    )


def solution(mesh):
    return jax.shard_map(
        per_device,
        mesh=mesh,
        in_specs=(
            P("clip", "wide", None, None),
            P("clip", "wide", None, None),
            P("clip", "wide"),
            P("clip", "wide"),
            P(),
            P(),
            P(None, None, "tp"),
            P("tp", None),
            P(),
            P(None, None, "tp"),
            P("tp", None),
            P(),
            P(None, "tp"),
            P("tp", None),
            P("clip", "wide", None, None),
            P("clip", "wide", None, None),
        ),
        out_specs=(
            P("clip", "wide", None, None),
            P("clip", "wide", None, None),
            P("clip", "wide", None, None),
            P("clip", "wide", None, None),
            P(None, "wide"),
            P("wide"),
            P(None, "wide", "tp"),
            P("tp", "wide"),
            P("wide"),
            P(None, "wide", "tp"),
            P("tp", "wide"),
            P("wide"),
            P("wide", "tp"),
            P("tp", "wide"),
        ),
        check_vma=False,
    )
```

profile of v0, /device:TPU:0, one launch (start us, length us, event | category | flops | bytes accessed | tf_op | source)
XLA Modules:
  0.0 1353.4 jit_solution(1315460391640081299)
XLA Ops:
  56.9 77.4 %all-reduce.25.cloned.1.call-done = (bf16[2,2,64,1024]{3,2,1,0:T(8,128)(2,1)}, bf16[2,2,256,1024]{3,2,1,0:T(8,128)(2,1)}) async-done(((bf16[2,2,64,1024]{3,2,1,0:T(8,128)(2,1)}, bf16[2,2,256,1024]{3,2,1,0:T(8,128)(2,1)}), (bf16[2,2,64,1024]{3,2,1,0:T(8,128)(2,1)}, bf16[2,2,256,1024]{3,2,1,0:T(8,128)(2,1)})) %all-reduce.25.cloned.1.call-update) | async-done | bytes 2621456 | tf_op jit(solution)/shard_map/psum | solution.py:108
  137.0 15.4 %all-to-all-start.2 = ((bf16[2,2,64,1024]{3,1,0,2:T(2,128)(2,1)}), bf16[2,2,64,1024]{3,1,0,2:T(2,128)(2,1)}, u32[]{:S(2)}, u32[]{:S(2)}) async-start(bf16[2,2,64,1024]{3,1,0,2:T(2,128)(2,1)} %copy.215), calls=%async_computation.2 | async-start | bytes 1048576 | tf_op jit(solution)/shard_map/all_to_all | solution.py:159
  193.8 27.4 %all-to-all-done = bf16[2,2,256,1024]{3,1,0,2:T(2,128)(2,1)} async-done(((bf16[2,2,256,1024]{3,1,0,2:T(2,128)(2,1)}), bf16[2,2,256,1024]{3,1,0,2:T(2,128)(2,1)}, u32[]{:S(2)}, u32[]{:S(2)}) %all-to-all-start) | async-done | bytes 2097184 | tf_op jit(solution)/shard_map/all_to_all | solution.py:158
  270.9 72.6 %all-reduce.23.cloned.1.call-done = (bf16[2,16,8,1024]{3,2,1,0:T(8,128)(2,1)}, bf16[2,16,32,1024]{3,2,1,0:T(8,128)(2,1)}) async-done(((bf16[2,16,8,1024]{3,2,1,0:T(8,128)(2,1)}, bf16[2,16,32,1024]{3,2,1,0:T(8,128)(2,1)}), (bf16[2,16,8,1024]{3,2,1,0:T(8,128)(2,1)}, bf16[2,16,32,1024]{3,2,1,0:T(8,128)(2,1)})) %all-reduce.23.cloned.1.call-update) | async-done | bytes 2621456 | tf_op jit(solution)/shard_map/psum | solution.py:108
  355.7 10.2 all-to-all-done.3
  372.2 47.1 %all-to-all-done.1 = bf16[2,16,32,1024]{3,2,0,1:T(8,128)(2,1)} async-done(((bf16[2,16,32,1024]{3,2,0,1:T(8,128)(2,1)}), bf16[2,16,32,1024]{3,2,0,1:T(8,128)(2,1)}, u32[]{:S(2)}, u32[]{:S(2)}) %all-to-all-start.1) | async-done | bytes 2097184 | tf_op jit(solution)/shard_map/all_to_all | solution.py:167
  433.3 15.7 %fusion.6 = bf16[1280,2048]{1,0:T(8,128)(2,1)} fusion(f32[1280,2048]{1,0:T(8,128)} %fusion.220, bf16[2048,1024]{1,0:T(8,128)(2,1)S(1)} %copy-done.134, bf16[256,1024]{1,0:T(8,128)(2,1)S(1)} %bitcast.564, bf16[1024,1024]{1,0:T(8,128)(2,1)S(1)} %bitcast.544), kind=kOutput, calls=%fused_computation.8 | convolution fusion | flops 5426380800 | bytes 22544384 | tf_op jit(solution)/shard_map/rd,fd->rf/dot_general | solution.py:190
  458.5 72.4 %all-reduce.17.cloned.1.call-done = bf16[1280,1024]{1,0:T(8,128)(2,1)} async-done(((bf16[1280,1024]{1,0:T(8,128)(2,1)}), bf16[1280,1024]{1,0:T(8,128)(2,1)}) %all-reduce.17.cloned.1.call-update) | async-done | bytes 2621456 | tf_op jit(solution)/shard_map/psum | solution.py:194
  556.9 10.4 all-to-all-done.6
  600.6 20.1 %all-to-all-done.4 = bf16[2,2,256,1024]{3,1,0,2:T(2,128)(2,1)} async-done(((bf16[2,2,256,1024]{3,1,0,2:T(2,128)(2,1)}), bf16[2,2,256,1024]{3,1,0,2:T(2,128)(2,1)}, u32[]{:S(2)}, u32[]{:S(2)}) %all-to-all-start.4) | async-done | bytes 2097184 | tf_op jit(solution)/shard_map/all_to_all | solution.py:204
  675.3 72.5 %all-reduce.21.cloned.1.call-done = (bf16[2,16,32,1024]{3,2,1,0:T(8,128)(2,1)}, bf16[2,16,8,1024]{3,2,1,0:T(8,128)(2,1)}) async-done(((bf16[2,16,32,1024]{3,2,1,0:T(8,128)(2,1)}, bf16[2,16,8,1024]{3,2,1,0:T(8,128)(2,1)}), (bf16[2,16,32,1024]{3,2,1,0:T(8,128)(2,1)}, bf16[2,16,8,1024]{3,2,1,0:T(8,128)(2,1)})) %all-reduce.21.cloned.1.call-update) | async-done | bytes 2621456 | tf_op jit(solution)/shard_map/psum | solution.py:224
  778.8 10.8 convolution_convert_fusion.1
  813.1 14.7 %all-to-all-done.5 = bf16[2,16,32,1024]{3,2,0,1:T(8,128)(2,1)S(1)} async-done(((bf16[2,16,32,1024]{3,2,0,1:T(8,128)(2,1)}), bf16[2,16,32,1024]{3,2,0,1:T(8,128)(2,1)S(1)}, u32[]{:S(2)}, u32[]{:S(2)}) %all-to-all-start.5) | async-done | bytes 2097184 | tf_op jit(solution)/shard_map/all_to_all | solution.py:235
  863.9 10.9 convolution_convert_fusion.2
  927.3 10.5 convolution_convert_fusion.3
  938.2 47.5 %all-reduce.19.cloned.1.call-done = (bf16[2,2,256,1024]{3,2,1,0:T(8,128)(2,1)}, bf16[2,2,64,1024]{3,2,1,0:T(8,128)(2,1)}, bf16[2,2,256,1024]{3,2,1,0:T(8,128)(2,1)}, bf16[2,2,64,1024]{3,2,1,0:T(8,128)(2,1)}) async-done(((bf16[2,2,256,1024]{3,2,1,0:T(8,128)(2,1)}, bf16[2,2,64,1024]{3,2,1,0:T(8,128)(2,1)}, bf16[2,2,256,1024]{3,2,1,0:T(8,128)(2,1)}, bf16[2,2,64,1024]{3,2,1,0:T(8,128)(2,1)}), ...) | async-done | bytes 5242896 | tf_op jit(solution)/shard_map/psum | solution.py:107
  1000.4 19.9 %reduce-scatter.30.cloned.1.call-done = bf16[128,512]{1,0:T(8,128)(2,1)} async-done(((bf16[1024,512]{1,0:T(8,128)(2,1)}), bf16[128,512]{1,0:T(8,128)(2,1)}) %reduce-scatter.30.cloned.1.call-update) | async-done | bytes 131088
  1021.9 49.3 %reduce-scatter.32.cloned.1.call-done = bf16[128,2048]{1,0:T(8,128)(2,1)} async-done(((bf16[1024,2048]{1,0:T(8,128)(2,1)}), bf16[128,2048]{1,0:T(8,128)(2,1)}) %reduce-scatter.32.cloned.1.call-update) | async-done | bytes 524304
  1073.2 31.3 %reduce-scatter.26.cloned.1.call-done = bf16[128,512]{1,0:T(8,128)(2,1)} async-done(((bf16[1024,512]{1,0:T(8,128)(2,1)}), bf16[128,512]{1,0:T(8,128)(2,1)}) %reduce-scatter.26.cloned.1.call-update) | async-done | bytes 131088
  1106.2 39.5 %reduce-scatter.28.cloned.1.call-done = bf16[128,1536]{1,0:T(8,128)(2,1)} async-done(((bf16[1024,1536]{1,0:T(8,128)(2,1)}), bf16[128,1536]{1,0:T(8,128)(2,1)}) %reduce-scatter.28.cloned.1.call-update) | async-done | bytes 393232
  1148.5 38.9 %reduce-scatter.24.cloned.1.call-done = bf16[128,1536]{1,0:T(8,128)(2,1)} async-done(((bf16[1024,1536]{1,0:T(8,128)(2,1)}), bf16[128,1536]{1,0:T(8,128)(2,1)}) %reduce-scatter.24.cloned.1.call-update) | async-done | bytes 393232
  1190.1 48.8 %reduce-scatter.20.cloned.1.call-done = bf16[128,2048]{1,0:T(8,128)(2,1)} async-done(((bf16[1024,2048]{1,0:T(8,128)(2,1)}), bf16[128,2048]{1,0:T(8,128)(2,1)}) %reduce-scatter.20.cloned.1.call-update) | async-done | bytes 524304 | tf_op jit(solution)/shard_map/reduce_scatter | solution.py:273
  1243.2 14.0 %all-reduce.3 = (bf16[1024]{0:T(1024)(128)(2,1)S(1)}, bf16[1024]{0:T(1024)(128)(2,1)S(1)}, bf16[1024]{0:T(1024)(128)(2,1)S(1)}) all-reduce(bf16[1024]{0:T(1024)(128)(2,1)S(1)} %get-tuple-element.128, bf16[1024]{0:T(1024)(128)(2,1)S(1)} %get-tuple-element.127, ...), channel_id=3, replica_groups=mesh['clip'=2,'wide'=8,'tp'=2] {'wide'}, use_global_device_ids=true, to_apply=%region_49.50.clone | all-reduce | flops 3072 | bytes 12288
  1278.1 57.9 %all-reduce.27.cloned.1.call-done = (bf16[3,128,512]{1,2,0:T(8,128)(2,1)}, bf16[3,128,512]{1,2,0:T(8,128)(2,1)}, bf16[512,128]{1,0:T(8,128)(2,1)}, bf16[512,128]...) async-done(((bf16[3,128,512]{1,2,0:T(8,128)(2,1)}, bf16[3,128,512]{1,2,0:T(8,128)(2,1)}, bf16[512,128]{1,0:T(8,128)(2,1)}, ...) | async-done | bytes 2097168 | tf_op jit(solution)/shard_map/psum | solution.py:293
  (555 shorter events, 501.4 us)
Async XLA Ops:
  7.2 169.9 %copy-start = (bf16[3,1024,512]{2,1,0:T(8,128)(2,1)S(1)}, bf16[3,1024,512]{2,1,0:T(8,128)(2,1)}, u32[]{:S(2)}) copy-start(bf16[3,1024,512]{2,1,0:T(8,128)(2,1)} %param.25) | copy-start | bytes 9437188
  7.2 127.1 %all-reduce.25.cloned.1.call-start = ((), (), s32[]{:S(2)}) async-start(), calls=%async_computation.26 | async-start | bytes 5242880 | tf_op jit(solution)/shard_map/psum | solution.py:108
  8.3 144.1 %copy-start.73 = (f32[2,2,1024]{2,1,0:T(2,128)}, f32[2,2,1024]{2,1,0:T(2,128)S(1)}, u32[]{:S(2)}) copy-start(f32[2,2,1024]{2,1,0:T(2,128)S(1)} %fusion.203) | copy-start | bytes 49156
  137.0 30.8 %all-to-all-start.2 = ((bf16[2,2,64,1024]{3,1,0,2:T(2,128)(2,1)}), bf16[2,2,64,1024]{3,1,0,2:T(2,128)(2,1)}, u32[]{:S(2)}, u32[]{:S(2)}) async-start(bf16[2,2,64,1024]{3,1,0,2:T(2,128)(2,1)} %copy.215), calls=%async_computation.2 | async-start | bytes 1048576 | tf_op jit(solution)/shard_map/all_to_all | solution.py:159
  167.8 53.4 %all-to-all-start = ((bf16[2,2,256,1024]{3,1,0,2:T(2,128)(2,1)}), bf16[2,2,256,1024]{3,1,0,2:T(2,128)(2,1)}, u32[]{:S(2)}, u32[]{:S(2)}) async-start(bf16[2,2,256,1024]{3,1,0,2:T(2,128)(2,1)} %copy.201), calls=%async_computation | async-start | bytes 4194304 | tf_op jit(solution)/shard_map/all_to_all | solution.py:158
  172.2 171.3 %all-reduce.23.cloned.1.call-start = ((), (), s32[]{:S(2)}) async-start(), calls=%async_computation.25 | async-start | bytes 5242880 | tf_op jit(solution)/shard_map/psum | solution.py:108
  345.8 20.1 %all-to-all-start.3 = ((bf16[2,16,8,1024]{3,2,0,1:T(8,128)(2,1)}), bf16[2,16,8,1024]{3,2,0,1:T(8,128)(2,1)}, u32[]{:S(2)}, u32[]{:S(2)}) async-start(bf16[2,16,8,1024]{3,2,0,1:T(8,128)(2,1)} %copy.222), calls=%async_computation.3 | async-start | bytes 1048576 | tf_op jit(solution)/shard_map/all_to_all | solution.py:168
  365.9 53.4 %all-to-all-start.1 = ((bf16[2,16,32,1024]{3,2,0,1:T(8,128)(2,1)}), bf16[2,16,32,1024]{3,2,0,1:T(8,128)(2,1)}, u32[]{:S(2)}, u32[]{:S(2)}) async-start(bf16[2,16,32,1024]{3,2,0,1:T(8,128)(2,1)} %copy.208), calls=%async_computation.1 | async-start | bytes 4194304 | tf_op jit(solution)/shard_map/all_to_all | solution.py:167
  370.3 160.6 %all-reduce.17.cloned.1.call-start = ((), (), s32[]{:S(2)}) async-start(), calls=%async_computation.15 | async-start | bytes 5242880 | tf_op jit(solution)/shard_map/psum | solution.py:194
  547.2 20.1 %all-to-all-start.6 = ((bf16[2,2,64,1024]{3,1,0,2:T(2,128)(2,1)}), bf16[2,2,64,1024]{3,1,0,2:T(2,128)(2,1)}, u32[]{:S(2)}, u32[]{:S(2)}) async-start(bf16[2,2,64,1024]{3,1,0,2:T(2,128)(2,1)} %copy.248), calls=%async_computation.6 | async-start | bytes 1048576 | tf_op jit(solution)/shard_map/all_to_all | solution.py:211
  567.3 53.4 %all-to-all-start.4 = ((bf16[2,2,256,1024]{3,1,0,2:T(2,128)(2,1)}), bf16[2,2,256,1024]{3,1,0,2:T(2,128)(2,1)}, u32[]{:S(2)}, u32[]{:S(2)}) async-start(bf16[2,2,256,1024]{3,1,0,2:T(2,128)(2,1)} %copy.224), calls=%async_computation.4 | async-start | bytes 4194304 | tf_op jit(solution)/shard_map/all_to_all | solution.py:204
  571.7 176.1 %all-reduce.21.cloned.1.call-start = ((), (), s32[]{:S(2)}) async-start(), calls=%async_computation.24 | async-start | bytes 5242880 | tf_op jit(solution)/shard_map/psum | solution.py:224
  755.1 20.0 %all-to-all-start.7 = ((bf16[2,16,8,1024]{3,2,0,1:T(8,128)(2,1)}), bf16[2,16,8,1024]{3,2,0,1:T(8,128)(2,1)S(1)}, u32[]{:S(2)}, u32[]{:S(2)}) async-start(bf16[2,16,8,1024]{3,2,0,1:T(8,128)(2,1)} %copy.263), calls=%async_computation.7 | async-start | bytes 1048576 | tf_op jit(solution)/shard_map/all_to_all | solution.py:236
  775.1 52.6 %all-to-all-start.5 = ((bf16[2,16,32,1024]{3,2,0,1:T(8,128)(2,1)}), bf16[2,16,32,1024]{3,2,0,1:T(8,128)(2,1)S(1)}, u32[]{:S(2)}, u32[]{:S(2)}) async-start(bf16[2,16,32,1024]{3,2,0,1:T(8,128)(2,1)} %copy.239), calls=%async_computation.5 | async-start | bytes 4194304 | tf_op jit(solution)/shard_map/all_to_all | solution.py:235
  778.7 206.9 %all-reduce.19.cloned.1.call-start = ((), (), s32[]{:S(2)}) async-start(), calls=%async_computation.23 | async-start | bytes 10485760 | tf_op jit(solution)/shard_map/psum | solution.py:107
  856.0 164.2 %reduce-scatter.30.cloned.1.call-start = ((), (), s32[]{:S(2)}) async-start(), calls=%async_computation.21 | async-start | bytes 1179648
  863.8 207.4 %reduce-scatter.32.cloned.1.call-start = ((), (), s32[]{:S(2)}) async-start(), calls=%async_computation.22 | async-start | bytes 4718592
  881.4 223.2 %reduce-scatter.26.cloned.1.call-start = ((), (), s32[]{:S(2)}) async-start(), calls=%async_computation.19 | async-start | bytes 1179648
  894.4 251.3 %reduce-scatter.28.cloned.1.call-start = ((), (), s32[]{:S(2)}) async-start(), calls=%async_computation.20 | async-start | bytes 3538944
  909.7 277.7 %reduce-scatter.24.cloned.1.call-start = ((), (), s32[]{:S(2)}) async-start(), calls=%async_computation.18 | async-start | bytes 3538944
  927.2 311.6 %reduce-scatter.20.cloned.1.call-start = ((), (), s32[]{:S(2)}) async-start(), calls=%async_computation.16 | async-start | bytes 4718592 | tf_op jit(solution)/shard_map/reduce_scatter | solution.py:273
  937.9 332.3 %reduce-scatter.22.cloned.1.call-start = ((), (), s32[]{:S(2)}) async-start(), calls=%async_computation.17 | async-start | bytes 294912
  999.2 239.7 %copy-start.142 = (u32[32]{0:T(128)S(1)}, u32[32]{0:T(128)}, u32[]{:S(2)}) copy-start(u32[32]{0:T(128)} %constant.81) | copy-start | bytes 388
  1000.3 335.7 %all-reduce.27.cloned.1.call-start = ((), (), s32[]{:S(2)}) async-start(), calls=%async_computation.27 | async-start | bytes 4194304 | tf_op jit(solution)/shard_map/psum | solution.py:293
  (143 other events, 1967.2 us)
Sparse Core Ops, SparseCore 0:
  57.0 77.2 all-reduce.24
  271.0 72.4 all-reduce.22
  458.6 72.2 all-reduce.16
  675.3 72.4 all-reduce.20
  856.1 129.4 all-reduce.18
  987.9 32.3 reduce-scatter.29
  1022.6 48.5 reduce-scatter.31
  1074.1 30.3 reduce-scatter.25
  1107.0 38.6 reduce-scatter.27
  1148.0 39.3 reduce-scatter.23
  1189.7 49.0 reduce-scatter.19
  1241.6 28.5 reduce-scatter.21
  1274.0 62.0 all-reduce.26
where the time goes:
time: 1360 us; the launch traced here: 1350 us
  waiting for transfers between devices  779 us (57%)
  matrix products  198 us (15%)
  local copies, waits for them, and re-layouts  190 us (14%)
  other arithmetic  103 us (8%)
  starting transfers between devices  47.6 us (4%)
  blocking collectives  18.9 us (1%)
  between operations  16.8 us (1%)
    unnamed x19, waiting for transfers between devices  186 us
    psum x2, waiting for transfers between devices, settle(): lax.psum(partials[1].astype(jnp.bfloat16), 'tp').astype(jnp.float32)  150 us
    psum x1, waiting for transfers between devices, per_device(): lax.psum(time_pieces[0][0].astype(jnp.bfloat16), 'tp').astype(jnp.float32)  72.5 us
    psum x1, waiting for transfers between devices, per_device(): lax.psum(jnp.einsum('rf,df->rd', d_hidden, ffn_up, preferred_element_type...  72.4 us
    unnamed x312, local copies, waits for them, and re-layouts  66 us
    psum x1, waiting for transfers between devices, per_device(): lax.psum(shares[0].astype(jnp.bfloat16), 'clip').astype(jnp.float32)  57.9 us
    reduce_scatter x1, waiting for transfers between devices, per_device(): lax.psum_scatter(grad_up.astype(jnp.bfloat16), 'wide', scatter_dimension=...  48.8 us
    psum x1, waiting for transfers between devices, settle(): lax.psum(partials[0].astype(jnp.bfloat16), 'tp').astype(jnp.float32)  47.5 us
  transfers between devices with their start and end apart: 21, of which 21 were waited for; matrix products, arithmetic and copies ran while one was open for 16% of the time, Pallas kernels for 0%

commit v1 on v0

v1 whole, which is shorter than its diff:
```python
from functools import partial

import jax
import jax.numpy as jnp
from jax import lax
from jax.experimental import pallas as pl
from jax.experimental.pallas import tpu as pltpu
from jax.sharding import PartitionSpec as P

HEAD = 64
PAIR = 2 * HEAD
BF = jnp.bfloat16
F32 = jnp.float32


def group_mask(kind, rows, length):
    if kind is None:
        return None
    name, size = kind
    query = lax.broadcasted_iota(jnp.int32, (rows, length), 0) & (length - 1)
    key = lax.broadcasted_iota(jnp.int32, (rows, length), 1)
    shift = size.bit_length() - 1
    same = (query >> shift) == (key >> shift)
    if name == "causal":
        same = same & (key <= query)
    return same


def head_factors(value):
    lane = lax.broadcasted_iota(jnp.int32, (1, PAIR), 1)
    first = jnp.where(lane < HEAD, value, 0.0).astype(BF)
    second = jnp.where(lane < HEAD, 0.0, value).astype(BF)
    return first, second


def dot_t(a, b):
    return lax.dot_general(a, b, (((1,), (1,)), ((), ())), preferred_element_type=F32)


def dot_n(a, b):
    return lax.dot_general(a, b, (((1,), (0,)), ((), ())), preferred_element_type=F32)


def dot_l(a, b):
    return lax.dot_general(a, b, (((0,), (0,)), ((), ())), preferred_element_type=F32)


def attend_kernel(groups, p_ref, o_ref, l_ref):
    first, second = head_factors(1.0)
    q_first, q_second = head_factors(HEAD**-0.5)
    left = lax.broadcasted_iota(jnp.int32, (1, PAIR), 1) < HEAD
    for start, length, kind in groups:
        rows = slice(start, start + length)
        query, key, value = (p_ref[i, rows, :] for i in range(3))
        outs, logs = [], []
        for q_part, v_part in ((q_first, first), (q_second, second)):
            scores = dot_t(query * q_part, key)
            mask = group_mask(kind, length, length)
            if mask is not None:
                scores = jnp.where(mask, scores, -1e30)
            largest = jnp.max(scores, -1, keepdims=True)
            shifted = jnp.exp(scores - largest)
            total = jnp.sum(shifted, -1, keepdims=True)
            soft = (shifted / total).astype(BF)
            outs.append(dot_n(soft, value * v_part))
            logs.append(largest + jnp.log(total))
        o_ref[rows, :] = (outs[0] + outs[1]).astype(BF)
        l_ref[rows, :] = jnp.where(left, logs[0], logs[1])


def attend_back_kernel(groups, p_ref, d_ref, l_ref, o_ref):
    first, second = head_factors(1.0)
    scale = HEAD**-0.5
    for start, length, kind in groups:
        rows = slice(start, start + length)
        query, key, value = (p_ref[i, rows, :] for i in range(3))
        d_out = d_ref[rows, :]
        d_query = d_key = d_value = None
        for index, part in enumerate((first, second)):
            q_part, d_part, k_part = query * part, d_out * part, key * part
            scores = dot_t(q_part, key) * scale
            soft = jnp.exp(scores - l_ref[rows, index * HEAD : index * HEAD + 1])
            mask = group_mask(kind, length, length)
            if mask is not None:
                soft = jnp.where(mask, soft, 0.0)
            d_soft = dot_t(d_part, value)
            row_dot = jnp.sum(soft * d_soft, -1, keepdims=True)
            d_scores = (soft * (d_soft - row_dot)).astype(BF)
            terms = (dot_n(d_scores, k_part), dot_l(d_scores, q_part), dot_l(soft.astype(BF), d_part))
            if index == 0:
                d_query, d_key, d_value = terms
            else:
                d_query, d_key, d_value = d_query + terms[0], d_key + terms[1], d_value + terms[2]
        o_ref[0, rows, :] = (d_query * scale).astype(BF)
        o_ref[1, rows, :] = (d_key * scale).astype(BF)
        o_ref[2, rows, :] = d_value.astype(BF)


def attend(projected, groups):
    _, rows, width = projected.shape
    return pl.pallas_call(
        partial(attend_kernel, groups),
        grid=(width // PAIR,),
        in_specs=[pl.BlockSpec((3, rows, PAIR), lambda h: (0, 0, h))],
        out_specs=[pl.BlockSpec((rows, PAIR), lambda h: (0, h))] * 2,
        out_shape=[
            jax.ShapeDtypeStruct((rows, width), BF),
            jax.ShapeDtypeStruct((rows, width), F32),
        ],
        cost_estimate=pl.CostEstimate(
            flops=4 * rows * 512 * width, bytes_accessed=12 * rows * width, transcendentals=rows * 256 * width // HEAD
        ),
        name="attend",
    )(projected)


def attend_back(projected, d_heads, logs, groups):
    _, rows, width = projected.shape
    return pl.pallas_call(
        partial(attend_back_kernel, groups),
        grid=(width // PAIR,),
        in_specs=[
            pl.BlockSpec((3, rows, PAIR), lambda h: (0, 0, h)),
            pl.BlockSpec((rows, PAIR), lambda h: (0, h)),
            pl.BlockSpec((rows, PAIR), lambda h: (0, h)),
        ],
        out_specs=pl.BlockSpec((3, rows, PAIR), lambda h: (0, 0, h)),
        out_shape=jax.ShapeDtypeStruct(projected.shape, BF),
        cost_estimate=pl.CostEstimate(
            flops=10 * rows * 512 * width, bytes_accessed=18 * rows * width, transcendentals=rows * 256 * width // HEAD
        ),
        name="attend_back",
    )(projected, d_heads, logs)


def frame_groups(first_frames, first_grid, second_frames, second_grid):
    groups = [(i * first_grid, first_grid, None) for i in range(first_frames)]
    base = first_frames * first_grid
    if second_frames % 2 == 0:
        groups += [
            (base + i * second_grid, 2 * second_grid, ("block", second_grid))
            for i in range(0, second_frames, 2)
        ]
    else:
        groups += [(base + i * second_grid, second_grid, None) for i in range(second_frames)]
    return tuple(groups)


def clip_groups(rows, frames):
    size = 128
    while rows % size:
        size //= 2
    return tuple((i, size, ("causal", frames)) for i in range(0, rows, size))


def swap(value, axis, size, step=1):
    return lax.ppermute(value, axis, [(i, i ^ step) for i in range(size)])


def flip(bit):
    return 1 - bit


def take(value, index, axis):
    return lax.dynamic_index_in_dim(value, index, axis, keepdims=False)


def fetch_other(weight, sizes, clip_bit, core_bit):
    rows = weight.shape[-2]
    quarter = rows // 4
    lead = (0,) * (weight.ndim - 2)

    def put(whole, piece, clip_at, core_at):
        return lax.dynamic_update_slice(whole, piece, (*lead, (2 * clip_at + core_at) * quarter, 0))

    mine = lax.dynamic_slice_in_dim(weight, (2 * clip_bit + core_bit) * quarter, quarter, weight.ndim - 2)
    from_x = swap(mine, "tp", sizes["tp"])
    from_y = swap(from_x, "clip", sizes["clip"])
    core_x = swap(from_x, "wide", sizes["wide"])
    core_y = swap(from_y, "wide", sizes["wide"])
    whole = jnp.zeros_like(weight)
    whole = put(whole, from_x, clip_bit, core_bit)
    whole = put(whole, from_y, flip(clip_bit), core_bit)
    whole = put(whole, core_x, clip_bit, flip(core_bit))
    return put(whole, core_y, flip(clip_bit), flip(core_bit))


def halves(value, index, axis):
    size = value.shape[axis] // 2
    return (
        lax.dynamic_slice_in_dim(value, index * size, size, axis),
        lax.dynamic_slice_in_dim(value, flip(index) * size, size, axis),
    )


def reduce_grad(left, own, other, sizes, bits, x_first):
    clip_bit, core_bit, z_index = bits
    n, depth = left.shape
    cuts = depth // sizes["wide"]
    stacks = sizes["wide"] // 2
    split = left.reshape(n, stacks, 2, cuts)
    keep_left = take(split, core_bit, 2).reshape(n, stacks * cuts)
    send_left = take(split, flip(core_bit), 2).reshape(n, stacks * cuts)

    def product(a, b):
        return jnp.einsum("nd,ntk->dtk", a, b, preferred_element_type=F32)

    own_keep, own_send = halves(own, clip_bit, 2)
    other_keep, other_send = halves(other, clip_bit, 2)

    def core_sum(b):
        return product(keep_left, b) + swap(product(send_left, b).astype(BF), "wide", sizes["wide"]).astype(F32)

    def x_swap(v):
        return swap(v.astype(BF), "tp", sizes["tp"]).astype(F32)

    def y_swap(v):
        return swap(v.astype(BF), "clip", sizes["clip"]).astype(F32)

    if x_first:
        keep = core_sum(own_keep) + x_swap(core_sum(other_keep))
        send = core_sum(own_send) + x_swap(core_sum(other_send))
        total = keep + y_swap(send)
    else:
        keep_own = core_sum(own_keep) + y_swap(core_sum(own_send))
        keep_other = core_sum(other_keep) + y_swap(core_sum(other_send))
        total = keep_own + x_swap(keep_other)
    for step in range(2, sizes["clip"].bit_length()):
        total = total + swap(total.astype(BF), "clip", sizes["clip"], 1 << (step - 1)).astype(F32)
    blocks = total.astype(BF).reshape((stacks, cuts) + total.shape[1:])
    result = take(total.reshape(blocks.shape), z_index, 0)
    for step in range(1, stacks):
        result = result + swap(take(blocks, z_index ^ step, 0), "wide", sizes["wide"], 2 * step).astype(F32)
    low = result.astype(BF)
    partner = swap(low, "clip", sizes["clip"])
    lower = jnp.where(clip_bit == 0, low, partner)
    upper = jnp.where(clip_bit == 0, partner, low)
    return jnp.concatenate([lower, upper], 2).astype(F32)


def reduce_small(rows, sizes, bits):
    clip_bit, core_bit, z_index = bits
    stacks = sizes["wide"] // 2
    count, depth = rows.shape
    blocks = rows.reshape(count, stacks, 2, depth // sizes["wide"]).transpose(1, 2, 0, 3)
    total = take(blocks, core_bit, 1) + swap(take(blocks, flip(core_bit), 1), "wide", sizes["wide"])
    total = total + swap(total, "tp", sizes["tp"])
    step = 1
    while step < sizes["clip"]:
        total = total + swap(total, "clip", sizes["clip"], step)
        step *= 2
    result = take(total, z_index, 0)
    for step in range(1, stacks):
        result = result + swap(take(total, z_index ^ step, 0), "wide", sizes["wide"], 2 * step)
    return result


def norm_stats(values):
    mean = jnp.mean(values, -1, keepdims=True)
    centered = values - mean
    spread = jnp.mean(centered * centered, -1, keepdims=True)
    return mean, lax.rsqrt(spread + 1e-05)


def norm_apply(values, gain, stats):
    return ((values - stats[0]) * stats[1] * gain).astype(BF)


def norm_back(values, gain, stats, d_normed):
    normal = (values - stats[0]) * stats[1]
    d_gain = jnp.sum(d_normed * normal, 0)
    scaled = d_normed * gain
    mean_first = jnp.mean(scaled, -1, keepdims=True)
    mean_second = jnp.mean(scaled * normal, -1, keepdims=True)
    return (scaled - mean_first - normal * mean_second) * stats[1], d_gain


def project(normed, weight):
    return jnp.einsum("nd,tde->tne", normed, weight, preferred_element_type=F32).astype(BF)


def mix(a, b):
    return jnp.dot(a, b, preferred_element_type=F32)


def gelu_parts(hidden):
    root = (2.0 / jnp.pi) ** 0.5
    square = hidden * hidden
    curve = jnp.tanh(root * (hidden + 0.044715 * square * hidden))
    slope = 0.5 * (1.0 + curve) + 0.5 * hidden * (1.0 - curve * curve) * root * (1.0 + 3 * 0.044715 * square)
    return 0.5 * hidden * (1.0 + curve), slope


def per_device(
    sizes,
    frames_a,
    frames_b,
    actions_a,
    actions_b,
    action_table,
    gain_space,
    space_qkv,
    space_out,
    gain_time,
    time_qkv,
    time_out,
    gain_ffn,
    ffn_up,
    ffn_down,
    cot_a,
    cot_b,
):
    n_wide = sizes["wide"]
    tp_index = lax.axis_index("tp")
    clip_bit = lax.axis_index("clip") % 2
    wide_index = lax.axis_index("wide")
    bits = (clip_bit, wide_index % 2, wide_index // 2)
    core_bit = bits[1]
    _, n_frames, grid_a, width = frames_a.shape
    grid_b = frames_b.shape[2]
    rows_a = n_frames * grid_a
    rows_b = n_frames * grid_b
    spots_a, spots_b = grid_a // n_wide, grid_b // n_wide
    spots = spots_a + spots_b
    all_frames = n_frames * n_wide
    rows = rows_a + rows_b

    def pick(value):
        return take(value, tp_index, 0)

    def to_grid(rows_in):
        first = rows_in[:rows_a].reshape(n_frames, n_wide, spots_a, width)
        second = rows_in[rows_a:].reshape(n_frames, n_wide, spots_b, width)
        packed = jnp.concatenate([first, second], 2).transpose(1, 0, 2, 3)
        moved = lax.all_to_all(packed, "wide", split_axis=0, concat_axis=0, tiled=True)
        return moved.reshape(all_frames, spots, width).transpose(1, 0, 2).reshape(rows, width)

    def to_frames(rows_in):
        packed = rows_in.reshape(spots, n_wide, n_frames, width).transpose(1, 2, 0, 3)
        moved = lax.all_to_all(packed, "wide", split_axis=0, concat_axis=0, tiled=True)
        first = moved[:, :, :spots_a].transpose(1, 0, 2, 3).reshape(rows_a, width)
        second = moved[:, :, spots_a:].transpose(1, 0, 2, 3).reshape(rows_b, width)
        return jnp.concatenate([first, second])

    def both_clips(rows_in):
        partner = swap(rows_in, "tp", sizes["tp"])
        pair = jnp.stack(
            [jnp.where(tp_index == 0, rows_in, partner), jnp.where(tp_index == 0, partner, rows_in)]
        )
        return (
            pair[:, :rows_a].reshape(2, n_frames, grid_a, width),
            pair[:, rows_a:].reshape(2, n_frames, grid_b, width),
        )

    other = {}
    names = ("space_qkv", "space_out", "time_qkv", "time_out", "ffn_up", "ffn_down")
    mine = dict(zip(names, (space_qkv, space_out, time_qkv, time_out, ffn_up, ffn_down)))
    for name in names:
        other[name] = fetch_other(mine[name], sizes, clip_bit, core_bit)

    space_groups = frame_groups(n_frames, grid_a, n_frames, grid_b)
    time_groups = clip_groups(rows, all_frames)

    cot = to_grid(jnp.concatenate([pick(cot_a).reshape(rows_a, width), pick(cot_b).reshape(rows_b, width)]))

    codes = lax.broadcasted_iota(jnp.int32, (1, action_table.shape[0]), 1)
    acts = jnp.concatenate([pick(actions_a), pick(actions_b)])
    one_hot = (acts[:, None] == codes).astype(F32)
    shifts = jnp.dot(one_hot, action_table.astype(F32), precision=lax.Precision.HIGHEST)
    started = jnp.concatenate(
        [
            (pick(frames_a).astype(F32) + shifts[:n_frames, None, :]).reshape(rows_a, width),
            (pick(frames_b).astype(F32) + shifts[n_frames:, None, :]).reshape(rows_b, width),
        ]
    )

    def branch(stream, gain, name, groups):
        stats = norm_stats(stream)
        normed = norm_apply(stream, gain, stats)
        kept = []
        total = stream
        for side in (mine, other):
            projected = project(normed, side[name + "_qkv"])
            heads, logs = attend(projected, groups)
            total = total + mix(heads, side[name + "_out"])
            kept.append((projected, heads, logs))
        return total.astype(BF), (stats, normed, kept)

    def branch_back(d_stream, stream, gain, name, groups, saved, x_first):
        stats, normed, kept = saved
        d_normed = 0.0
        d_projected = []
        for side, (projected, heads, logs) in zip((mine, other), kept):
            d_heads = dot_t(d_stream, side[name + "_out"]).astype(BF)
            piece = attend_back(projected, d_heads, logs, groups)
            d_projected.append(piece.transpose(1, 0, 2))
            d_normed = d_normed + jnp.einsum(
                "tne,tde->nd", piece, side[name + "_qkv"], preferred_element_type=F32
            )
        grad_out = reduce_grad(
            d_stream, kept[0][1][:, None, :], kept[1][1][:, None, :], sizes, bits, not x_first
        )
        grad_qkv = reduce_grad(normed, d_projected[0], d_projected[1], sizes, bits, x_first)
        d_values, d_gain = norm_back(stream, gain, stats, d_normed)
        return d_stream.astype(F32) + d_values, d_gain, grad_qkv.transpose(1, 0, 2), grad_out[:, 0, :].T

    middle, space_saved = branch(started, gain_space, "space", space_groups)
    middle = to_grid(middle).astype(F32)
    latest, time_saved = branch(middle, gain_time, "time", time_groups)
    latest = latest.astype(F32)
    ffn_stats = norm_stats(latest)
    normed_ffn = norm_apply(latest, gain_ffn, ffn_stats)
    total = latest
    d_normed_ffn = 0.0
    gelus, d_hiddens = [], []
    for side in (mine, other):
        hidden = mix(normed_ffn, side["ffn_up"])
        gelu, slope = gelu_parts(hidden)
        gelu = gelu.astype(BF)
        d_hidden = (dot_t(cot, side["ffn_down"]) * slope).astype(BF)
        d_normed_ffn = d_normed_ffn + dot_t(d_hidden, side["ffn_up"])
        total = total + mix(gelu, side["ffn_down"])
        gelus.append(gelu[:, None, :])
        d_hiddens.append(d_hidden[:, None, :])
    out_a, out_b = both_clips(to_frames(total.astype(BF)))
    grad_down = reduce_grad(cot, gelus[0], gelus[1], sizes, bits, False)
    grad_up = reduce_grad(normed_ffn, d_hiddens[0], d_hiddens[1], sizes, bits, True)
    d_values, d_gain_ffn = norm_back(latest, gain_ffn, ffn_stats, d_normed_ffn)
    d_latest = (cot.astype(F32) + d_values).astype(BF)
    d_middle, d_gain_time, grad_time_qkv, grad_time_out = branch_back(
        d_latest, middle, gain_time, "time", time_groups, time_saved, True
    )
    d_middle = to_frames(d_middle.astype(BF))
    d_started, d_gain_space, grad_space_qkv, grad_space_out = branch_back(
        d_middle, started, gain_space, "space", space_groups, space_saved, True
    )
    d_frames_a, d_frames_b = both_clips(d_started.astype(BF))
    frame_sums = jnp.concatenate(
        [
            jnp.sum(d_started[:rows_a].reshape(n_frames, grid_a, width), 1),
            jnp.sum(d_started[rows_a:].reshape(n_frames, grid_b, width), 1),
        ]
    )
    d_table = jnp.einsum("fa,fd->ad", one_hot, frame_sums, precision=lax.Precision.HIGHEST)
    small = reduce_small(
        jnp.concatenate([d_table, d_gain_space[None], d_gain_time[None], d_gain_ffn[None]]), sizes, bits
    )
    n_codes = action_table.shape[0]
    return (
        out_a,
        out_b,
        d_frames_a,
        d_frames_b,
        small[:n_codes],
        small[n_codes],
        grad_space_qkv,
        grad_space_out,
        small[n_codes + 1],
        grad_time_qkv,
        grad_time_out,
        small[n_codes + 2],
        grad_up[:, 0, :],
        grad_down[:, 0, :].T,
    )


def solution(mesh):
    sizes = dict(mesh.shape)
    return jax.shard_map(
        partial(per_device, sizes),
        mesh=mesh,
        in_specs=(
            P("clip", "wide", None, None),
            P("clip", "wide", None, None),
            P("clip", "wide"),
            P("clip", "wide"),
            P(),
            P(),
            P(None, None, "tp"),
            P("tp", None),
            P(),
            P(None, None, "tp"),
            P("tp", None),
            P(),
            P(None, "tp"),
            P("tp", None),
            P("clip", "wide", None, None),
            P("clip", "wide", None, None),
        ),
        out_specs=(
            P("clip", "wide", None, None),
            P("clip", "wide", None, None),
            P("clip", "wide", None, None),
            P("clip", "wide", None, None),
            P(None, "wide"),
            P("wide"),
            P(None, "wide", "tp"),
            P("tp", "wide"),
            P("wide"),
            P(None, "wide", "tp"),
            P("tp", "wide"),
            P("wide"),
            P("wide", "tp"),
            P("tp", "wide"),
        ),
        check_vma=False,
    )
```

time: 1360 us -> 922 us (0.68)
  waiting for transfers between devices: 779 us -> 209 us
  Pallas kernels: 0 us -> 73.6 us
  starting transfers between devices: 47.6 us -> 113 us
  local copies, waits for them, and re-layouts: 190 us -> 240 us
  other arithmetic: 103 us -> 79.3 us
  blocking collectives: 18.9 us -> 0 us
  between operations: 16.8 us -> 2.67 us
    psum x6 -> x0, waiting for transfers between devices: 400 us -> none  [the longest x2 150 us: settle(): lax.psum(partials[1].astype(jnp.bfloat16), 'tp').astype(jnp.float32)]
    ppermute x0 -> x98, waiting for transfers between devices: none -> 209 us  [swap(): return lax.ppermute(value, axis, [(i, i ^ step) for i in range(size)])]
    unnamed x19 -> x0, waiting for transfers between devices: 186 us -> none
    all_to_all x8 -> x4, waiting for transfers between devices: 144 us -> 0.01 us  [the longest x2 0.01 us: to_frames(): lax.all_to_all(packed, 'wide', split_axis=0, concat_axis=0, tiled=True)]
    ppermute x0 -> x98, starting transfers between devices: none -> 93.9 us  [swap(): return lax.ppermute(value, axis, [(i, i ^ step) for i in range(size)])]
    dynamic_slice x0 -> x43, local copies, waits for them, and re-layouts: none -> 90.8 us  [the longest x37 79.8 us: take(): return lax.dynamic_index_in_dim(value, index, axis, keepdims=False)]
    pallas_call x0 -> x8, Pallas kernels: none -> 73.6 us  [the longest x4 39.7 us: attend_back(): pl.pallas_call(partial(attend_back_kernel, groups), grid=(width // PAIR,)...]
    reduce_sum x26 -> x7, other arithmetic: 53.6 us -> 4.6 us  [the longest x3 2.66 us: norm_stats(): spread = jnp.mean(centered * centered, -1, keepdims=True)]
  transfers between devices with their start and end apart: 21 -> 102, of which waited for: 21 -> 35; matrix products, arithmetic and copies ran while one was open for 16% -> 35% of each run, Pallas kernels for 0% -> 4%
where the time goes in v1:
time: 922 us; the launch traced here: 911 us
  local copies, waits for them, and re-layouts  240 us (26%)
  waiting for transfers between devices  209 us (23%)
  matrix products  193 us (21%)
  starting transfers between devices  113 us (12%)
  other arithmetic  79.3 us (9%)
  Pallas kernels  73.6 us (8%)
    ppermute x98, waiting for transfers between devices, swap(): return lax.ppermute(value, axis, [(i, i ^ step) for i in range(size)])  209 us
    ppermute x98, starting transfers between devices, swap(): return lax.ppermute(value, axis, [(i, i ^ step) for i in range(size)])  93.9 us
    dot_general x48, matrix products, product(): return jnp.einsum('nd,ntk->dtk', a, b, preferred_element_type=F32)  90 us
    dynamic_slice x37, local copies, waits for them, and re-layouts, take(): return lax.dynamic_index_in_dim(value, index, axis, keepdims=False)  79.8 us
    pallas_call x4, Pallas kernels, attend_back(): pl.pallas_call(partial(attend_back_kernel, groups), grid=(width // PAIR,)...  39.7 us
    dynamic_update_slice x24, local copies, waits for them, and re-layouts, put(): lax.dynamic_update_slice(whole, piece, (*lead, (2 * clip_at + core_at) *...  35.2 us
    pallas_call x4, Pallas kernels, attend(): pl.pallas_call(partial(attend_kernel, groups), grid=(width // PAIR,), in_...  34 us
    dot_general x8, matrix products, dot_t(): lax.dot_general(a, b, (((1,), (1,)), ((), ())), preferred_element_type=F32)  33.2 us
  transfers between devices with their start and end apart: 102, of which 35 were waited for; matrix products, arithmetic and copies ran while one was open for 35% of the time, Pallas kernels for 4%

profile of v1, /device:TPU:0, one launch (start us, length us, event | category | flops | bytes accessed | tf_op | source)
XLA Modules:
  0.0 910.7 jit_solution(8985595567860525866)
XLA Ops:
  64.6 7.7 attend.4
  94.9 9.4 %collective-permute-done.13 = bf16[128,1024]{1,0:T(8,128)(2,1)} collective-permute-done((bf16[128,1024]{1,0:T(8,128)(2,1)}, bf16[128,1024]{1,0:T(8,128)(2,1)}, u32[]{:S(2)}, u32[]{:S(2)}) %collective-permute-start.13) | collective-permute-done | bytes 262176 | tf_op jit(solution)/shard_map/ppermute | solution.py:157
  119.9 14.8 %collective-permute-done.8 = bf16[3,256,512]{2,1,0:T(8,128)(2,1)} collective-permute-done((bf16[3,256,512]{2,1,0:T(8,128)(2,1)S(1)}, bf16[3,256,512]{2,1,0:T(8,128)(2,1)}, u32[]{:S(2)}, u32[]{:S(2)}) %collective-permute-start.8) | collective-permute-done | bytes 786464 | tf_op jit(solution)/shard_map/ppermute | solution.py:157
  141.3 7.2 attend.5
  179.1 21.8 %collective-permute-done.17 = bf16[256,2048]{1,0:T(8,128)(2,1)} collective-permute-done((bf16[256,2048]{1,0:T(8,128)(2,1)}, bf16[256,2048]{1,0:T(8,128)(2,1)}, u32[]{:S(2)}, u32[]{:S(2)}) %collective-permute-start.17) | collective-permute-done | bytes 1048608 | tf_op jit(solution)/shard_map/ppermute | solution.py:157
  258.9 9.5 %attend.6 = (bf16[640,512]{1,0:T(8,128)(2,1)}, f32[640,512]{1,0:T(8,128)}) custom-call(bf16[3,640,512]{2,1,0:T(8,128)(2,1)} %convert_bitcast_fusion.2.p_ref), custom_call_target="tpu_custom_call" | custom-call | flops 671088640 | bytes 3932160 | tf_op jit(solution)/shard_map/attend/pallas_call | solution.py:101
  268.4 9.5 %attend.7 = (bf16[640,512]{1,0:T(8,128)(2,1)}, f32[640,512]{1,0:T(8,128)}) custom-call(bf16[3,640,512]{2,1,0:T(8,128)(2,1)} %convert_bitcast_fusion.1.p_ref), custom_call_target="tpu_custom_call" | custom-call | flops 671088640 | bytes 3932160 | tf_op jit(solution)/shard_map/attend/pallas_call | solution.py:101
  305.7 8.8 multiply_convert_fusion
  391.6 10.0 %attend_back.5 = bf16[3,640,512]{2,1,0:T(8,128)(2,1)} custom-call(bf16[3,640,512]{2,1,0:T(8,128)(2,1)} %convert_bitcast_fusion.1.p_ref, bf16[640,512]{1,0:T(8,128)(2,1)} %convolution_convert_fusion.18.d_ref, f32[640,512]{1,0:T(8,128)} %get-tuple-element.27.l_ref), custom_call_target="tpu_custom_call" | custom-call | flops 1677721600 | bytes 5898240 | tf_op jit(solution)/shard_map/attend_back/pallas_call | solution.py:119
  424.0 10.2 %attend_back.4 = bf16[3,640,512]{2,1,0:T(8,128)(2,1)} custom-call(bf16[3,640,512]{2,1,0:T(8,128)(2,1)} %convert_bitcast_fusion.2.p_ref, bf16[640,512]{1,0:T(8,128)(2,1)} %convolution_convert_fusion.19.d_ref, f32[640,512]{1,0:T(8,128)} %get-tuple-element.26.l_ref), custom_call_target="tpu_custom_call" | custom-call | flops 1677721600 | bytes 5898240 | tf_op jit(solution)/shard_map/attend_back/pallas_call | solution.py:119
  465.9 6.7 multiply_reduce_fusion
  507.4 28.4 %collective-permute-done.73 = bf16[128,1,256]{0,2,1:T(8,128)(2,1)} collective-permute-done((bf16[128,1,256]{0,2,1:T(8,128)(2,1)}, bf16[128,1,256]{0,2,1:T(8,128)(2,1)}, u32[]{:S(2)}, u32[]{:S(2)}) %collective-permute-start.73) | collective-permute-done | bytes 65568 | tf_op jit(solution)/shard_map/ppermute | solution.py:157
  556.1 12.1 %collective-permute-done.59 = bf16[512,3,256]{2,0,1:T(8,128)(2,1)S(1)} collective-permute-done((bf16[512,3,256]{2,0,1:T(8,128)(2,1)S(1)}, bf16[512,3,256]{2,0,1:T(8,128)(2,1)S(1)}, u32[]{:S(2)}, u32[]{:S(2)}) %collective-permute-start.59) | collective-permute-done | bytes 786464 | tf_op jit(solution)/shard_map/ppermute | solution.py:157
  576.7 13.9 %collective-permute-done.81 = bf16[512,1,1024]{2,0,1:T(8,128)(2,1)S(1)} collective-permute-done((bf16[512,1,1024]{2,0,1:T(8,128)(2,1)S(1)}, bf16[512,1,1024]{2,0,1:T(8,128)(2,1)S(1)}, u32[]{:S(2)}, u32[]{:S(2)}) %collective-permute-start.81) | collective-permute-done | bytes 1048608 | tf_op jit(solution)/shard_map/ppermute | solution.py:157
  608.9 9.7 %attend_back.6 = bf16[3,640,512]{2,1,0:T(8,128)(2,1)} custom-call(bf16[3,640,512]{2,1,0:T(8,128)(2,1)} %convert_bitcast_fusion.4.p_ref, bf16[640,512]{1,0:T(8,128)(2,1)} %convolution_convert_fusion.17.d_ref, f32[640,512]{1,0:T(8,128)} %get-tuple-element.28.l_ref), custom_call_target="tpu_custom_call" | custom-call | flops 1677721600 | bytes 5898240 | tf_op jit(solution)/shard_map/attend_back/pallas_call | solution.py:119
  624.8 9.7 %attend_back.7 = bf16[3,640,512]{2,1,0:T(8,128)(2,1)} custom-call(bf16[3,640,512]{2,1,0:T(8,128)(2,1)} %convert_bitcast_fusion.3.p_ref, bf16[640,512]{1,0:T(8,128)(2,1)} %convolution_convert_fusion.16.d_ref, f32[640,512]{1,0:T(8,128)} %get-tuple-element.29.l_ref), custom_call_target="tpu_custom_call" | custom-call | flops 1677721600 | bytes 5898240 | tf_op jit(solution)/shard_map/attend_back/pallas_call | solution.py:119
  634.6 6.8 multiply_reduce_fusion.1
  710.5 7.4 collective-permute-done.62
  750.5 7.0 collective-permute-done.89
  767.5 14.3 %collective-permute-done.78 = bf16[512,1,1024]{2,0,1:T(8,128)(2,1)} collective-permute-done((bf16[512,1,1024]{2,0,1:T(8,128)(2,1)}, bf16[512,1,1024]{2,0,1:T(8,128)(2,1)}, u32[]{:S(2)}, u32[]{:S(2)}) %collective-permute-start.78) | collective-permute-done | bytes 1048608 | tf_op jit(solution)/shard_map/ppermute | solution.py:157
  820.6 11.7 %collective-permute-start.83 = (bf16[128,1,1024]{0,2,1:T(8,128)(2,1)}, bf16[128,1,1024]{0,2,1:T(8,128)(2,1)S(1)}, u32[]{:S(2)}, u32[]{:S(2)}) collective-permute-start(bf16[128,1,1024]{0,2,1:T(8,128)(2,1)} %bitcast.604), channel_id=1, source_target_pairs={{0,4},{2,6},{4,0},{6,2},{8,12},{10,14},{12,8},{14,10},{1,5},{3,7},... | collective-permute-start | bytes 786440 | tf_op jit(solution)/shard_map/ppermute | solution.py:157
  850.8 9.0 collective-permute-done.37
  868.0 6.8 collective-permute-done.34
  879.5 6.4 collective-permute-start.39
  (685 shorter events, 649.2 us)
Async XLA Ops:
  2.5 81.8 %collective-permute-start.12 = (bf16[128,1024]{1,0:T(8,128)(2,1)}, bf16[128,1024]{1,0:T(8,128)(2,1)}, u32[]{:S(2)}, u32[]{:S(2)}) collective-permute-start(bf16[128,1024]{1,0:T(8,128)(2,1)} %constant_dynamic-slice_fusion.35), channel_id=1, source_target_pairs={{0,1},{1,0},{2,3},{3,2},{4,5},{5,4},{6,7},{7,6},{8,9},{9,8},{10,11... | collective-permute-start | bytes 786440 | tf_op jit(solution)/shard_map/ppermute | solution.py:157
  7.1 80.2 %collective-permute-start.4 = (bf16[128,1024]{1,0:T(8,128)(2,1)}, bf16[128,1024]{1,0:T(8,128)(2,1)S(1)}, u32[]{:S(2)}, u32[]{:S(2)}) collective-permute-start(bf16[128,1024]{1,0:T(8,128)(2,1)} %constant_dynamic-slice_fusion.37), channel_id=1, source_target_pairs={{0,1},{1,0},{2,3},{3,2},{4,5},{5,4},{6,7},{7,6},{8,9},{9,8},{10,11... | collective-permute-start | bytes 786440 | tf_op jit(solution)/shard_map/ppermute | solution.py:157
  9.2 68.8 %collective-permute-start = (bf16[3,256,512]{2,1,0:T(8,128)(2,1)}, bf16[3,256,512]{2,1,0:T(8,128)(2,1)}, u32[]{:S(2)}, u32[]{:S(2)}) collective-permute-start(bf16[3,256,512]{2,1,0:T(8,128)(2,1)} %constant_dynamic-slice_fusion.38), channel_id=1, source_target_pairs={{0,1},{1,0},{2,3},{3,2},{4,5},{5,4},{6,7},{7,6},{8,9},{9,8},{10,11... | collective-permute-start | bytes 2359304 | tf_op jit(solution)/shard_map/ppermute | solution.py:157
  14.9 143.6 %all-to-all-start.2 = ((bf16[8,2,40,1024]{3,2,1,0:T(8,128)(2,1)}), bf16[8,2,40,1024]{3,2,1,0:T(8,128)(2,1)}, u32[]{:S(2)}, u32[]{:S(2)}) async-start(bf16[8,2,40,1024]{3,2,1,0:T(8,128)(2,1)} %copy.156), calls=%async_computation.2 | async-start | bytes 2621440 | tf_op jit(solution)/shard_map/all_to_all | solution.py:335
  91.6 43.7 %collective-permute-start.20 = (bf16[512,1024]{1,0:T(8,128)(2,1)}, bf16[512,1024]{1,0:T(8,128)(2,1)}, u32[]{:S(2)}, u32[]{:S(2)}) collective-permute-start(bf16[512,1024]{1,0:T(8,128)(2,1)} %constant_dynamic-slice_fusion.33), channel_id=1, source_target_pairs={{0,1},{1,0},{2,3},{3,2},{4,5},{5,4},{6,7},{7,6},{8,9},{9,8},{10,11... | collective-permute-start | bytes 3145736 | tf_op jit(solution)/shard_map/ppermute | solution.py:157
  115.8 41.0 %collective-permute-start.16 = (bf16[256,2048]{1,0:T(8,128)(2,1)}, bf16[256,2048]{1,0:T(8,128)(2,1)}, u32[]{:S(2)}, u32[]{:S(2)}) collective-permute-start(bf16[256,2048]{1,0:T(8,128)(2,1)} %constant_dynamic-slice_fusion.34), channel_id=1, source_target_pairs={{0,1},{1,0},{2,3},{3,2},{4,5},{5,4},{6,7},{7,6},{8,9},{9,8},{10,11... | collective-permute-start | bytes 3145736 | tf_op jit(solution)/shard_map/ppermute | solution.py:157
  134.7 42.6 %collective-permute-start.10 = (bf16[3,256,512]{2,1,0:T(8,128)(2,1)}, bf16[3,256,512]{2,1,0:T(8,128)(2,1)}, u32[]{:S(2)}, u32[]{:S(2)}) collective-permute-start(bf16[3,256,512]{2,1,0:T(8,128)(2,1)} %collective-permute-done.8), channel_id=1, source_target_pairs={{0,2},{2,0},{4,6},{6,4},{8,10},{10,8},{12,14},{14,12},{1,3},{3,1},... | collective-permute-start | bytes 2359304 | tf_op jit(solution)/shard_map/ppermute | solution.py:157
  135.9 67.4 %collective-permute-start.22 = (bf16[512,1024]{1,0:T(8,128)(2,1)}, bf16[512,1024]{1,0:T(8,128)(2,1)}, u32[]{:S(2)}, u32[]{:S(2)}) collective-permute-start(bf16[512,1024]{1,0:T(8,128)(2,1)} %collective-permute-done.20), channel_id=1, source_target_pairs={{0,2},{2,0},{4,6},{6,4},{8,10},{10,8},{12,14},{14,12},{1,3},{3,1},... | collective-permute-start | bytes 3145736 | tf_op jit(solution)/shard_map/ppermute | solution.py:157
  156.8 44.2 %collective-permute-start.17 = (bf16[256,2048]{1,0:T(8,128)(2,1)}, bf16[256,2048]{1,0:T(8,128)(2,1)}, u32[]{:S(2)}, u32[]{:S(2)}) collective-permute-start(bf16[256,2048]{1,0:T(8,128)(2,1)} %collective-permute-done.16), channel_id=1, source_target_pairs={{0,16},{16,0},{1,17},{17,1},{2,18},{18,2},{3,19},{19,3},{4,20},{20... | collective-permute-start | bytes 3145736 | tf_op jit(solution)/shard_map/ppermute | solution.py:157
  158.4 78.0 %all-to-all-start = ((bf16[8,2,40,1024]{3,2,1,0:T(8,128)(2,1)}), bf16[8,2,40,1024]{3,2,1,0:T(8,128)(2,1)}, u32[]{:S(2)}, u32[]{:S(2)}) async-start(bf16[8,2,40,1024]{3,2,1,0:T(8,128)(2,1)} %copy_bitcast_fusion), calls=%async_computation | async-start | bytes 2621440 | tf_op jit(solution)/shard_map/all_to_all | solution.py:335
  165.8 42.2 %collective-permute-start.18 = (bf16[256,2048]{1,0:T(8,128)(2,1)}, bf16[256,2048]{1,0:T(8,128)(2,1)S(1)}, u32[]{:S(2)}, u32[]{:S(2)}) collective-permute-start(bf16[256,2048]{1,0:T(8,128)(2,1)} %collective-permute-done.16), channel_id=1, source_target_pairs={{0,2},{2,0},{4,6},{6,4},{8,10},{10,8},{12,14},{14,12},{1,3},{3,1},... | collective-permute-start | bytes 3145736 | tf_op jit(solution)/shard_map/ppermute | solution.py:157
  177.3 52.4 %collective-permute-start.11 = (bf16[3,256,512]{2,1,0:T(8,128)(2,1)}, bf16[3,256,512]{2,1,0:T(8,128)(2,1)}, u32[]{:S(2)}, u32[]{:S(2)}) collective-permute-start(bf16[3,256,512]{2,1,0:T(8,128)(2,1)} %collective-permute-done.9), channel_id=1, source_target_pairs={{0,2},{2,0},{4,6},{6,4},{8,10},{10,8},{12,14},{14,12},{1,3},{3,1},... | collective-permute-start | bytes 2359304 | tf_op jit(solution)/shard_map/ppermute | solution.py:157
  178.9 52.9 %collective-permute-start.23 = (bf16[512,1024]{1,0:T(8,128)(2,1)}, bf16[512,1024]{1,0:T(8,128)(2,1)}, u32[]{:S(2)}, u32[]{:S(2)}) collective-permute-start(bf16[512,1024]{1,0:T(8,128)(2,1)} %collective-permute-done.21), channel_id=1, source_target_pairs={{0,2},{2,0},{4,6},{6,4},{8,10},{10,8},{12,14},{14,12},{1,3},{3,1},... | collective-permute-start | bytes 3145736 | tf_op jit(solution)/shard_map/ppermute | solution.py:157
  458.4 78.9 %collective-permute-start.58 = (bf16[512,3,256]{2,0,1:T(8,128)(2,1)}, bf16[512,3,256]{2,0,1:T(8,128)(2,1)}, u32[]{:S(2)}, u32[]{:S(2)}) collective-permute-start(bf16[512,3,256]{2,0,1:T(8,128)(2,1)} %convolution_convert_fusion.8), channel_id=1, source_target_pairs={{0,2},{2,0},{4,6},{6,4},{8,10},{10,8},{12,14},{14,12},{1,3},{3,1},... | collective-permute-start | bytes 2359304 | tf_op jit(solution)/shard_map/ppermute | solution.py:157
  458.9 82.5 %collective-permute-start.55 = (bf16[512,3,256]{2,0,1:T(8,128)(2,1)}, bf16[512,3,256]{2,0,1:T(8,128)(2,1)}, u32[]{:S(2)}, u32[]{:S(2)}) collective-permute-start(bf16[512,3,256]{2,0,1:T(8,128)(2,1)} %convolution_convert_fusion.10), channel_id=1, source_target_pairs={{0,2},{2,0},{4,6},{6,4},{8,10},{10,8},{12,14},{14,12},{1,3},{3,1},... | collective-permute-start | bytes 2359304 | tf_op jit(solution)/shard_map/ppermute | solution.py:157
  493.9 98.3 %all-to-all-start.3 = ((bf16[8,2,40,1024]{3,2,1,0:T(8,128)(2,1)}), bf16[8,2,40,1024]{3,2,1,0:T(8,128)(2,1)}, u32[]{:S(2)}, u32[]{:S(2)}) async-start(bf16[8,2,40,1024]{3,2,1,0:T(8,128)(2,1)} %bitcast.562), calls=%async_computation.3 | async-start | bytes 2621440 | tf_op jit(solution)/shard_map/all_to_all | solution.py:340
  568.2 118.4 %collective-permute-start.54 = (bf16[512,3,256]{2,0,1:T(8,128)(2,1)}, bf16[512,3,256]{2,0,1:T(8,128)(2,1)}, u32[]{:S(2)}, u32[]{:S(2)}) collective-permute-start(bf16[512,3,256]{2,0,1:T(8,128)(2,1)} %convolution_convert_fusion.11), channel_id=1, source_target_pairs={{0,2},{2,0},{4,6},{6,4},{8,10},{10,8},{12,14},{14,12},{1,3},{3,1},... | collective-permute-start | bytes 2359304 | tf_op jit(solution)/shard_map/ppermute | solution.py:157
  569.3 118.5 %collective-permute-start.56 = (bf16[512,3,256]{2,0,1:T(8,128)(2,1)}, bf16[512,3,256]{2,0,1:T(8,128)(2,1)}, u32[]{:S(2)}, u32[]{:S(2)}) collective-permute-start(bf16[512,3,256]{2,0,1:T(8,128)(2,1)} %add_convert_fusion.4), channel_id=1, source_target_pairs={{0,1},{1,0},{2,3},{3,2},{4,5},{5,4},{6,7},{7,6},{8,9},{9,8},{10,11... | collective-permute-start | bytes 2359304 | tf_op jit(solution)/shard_map/ppermute | solution.py:157
  574.1 113.7 %collective-permute-start.60 = (bf16[512,3,256]{2,0,1:T(8,128)(2,1)}, bf16[512,3,256]{2,0,1:T(8,128)(2,1)}, u32[]{:S(2)}, u32[]{:S(2)}) collective-permute-start(bf16[512,3,256]{2,0,1:T(8,128)(2,1)} %add_convert_fusion.2), channel_id=1, source_target_pairs={{0,16},{16,0},{1,17},{17,1},{2,18},{18,2},{3,19},{19,3},{4,20},{20... | collective-permute-start | bytes 2359304 | tf_op jit(solution)/shard_map/ppermute | solution.py:157
  592.2 83.8 %all-to-all-start.1 = ((bf16[8,2,40,1024]{3,2,1,0:T(8,128)(2,1)}), bf16[8,2,40,1024]{3,2,1,0:T(8,128)(2,1)}, u32[]{:S(2)}, u32[]{:S(2)}) async-start(bf16[8,2,40,1024]{3,2,1,0:T(8,128)(2,1)} %bitcast.561), calls=%async_computation.1 | async-start | bytes 2621440 | tf_op jit(solution)/shard_map/all_to_all | solution.py:340
  743.1 40.9 %collective-permute-start.82 = (bf16[512,1,1024]{2,0,1:T(8,128)(2,1)}, bf16[512,1,1024]{2,0,1:T(8,128)(2,1)}, u32[]{:S(2)}, u32[]{:S(2)}) collective-permute-start(bf16[512,1,1024]{2,0,1:T(8,128)(2,1)} %fusion.36), channel_id=1, source_target_pairs={{0,16},{16,0},{1,17},{17,1},{2,18},{18,2},{3,19},{19,3},{4,20},{20... | collective-permute-start | bytes 3145736 | tf_op jit(solution)/shard_map/ppermute | solution.py:157
  757.5 84.2 %collective-permute-start.24 = (bf16[640,1024]{1,0:T(8,128)(2,1)}, bf16[640,1024]{1,0:T(8,128)(2,1)}, u32[]{:S(2)}, u32[]{:S(2)}) collective-permute-start(bf16[640,1024]{1,0:T(8,128)(2,1)} %pad_maximum_fusion.2), channel_id=1, source_target_pairs={{0,1},{1,0},{2,3},{3,2},{4,5},{5,4},{6,7},{7,6},{8,9},{9,8},{10,11... | collective-permute-start | bytes 3932168 | tf_op jit(solution)/shard_map/ppermute | solution.py:157
  759.4 87.4 %collective-permute-start.25 = (bf16[640,1024]{1,0:T(8,128)(2,1)}, bf16[640,1024]{1,0:T(8,128)(2,1)}, u32[]{:S(2)}, u32[]{:S(2)}) collective-permute-start(bf16[640,1024]{1,0:T(8,128)(2,1)} %get-tuple-element.107), channel_id=1, source_target_pairs={{0,1},{1,0},{2,3},{3,2},{4,5},{5,4},{6,7},{7,6},{8,9},{9,8},{10,11... | collective-permute-start | bytes 3932168 | tf_op jit(solution)/shard_map/ppermute | solution.py:157
  846.8 41.0 %collective-permute-start.97 = (bf16[128,1,1024]{0,2,1:T(8,128)(2,1)}, bf16[128,1,1024]{0,2,1:T(8,128)(2,1)S(1)}, u32[]{:S(2)}, u32[]{:S(2)}) collective-permute-start(bf16[128,1,1024]{0,2,1:T(8,128)(2,1)} %fusion.130), channel_id=1, source_target_pairs={{0,16},{16,0},{1,17},{17,1},{2,18},{18,2},{3,19},{19,3},{4,20},{20... | collective-permute-start | bytes 786440 | tf_op jit(solution)/shard_map/ppermute | solution.py:157
  (187 other events, 2549.0 us)

commit v2 on v0

v2 whole, which is shorter than its diff:
```python
from functools import partial

import jax
import jax.numpy as jnp
from jax import lax
from jax.experimental import pallas as pl
from jax.experimental.pallas import tpu as pltpu
from jax.sharding import PartitionSpec as P

HEAD = 64
PAIR = 2 * HEAD
BLOCK = 2 * PAIR
BF = jnp.bfloat16
F32 = jnp.float32
LIMIT = 60 * 2**20


def dot_n(a, b):
    return lax.dot_general(a, b, (((1,), (0,)), ((), ())), preferred_element_type=F32)


def dot_t(a, b):
    return lax.dot_general(a, b, (((1,), (1,)), ((), ())), preferred_element_type=F32)


def shape_of(*dims, dtype=BF):
    return jax.ShapeDtypeStruct(dims, dtype)


def whole(*dims):
    return pl.BlockSpec(dims, lambda *_: (0,) * len(dims))


def any_spec():
    return pl.BlockSpec(memory_space=pl.ANY)


def params():
    return pltpu.CompilerParams(vmem_limit_bytes=LIMIT)


def cost(micros):
    return pl.CostEstimate(flops=int(micros * 4e9), bytes_accessed=2**20, transcendentals=0)


def group_mask(kind, length):
    if kind is None:
        return None
    name, size, inner = kind
    key = lax.broadcasted_iota(jnp.int32, (length, length), 0)
    query = lax.broadcasted_iota(jnp.int32, (length, length), 1)
    if name == "block":
        shift = size.bit_length() - 1
        return (query >> shift) == (key >> shift)
    shift = inner.bit_length() - 1
    return ((query & (inner - 1)) == (key & (inner - 1))) & ((key >> shift) <= (query >> shift))


def head_masks(value):
    lane = lax.broadcasted_iota(jnp.int32, (1, PAIR), 1)
    return (
        jnp.where(lane < HEAD, value, 0.0).astype(BF),
        jnp.where(lane < HEAD, 0.0, value).astype(BF),
    )


def attend_block(groups, proj_ref, heads_ref, logs_ref):
    scaled = head_masks(HEAD**-0.5)
    masks = {kind: group_mask(kind, length) for _, length, kind in groups}
    for pair in range(2):
        cols = slice(pair * PAIR, (pair + 1) * PAIR)
        for start, length, kind in groups:
            rows = slice(start, start + length)
            query, key, value = (proj_ref[i, rows, cols] for i in range(3))
            value_t = value.T
            outs = []
            for h in range(2):
                scores = dot_t(key * scaled[h], query)
                if kind is not None:
                    scores = jnp.where(masks[kind], scores, -1e30)
                largest = jnp.max(scores, 0, keepdims=True)
                shifted = jnp.exp(scores - largest)
                total = jnp.sum(shifted, 0, keepdims=True)
                out = dot_n(value_t[h * HEAD : (h + 1) * HEAD], shifted.astype(BF))
                outs.append(out * (1.0 / total))
                if logs_ref is not None:
                    logs_ref[2 * pair + h : 2 * pair + h + 1, rows] = largest + jnp.log(total)
            heads_ref[rows, cols] = jnp.concatenate(outs, 0).T.astype(BF)


def attend_back_block(groups, proj_ref, d_ref, logs_ref, o_ref):
    scale = HEAD**-0.5
    scaled = head_masks(scale)
    parts = head_masks(1.0)
    masks = {kind: group_mask(kind, length) for _, length, kind in groups}
    for pair in range(2):
        cols = slice(pair * PAIR, (pair + 1) * PAIR)
        for start, length, kind in groups:
            rows = slice(start, start + length)
            query, key, value = (proj_ref[i, rows, cols] for i in range(3))
            d_out = d_ref[rows, cols]
            key_t = key.T
            d_key = d_value = None
            d_query = []
            for h in range(2):
                soft = jnp.exp(
                    dot_t(key * scaled[h], query) - logs_ref[2 * pair + h : 2 * pair + h + 1, rows]
                )
                if kind is not None:
                    soft = jnp.where(masks[kind], soft, 0.0)
                d_soft = dot_t(value * parts[h], d_out)
                row_dot = jnp.sum(soft * d_soft, 0, keepdims=True)
                d_scores = (soft * (d_soft - row_dot)).astype(BF)
                key_term = dot_n(d_scores, query * parts[h])
                value_term = dot_n(soft.astype(BF), d_out * parts[h])
                d_key = key_term if h == 0 else d_key + key_term
                d_value = value_term if h == 0 else d_value + value_term
                d_query.append(dot_n(key_t[h * HEAD : (h + 1) * HEAD], d_scores))
            o_ref[0, rows, cols] = (jnp.concatenate(d_query, 0).T * scale).astype(BF)
            o_ref[1, rows, cols] = (d_key * scale).astype(BF)
            o_ref[2, rows, cols] = d_value.astype(BF)


def row_chunks(rows, size=64):
    return [slice(i, i + size) for i in range(0, rows, size)]


def norm_parts(values):
    centered = values - jnp.mean(values, -1, keepdims=True)
    inverse = lax.rsqrt(jnp.mean(centered * centered, -1, keepdims=True) + 1e-05)
    return centered * inverse, inverse


def project_block(normed_ref, weight, proj_ref):
    for i in range(3):
        proj_ref[i] = dot_n(normed_ref[...], weight(i)).astype(BF)


def space_kernel(groups, full, _, fa_ref, fb_ref, shift_ref, gain_ref, w_ref, *refs):
    if full:
        heads_ref, proj_ref, logs_ref, started_ref, normed_ref = refs
        proj, logs = proj_ref.at[0], logs_ref.at[0]
    else:
        heads_ref, proj, normed_ref = refs
        logs = None
    _, frames, grid_a, _ = fa_ref.shape
    grid_b = fb_ref.shape[2]

    @pl.when(pl.program_id(0) == 0)
    def _():
        gain = gain_ref[...]
        base = 0
        for frame_ref, grid, first in ((fa_ref, grid_a, 0), (fb_ref, grid_b, frames)):
            for f in range(frames):
                move = shift_ref[0, first + f : first + f + 1, :]
                for rows in row_chunks(grid):
                    values = frame_ref[0, f, rows, :].astype(F32) + move
                    out = slice(base + rows.start, base + rows.stop)
                    if full:
                        started_ref[out, :] = values
                    normed_ref[out, :] = (norm_parts(values)[0] * gain).astype(BF)
                base += grid

    project_block(normed_ref, lambda i: w_ref[i], proj)
    attend_block(groups, proj, heads_ref.at[0], logs)


def space_heads(clip, frames_a, frames_b, shifts, gain, qkv, groups, full):
    _, frames, grid_a, depth = frames_a.shape
    grid_b = frames_b.shape[2]
    rows = frames * (grid_a + grid_b)
    blocks = qkv.shape[2] // BLOCK

    def chosen(*dims):
        return pl.BlockSpec((1, *dims), lambda s, c: (c[0],) + (0,) * len(dims))

    heads = (pl.BlockSpec((1, rows, BLOCK), lambda s, c: (s, 0, 0)), shape_of(blocks, rows, BLOCK))
    if full:
        outs = [
            heads,
            (pl.BlockSpec((1, 3, rows, BLOCK), lambda s, c: (s, 0, 0, 0)), shape_of(blocks, 3, rows, BLOCK)),
            (pl.BlockSpec((1, 8, rows), lambda s, c: (s, 0, 0)), shape_of(blocks, 8, rows, dtype=F32)),
            (whole(rows, depth), shape_of(rows, depth, dtype=F32)),
            (whole(rows, depth), shape_of(rows, depth)),
        ]
        scratch = []
    else:
        outs = [heads]
        scratch = [pltpu.VMEM((3, rows, BLOCK), BF), pltpu.VMEM((rows, depth), BF)]
    return pl.pallas_call(
        partial(space_kernel, groups, full),
        grid_spec=pltpu.PrefetchScalarGridSpec(
            num_scalar_prefetch=1,
            grid=(blocks,),
            in_specs=[
                chosen(frames, grid_a, depth),
                chosen(frames, grid_b, depth),
                chosen(2 * frames, depth),
                whole(1, depth),
                pl.BlockSpec((3, depth, BLOCK), lambda s, c: (0, 0, s)),
            ],
            out_specs=[o[0] for o in outs],
            scratch_shapes=scratch,
        ),
        out_shape=[o[1] for o in outs],
        compiler_params=params(),
        cost_estimate=cost(12),
        name="space_own" if full else "space_partner",
    )(clip, frames_a, frames_b, shifts, gain, qkv)


def stream_weights(own_qkv, own_out, qkv_slots, out_slots, wq, wo, sems, step, steps, first=0):
    def start(index, slot):
        for s in range(steps):

            @pl.when(index == s)
            def _(s=s):
                if s + first < 2:
                    cols = pl.ds((s + first) * BLOCK, BLOCK)
                    pltpu.make_async_copy(own_qkv.at[:, :, cols], wq.at[slot], sems.at[slot, 0]).start()
                    if wo is not None:
                        pltpu.make_async_copy(own_out.at[cols, :], wo.at[slot], sems.at[slot, 1]).start()
                else:
                    for i in range(2):
                        part = 2 * (s + first - 2) + i
                        cols = pl.ds(i * PAIR, PAIR)
                        pltpu.make_async_copy(
                            qkv_slots[part].at[0:3], wq.at[slot, :, :, cols], sems.at[slot, 0]
                        ).start()
                        if wo is None:
                            continue
                        if out_slots is not None:
                            pltpu.make_async_copy(
                                out_slots[part], wo.at[slot, cols, :], sems.at[slot, 1]
                            ).start()
                            continue
                        for j in range(wo.shape[2] // PAIR):
                            place = pl.ds(j * PAIR, PAIR)
                            pltpu.make_async_copy(
                                qkv_slots[part].at[3, place, :], wo.at[slot, cols, place], sems.at[slot, 1]
                            ).start()

    slot = step % 2

    @pl.when(step == 0)
    def _():
        start(step, slot)

    @pl.when(step + 1 < steps)
    def _():
        start(step + 1, 1 - slot)

    pltpu.make_async_copy(wq.at[slot], wq.at[slot], sems.at[slot, 0]).wait()
    if wo is not None:
        pltpu.make_async_copy(wo.at[slot], wo.at[slot], sems.at[slot, 1]).wait()
    return slot


def rest_kernel(groups, normed_ref, q0, q1, q2, q3, heads_ref, proj_ref, logs_ref, wq, sems):
    slot = stream_weights(None, None, (q0, q1, q2, q3), None, wq, None, sems, pl.program_id(0), 2, 2)
    project_block(normed_ref, lambda i: wq[slot, i], proj_ref.at[0])
    attend_block(groups, proj_ref.at[0], heads_ref.at[0], logs_ref.at[0])


def space_rest(normed, qkv_slots, groups):
    rows, depth = normed.shape
    return pl.pallas_call(
        partial(rest_kernel, groups),
        grid=(2,),
        in_specs=[whole(rows, depth)] + [any_spec()] * 4,
        out_specs=[
            pl.BlockSpec((1, rows, BLOCK), lambda s: (s, 0, 0)),
            pl.BlockSpec((1, 3, rows, BLOCK), lambda s: (s, 0, 0, 0)),
            pl.BlockSpec((1, 8, rows), lambda s: (s, 0, 0)),
        ],
        out_shape=[
            shape_of(2, rows, BLOCK),
            shape_of(2, 3, rows, BLOCK),
            shape_of(2, 8, rows, dtype=F32),
        ],
        scratch_shapes=[pltpu.VMEM((2, 3, depth, BLOCK), BF), pltpu.SemaphoreType.DMA((2, 2))],
        compiler_params=params(),
        cost_estimate=cost(12),
        name="space_rest",
    )(normed, *qkv_slots)


def out_kernel(bits_ref, stream_ref, own_ref, other_ref, w_ref, o0, o1, o2, o3, mid_ref, assembled):
    clip_bit, core_bit = bits_ref[0], bits_ref[1]
    for i, piece in enumerate((o0, o1, o2, o3)):
        place = 2 * (clip_bit if i < 2 else 1 - clip_bit) + (core_bit if i % 2 == 0 else 1 - core_bit)
        assembled[pl.ds(pl.multiple_of(place * PAIR, PAIR), PAIR), :] = piece[...]
    total = stream_ref[...]
    for b in range(own_ref.shape[0]):
        cols = slice(b * BLOCK, (b + 1) * BLOCK)
        total = total + dot_n(own_ref[b], w_ref[cols, :]) + dot_n(other_ref[b], assembled[cols, :])
    mid_ref[...] = total.astype(BF)


def space_mix(bits, started, own, other, weight, out_slots):
    rows, depth = started.shape
    half = weight.shape[0]
    return pl.pallas_call(
        out_kernel,
        grid_spec=pltpu.PrefetchScalarGridSpec(
            num_scalar_prefetch=1,
            grid=(1,),
            in_specs=[whole(rows, depth), whole(*own.shape), whole(*other.shape), whole(half, depth)]
            + [whole(half // 4, depth)] * 4,
            out_specs=whole(rows, depth),
            scratch_shapes=[pltpu.VMEM((half, depth), BF)],
        ),
        out_shape=shape_of(rows, depth),
        compiler_params=params(),
        cost_estimate=cost(6),
        name="space_mix",
    )(bits, started, own, other, weight, *out_slots)


def time_kernel(groups, mid_ref, gain_ref, wq_any, wo_any, q0, q1, q2, q3,
                late_ref, normed_ref, heads_ref, proj_ref, logs_ref, acc, wq, wo, sems):
    step = pl.program_id(0)
    rows = mid_ref.shape[0]

    @pl.when(step == 0)
    def _():
        gain = gain_ref[...]
        for chunk in row_chunks(rows):
            values = mid_ref[chunk, :].astype(F32)
            acc[chunk, :] = values
            normed_ref[chunk, :] = (norm_parts(values)[0] * gain).astype(BF)

    slot = stream_weights(wq_any, wo_any, (q0, q1, q2, q3), None, wq, wo, sems, step, 4)
    project_block(normed_ref, lambda i: wq[slot, i], proj_ref.at[0])
    attend_block(groups, proj_ref.at[0], heads_ref.at[0], logs_ref.at[0])
    acc[...] += dot_n(heads_ref[0], wo[slot])

    @pl.when(step == 3)
    def _():
        late_ref[...] = acc[...].astype(BF)


def time_forward(middle, gain, qkv, out, slots, groups):
    rows, depth = middle.shape
    return pl.pallas_call(
        partial(time_kernel, groups),
        grid=(4,),
        in_specs=[whole(rows, depth), whole(1, depth)] + [any_spec()] * 6,
        out_specs=[
            whole(rows, depth),
            whole(rows, depth),
            pl.BlockSpec((1, rows, BLOCK), lambda s: (s, 0, 0)),
            pl.BlockSpec((1, 3, rows, BLOCK), lambda s: (s, 0, 0, 0)),
            pl.BlockSpec((1, 8, rows), lambda s: (s, 0, 0)),
        ],
        out_shape=[
            shape_of(rows, depth),
            shape_of(rows, depth),
            shape_of(4, rows, BLOCK),
            shape_of(4, 3, rows, BLOCK),
            shape_of(4, 8, rows, dtype=F32),
        ],
        scratch_shapes=[
            pltpu.VMEM((rows, depth), F32),
            pltpu.VMEM((2, 3, depth, BLOCK), BF),
            pltpu.VMEM((2, BLOCK, depth), BF),
            pltpu.SemaphoreType.DMA((2, 2)),
        ],
        compiler_params=params(),
        cost_estimate=cost(29),
        name="time_forward",
    )(middle, gain, qkv, out, *slots)


def gelu_parts(hidden):
    root = 0.7978845608028654
    square = hidden * hidden
    curve = jnp.tanh(hidden * (root + (root * 0.044715) * square))
    half = 0.5 + 0.5 * curve
    slope = half + hidden * (half * (1.0 - curve)) * (root + (3 * 0.044715 * root) * square)
    return hidden * half, slope


def norm_back_rows(values, gain, d_normed):
    normal, inverse = norm_parts(values)
    scaled = d_normed * gain
    mean_first = jnp.mean(scaled, -1, keepdims=True)
    mean_second = jnp.mean(scaled * normal, -1, keepdims=True)
    return (scaled - mean_first - normal * mean_second) * inverse, d_normed * normal


def ffn_kernel(late_ref, cot_ref, gain_ref, up_any, down_any, u0, u1, u2, u3, d0, d1, d2, d3,
               out_ref, d_late_ref, normed_ref, gelu_ref, d_hidden_ref, d_gain_ref, total, d_normed, wu, wd, sems):
    step = pl.program_id(0)
    rows, depth = late_ref.shape
    width = wu.shape[2]
    steps = 8

    @pl.when(step == 0)
    def _():
        gain = gain_ref[...]
        for chunk in row_chunks(rows):
            values = late_ref[chunk, :].astype(F32)
            total[chunk, :] = values
            d_normed[chunk, :] = jnp.zeros_like(values)
            normed_ref[chunk, :] = (norm_parts(values)[0] * gain).astype(BF)

    def start(index, slot):
        for s in range(steps):

            @pl.when(index == s)
            def _(s=s):
                cols = pl.ds(s * width, width)
                up = up_any.at[:, cols] if s < 4 else (u0, u1, u2, u3)[s - 4]
                down = down_any.at[cols, :] if s < 4 else (d0, d1, d2, d3)[s - 4]
                pltpu.make_async_copy(up, wu.at[slot], sems.at[slot, 0]).start()
                pltpu.make_async_copy(down, wd.at[slot], sems.at[slot, 1]).start()

    slot = step % 2

    @pl.when(step == 0)
    def _():
        start(step, slot)

    @pl.when(step + 1 < steps)
    def _():
        start(step + 1, 1 - slot)

    pltpu.make_async_copy(wu.at[slot], wu.at[slot], sems.at[slot, 0]).wait()
    pltpu.make_async_copy(wd.at[slot], wd.at[slot], sems.at[slot, 1]).wait()
    for chunk in row_chunks(rows, rows // 2):
        gelu, slope = gelu_parts(dot_n(normed_ref[chunk, :], wu[slot]))
        gelu = gelu.astype(BF)
        gelu_ref[0, 0, chunk, :] = gelu
        d_hidden = (dot_t(cot_ref[chunk, :], wd[slot]) * slope).astype(BF)
        d_hidden_ref[0, 0, chunk, :] = d_hidden
        total[chunk, :] += dot_n(gelu, wd[slot])
        d_normed[chunk, :] += dot_t(d_hidden, wu[slot])

    @pl.when(step == steps - 1)
    def _():
        gain = gain_ref[...]
        d_gain = jnp.zeros_like(gain)
        for chunk in row_chunks(rows):
            out_ref[chunk, :] = total[chunk, :].astype(BF)
            back, d_gain_rows = norm_back_rows(late_ref[chunk, :].astype(F32), gain, d_normed[chunk, :])
            d_late_ref[chunk, :] = (cot_ref[chunk, :].astype(F32) + back).astype(BF)
            d_gain = d_gain + jnp.sum(d_gain_rows, 0, keepdims=True)
        d_gain_ref[...] = d_gain


def feed_forward(latest, cot, gain, up, down, up_slots, down_slots):
    rows, depth = latest.shape
    width = up.shape[1] // 4
    stream = pl.BlockSpec((1, 1, rows, width), lambda s: (s, 0, 0, 0))
    return pl.pallas_call(
        ffn_kernel,
        grid=(8,),
        in_specs=[whole(rows, depth), whole(rows, depth), whole(1, depth)] + [any_spec()] * 10,
        out_specs=[whole(rows, depth), whole(rows, depth), whole(rows, depth), stream, stream, whole(1, depth)],
        out_shape=[
            shape_of(rows, depth),
            shape_of(rows, depth),
            shape_of(rows, depth),
            shape_of(8, 1, rows, width),
            shape_of(8, 1, rows, width),
            shape_of(1, depth, dtype=F32),
        ],
        scratch_shapes=[
            pltpu.VMEM((rows, depth), F32),
            pltpu.VMEM((rows, depth), F32),
            pltpu.VMEM((2, depth, width), BF),
            pltpu.VMEM((2, width, depth), BF),
            pltpu.SemaphoreType.DMA((2, 2)),
        ],
        compiler_params=params(),
        cost_estimate=cost(34),
        name="feed_forward",
    )(latest, cot, gain, up, down, *up_slots, *down_slots)


def back_kernel(groups, segments, sums, final, packed, offset, dy_ref, proj_any, logs_any, *refs):
    if final:
        stream_ref, gain_ref, partial_ref, q0, q1, q2, q3 = refs[:7]
        refs = refs[7:]
        out_slots = None
        if not packed:
            out_slots, refs = refs[:4], refs[4:]
        own, slots = (None, None), ((q0, q1, q2, q3), out_slots)
        d_stream_ref, d_proj_ref, d_gain_ref, sums_ref, d_normed = refs[:5]
        first = 2
    else:
        own, slots = refs[:2], (None, None)
        d_normed, d_proj_ref = refs[2:4]
        first = 0
    d_heads, proj, logs, wq, wo, sems, more = refs[-7:]
    step = pl.program_id(0)

    def start(index, slot):
        pltpu.make_async_copy(proj_any.at[index + offset], proj.at[slot], more.at[slot, 0]).start()
        pltpu.make_async_copy(logs_any.at[index + offset], logs.at[slot], more.at[slot, 1]).start()

    slot = step % 2

    @pl.when(step == 0)
    def _():
        start(step, slot)
        start(step + 1, 1 - slot)

    slot = stream_weights(*own, *slots, wq, wo, sems, step, 2, first)
    d_heads[...] = dot_t(dy_ref[...], wo[slot]).astype(BF)
    pltpu.make_async_copy(proj.at[slot], proj.at[slot], more.at[slot, 0]).wait()
    pltpu.make_async_copy(logs.at[slot], logs.at[slot], more.at[slot, 1]).wait()
    attend_back_block(groups, proj.at[slot], d_heads, logs.at[slot], d_proj_ref.at[0])
    term = (
        dot_t(d_proj_ref[0, 0], wq[slot, 0])
        + dot_t(d_proj_ref[0, 1], wq[slot, 1])
        + dot_t(d_proj_ref[0, 2], wq[slot, 2])
    )

    @pl.when(step == 0)
    def _():
        d_normed[...] = term + partial_ref[...] if final else term

    @pl.when(step > 0)
    def _():
        d_normed[...] += term

    if not final:
        return

    @pl.when(step == 1)
    def _():
        gain = gain_ref[...]
        d_gain = jnp.zeros_like(gain)
        for index, (begin, count) in enumerate(segments):
            summed = jnp.zeros_like(gain)
            for piece in row_chunks(count):
                chunk = slice(begin + piece.start, begin + piece.stop)
                back, d_gain_rows = norm_back_rows(stream_ref[chunk, :].astype(F32), gain, d_normed[chunk, :])
                d_values = dy_ref[chunk, :].astype(F32) + back
                d_stream_ref[chunk, :] = d_values.astype(BF)
                d_gain = d_gain + jnp.sum(d_gain_rows, 0, keepdims=True)
                if sums:
                    summed = summed + jnp.sum(d_values, 0, keepdims=True)
            if sums:
                sums_ref[index : index + 1, :] = summed
        d_gain_ref[...] = d_gain
        if not sums:
            sums_ref[...] = jnp.zeros_like(sums_ref)


def branch_back(name, dy, proj, logs, offset, weights, groups, tail=None, segments=(), sums=False):
    rows, depth = dy.shape
    final = tail is not None
    if final:
        slots = [piece for group in weights for piece in group]
        others = [*tail, *slots]
        specs = [whole(rows, depth), whole(1, depth), whole(rows, depth)] + [any_spec()] * len(slots)
        outs = [
            (whole(rows, depth), shape_of(rows, depth)),
            (pl.BlockSpec((1, 3, rows, BLOCK), lambda s: (s, 0, 0, 0)), shape_of(2, 3, rows, BLOCK)),
            (whole(1, depth), shape_of(1, depth, dtype=F32)),
            (whole(8, depth), shape_of(8, depth, dtype=F32)),
        ]
        scratch = [pltpu.VMEM((rows, depth), F32)]
    else:
        others = list(weights)
        specs = [any_spec()] * 2
        outs = [
            (whole(rows, depth), shape_of(rows, depth, dtype=F32)),
            (pl.BlockSpec((1, 3, rows, BLOCK), lambda s: (s, 0, 0, 0)), shape_of(2, 3, rows, BLOCK)),
        ]
        scratch = []
    return pl.pallas_call(
        partial(back_kernel, groups, segments, sums, final, len(weights) == 1, offset),
        grid=(2,),
        in_specs=[whole(rows, depth), any_spec(), any_spec()] + specs,
        out_specs=[o[0] for o in outs],
        out_shape=[o[1] for o in outs],
        scratch_shapes=scratch
        + [
            pltpu.VMEM((rows, BLOCK), BF),
            pltpu.VMEM((2, 3, rows, BLOCK), BF),
            pltpu.VMEM((2, 8, rows), F32),
            pltpu.VMEM((2, 3, depth, BLOCK), BF),
            pltpu.VMEM((2, BLOCK, depth), BF),
            pltpu.SemaphoreType.DMA((2, 2)),
            pltpu.SemaphoreType.DMA((2, 2)),
        ],
        compiler_params=params(),
        cost_estimate=cost(21 if final else 18),
        name=name,
    )(dy, proj, logs, *others)


def grad_kernel(chunk, y_first, lefts, bits_ref, *refs):
    count = len(lefts)
    n_left = max(lefts) + 1
    left_refs, own_refs, other_refs = refs[:n_left], refs[n_left : n_left + count], refs[n_left + count : n_left + 2 * count]
    send_ref, keep_ref, turned = refs[n_left + 2 * count :]
    step = pl.program_id(0)
    core_bit, z_index = bits_ref[1], bits_ref[2]
    stacks = send_ref.shape[2]
    cut = send_ref.shape[3]

    @pl.when(step == 0)
    def _():
        for n, left_ref in enumerate(left_refs):
            for j in range(stacks):
                start = pl.multiple_of((z_index ^ j) * 2 * cut, 2 * cut)
                both = left_ref[:, pl.ds(start, 2 * cut)].T
                rows = slice(j * cut, (j + 1) * cut)
                for core in range(2):

                    @pl.when(core_bit == core)
                    def _(core=core, both=both, rows=rows, n=n):
                        turned[n, 1, rows, :] = both[core * cut : (core + 1) * cut]
                        turned[n, 0, rows, :] = both[(1 - core) * cut : (2 - core) * cut]

    def fill(side, half, out_ref):
        matrix = 0
        for n, own_ref, other_ref in zip(lefts, own_refs, other_refs):
            source = own_ref if half == 0 else other_ref
            span = source.shape[3]
            for t in range(source.shape[1]):
                for b in range(source.shape[0]):
                    block = dot_n(turned[n, side], source[b, t]).astype(BF)
                    for i in range(span // chunk):
                        index = b * (span // chunk) + i
                        if half == 1:
                            index = index ^ core_bit
                        lanes = pl.ds(pl.multiple_of((2 * matrix + index) * chunk, chunk), chunk)
                        for j in range(stacks):
                            out_ref[0, 0, j, :, lanes] = block[
                                j * cut : (j + 1) * cut, i * chunk : (i + 1) * chunk
                            ]
                matrix += 1

    for g in range(8):

        @pl.when(step == g)
        def _(g=g):
            first, second = g // 2 % 2, g % 2
            fill(g // 4, second if y_first else first, send_ref if g < 4 else keep_ref)


def grad_product(bits, left_arrays, terms, chunk, y_first, sizes, micros):
    rows, depth = left_arrays[0].shape
    stacks = sizes["wide"] // 2
    cut = depth // sizes["wide"]
    columns = 2 * sum(term[4] for term in terms) * chunk

    def y_flip(g):
        return g % 4 // 2 if y_first else g % 2

    def own_index(g, b):
        flip = y_flip(g)
        if not y_first:
            flip = jnp.where(g % 4 // 2 == 0, flip, 1)
        return b[0] ^ flip

    def other_index(g, b):
        flip = y_flip(g)
        if not y_first:
            flip = jnp.where(g % 4 // 2 == 1, flip, 0)
        return flip

    def half_spec(value, index, first_part, parts):
        array, at = value
        lead = 2 * chunk // array.shape[3]
        return pl.BlockSpec(
            (lead, parts, *array.shape[2:]),
            lambda g, b: (2 * at + index(g, b), first_part // parts, 0, 0),
        )

    block = (1, 1, stacks, cut, columns)
    return pl.pallas_call(
        partial(grad_kernel, chunk, y_first, [term[0] for term in terms]),
        grid_spec=pltpu.PrefetchScalarGridSpec(
            num_scalar_prefetch=1,
            grid=(8,),
            in_specs=[whole(rows, depth)] * len(left_arrays)
            + [half_spec(term[1], own_index, *term[3:]) for term in terms]
            + [half_spec(term[2], other_index, *term[3:]) for term in terms],
            out_specs=[
                pl.BlockSpec(block, lambda g, b: (jnp.minimum(g, 3) // 2, jnp.minimum(g, 3) % 2, 0, 0, 0)),
                pl.BlockSpec(
                    block, lambda g, b: (jnp.maximum(g - 4, 0) // 2, jnp.maximum(g - 4, 0) % 2, 0, 0, 0)
                ),
            ],
            scratch_shapes=[pltpu.VMEM((len(left_arrays), 2, stacks * cut, rows), BF)],
        ),
        out_shape=[shape_of(2, 2, stacks, cut, columns)] * 2,
        compiler_params=params(),
        cost_estimate=cost(micros),
        name="grad_product",
    )(bits, *left_arrays, *[term[1][0] for term in terms], *[term[2][0] for term in terms])


def swap(value, axis, sizes, step=1):
    return lax.ppermute(value, axis, [(i, i ^ step) for i in range(sizes[axis])])


def after(value, *others):
    return lax.optimization_barrier((value, *others))[0]


def wide(value):
    return value.astype(F32)


class Moves:
    def __init__(self, sizes):
        self.sizes = sizes
        self.tp = lax.axis_index("tp")
        self.clip = lax.axis_index("clip")
        self.clip_bit = self.clip % 2
        place = lax.axis_index("wide")
        self.core_bit = place % 2
        self.z = place // 2
        self.bits = jnp.stack([self.clip_bit, self.core_bit, self.z]).astype(jnp.int32)

    def quarter(self, weight, axis):
        size = weight.shape[axis] // 4
        return lax.dynamic_slice_in_dim(weight, (2 * self.clip_bit + self.core_bit) * size, size, axis)

    def spread(self, from_x):
        from_y = swap(from_x, "clip", self.sizes)
        return (from_x, swap(from_x, "wide", self.sizes), from_y, swap(from_y, "wide", self.sizes))

    def spread_core(self, from_x, from_y):
        return (from_x, swap(from_x, "wide", self.sizes), from_y, swap(from_y, "wide", self.sizes))

    def reduction(self, product, y_first):
        return Reduction(self, *product, y_first)

    def take(self, value, index, axis):
        return lax.dynamic_index_in_dim(value, index, axis, keepdims=False)

    def small_first(self, rows):
        count, depth = rows.shape
        wide_size = self.sizes["wide"]
        blocks = rows.reshape(count, wide_size // 2, 2, depth // wide_size).transpose(1, 2, 0, 3)
        other = swap(self.take(blocks, 1 - self.core_bit, 1), "wide", self.sizes)
        return self.take(blocks, self.core_bit, 1), other

    def small_last(self, total):
        result = self.take(total, self.z, 0)
        for j in range(1, self.sizes["wide"] // 2):
            result = result + swap(self.take(total, self.z ^ j, 0), "wide", self.sizes, 2 * j)
        return result


class Reduction:
    def __init__(self, moves, send, keep, y_first):
        self.moves, self.sizes, self.keep = moves, moves.sizes, keep
        self.axes = ("clip", "tp") if y_first else ("tp", "clip")
        self.got = swap(send, "wide", self.sizes)

    def second(self, *deps):
        self.leaving = (wide(self.keep[1]) + wide(self.got[1])).astype(BF)
        if deps:
            self.leaving = after(self.leaving, *deps)
        self.arrived = swap(self.leaving, self.axes[0], self.sizes)
        return self.leaving

    def third(self, *deps):
        total = wide(self.keep[0]) + wide(self.got[0]) + wide(self.arrived)
        self.leaving = total[1].astype(BF)
        if deps:
            self.leaving = after(self.leaving, *deps)
        self.mine = total[0].astype(BF)
        self.arrived = swap(self.leaving, self.axes[1], self.sizes)
        return self.leaving

    def sum(self, *deps):
        if deps:
            self.mine = after(self.mine, *deps)
        total = wide(self.mine) + wide(self.arrived)
        step = 2
        while step < self.sizes["clip"]:
            total = total + wide(swap(total.astype(BF), "clip", self.sizes, step))
            step *= 2
        self.total = total.astype(BF)
        return self.total


class Pair:
    def __init__(self, moves, one, two):
        self.moves, self.sizes, self.one, self.two = moves, moves.sizes, one, two

    def fourth(self, *deps):
        one, two = self.one.total, self.two.total
        if deps:
            one = after(one, *deps)
        low = jnp.stack([one, two], 1)
        self.mine = low[0]
        self.pieces = [swap(low[j], "wide", self.sizes, 2 * j) for j in range(1, low.shape[0])]
        return low

    def fifth(self, *deps):
        result = wide(after(self.mine, *deps) if deps else self.mine)
        for piece in self.pieces:
            result = result + wide(piece)
        self.mine = result.astype(BF)
        self.arrived = swap(self.mine, "clip", self.sizes)
        return self.mine

    def halves(self, which, matrix, count):
        first = self.moves.clip_bit == 0
        columns = self.mine.shape[2] // count
        part = slice(matrix * columns, (matrix + 1) * columns)
        mine, arrived = self.mine[which, :, part], self.arrived[which, :, part]
        return jnp.concatenate(
            [wide(jnp.where(first, mine, arrived)), wide(jnp.where(first, arrived, mine))], -1
        )


def frame_groups(frames, grid_a, grid_b):
    groups = [(i * grid_a, grid_a, None) for i in range(frames)]
    base = frames * grid_a
    if frames % 2 == 0:
        groups += [(base + i * grid_b, 2 * grid_b, ("block", grid_b, 1)) for i in range(0, frames, 2)]
    else:
        groups += [(base + i * grid_b, grid_b, None) for i in range(frames)]
    return tuple(groups)


def per_device(
    sizes,
    frames_a,
    frames_b,
    actions_a,
    actions_b,
    action_table,
    gain_space,
    space_qkv,
    space_out,
    gain_time,
    time_qkv,
    time_out,
    gain_ffn,
    ffn_up,
    ffn_down,
    cot_a,
    cot_b,
):
    moves = Moves(sizes)
    n_wide = sizes["wide"]
    _, n_frames, grid_a, depth = frames_a.shape
    grid_b = frames_b.shape[2]
    rows_a, rows_b = n_frames * grid_a, n_frames * grid_b
    rows = rows_a + rows_b
    spots_a, spots_b = grid_a // n_wide, grid_b // n_wide
    spots = spots_a + spots_b
    all_frames = n_frames * n_wide
    inner = 8 if spots % 8 == 0 else 4
    gain_space, gain_time, gain_ffn = (g[None] for g in (gain_space, gain_time, gain_ffn))

    def exchange(packed):
        return lax.all_to_all(packed, "wide", split_axis=0, concat_axis=0, tiled=True)

    def pack_grid(first, second):
        first = first.reshape(n_frames, n_wide, spots_a, depth)
        second = second.reshape(n_frames, n_wide, spots_b, depth)
        return jnp.concatenate([first, second], 2).transpose(1, 0, 2, 3)

    def unpack_grid(moved):
        moved = moved.reshape(all_frames, spots // inner, inner, depth)
        return moved.transpose(1, 0, 2, 3).reshape(rows, depth)

    def pack_frames(rows_in):
        packed = rows_in.reshape(spots // inner, n_wide, n_frames, inner, depth)
        return packed.transpose(1, 2, 0, 3, 4).reshape(n_wide, n_frames, spots, depth)

    def unpack_frames(moved):
        first = moved[:, :, :spots_a].transpose(1, 0, 2, 3).reshape(rows_a, depth)
        second = moved[:, :, spots_a:].transpose(1, 0, 2, 3).reshape(rows_b, depth)
        return jnp.concatenate([first, second])

    def both_clips(mine, partner):
        low = moves.tp == 0
        pair = jnp.stack([jnp.where(low, mine, partner), jnp.where(low, partner, mine)])
        return (
            pair[:, :rows_a].reshape(2, n_frames, grid_a, depth),
            pair[:, rows_a:].reshape(2, n_frames, grid_b, depth),
        )

    def pick(value):
        return lax.dynamic_index_in_dim(value, moves.tp, 0, keepdims=False)

    space_groups = frame_groups(n_frames, grid_a, grid_b)
    group = inner * all_frames
    time_groups = tuple((i, group, ("causal", all_frames, inner)) for i in range(0, rows, group))
    codes = jnp.arange(action_table.shape[0])
    acts = jnp.concatenate([actions_a, actions_b], 1)
    one_hot = (acts[:, :, None] == codes).astype(F32)
    shifts = jnp.einsum("cfa,ad->cfd", one_hot, action_table.astype(F32), precision=lax.Precision.HIGHEST)

    clip = moves.tp[None].astype(jnp.int32)
    n_codes = action_table.shape[0]

    def from_x(weight, axis, *deps):
        piece = moves.quarter(weight, axis)
        return swap(after(piece, *deps) if deps else piece, "tp", sizes)

    def from_y(value, *deps):
        return swap(after(value, *deps) if deps else value, "clip", sizes)

    def cores(value, *deps):
        return swap(after(value, *deps) if deps else value, "wide", sizes)

    so_x = from_x(space_out, 0)
    cot_moved = exchange(pack_grid(pick(cot_a), pick(cot_b)))
    (partner_heads,) = space_heads(
        1 - clip, frames_a, frames_b, shifts, gain_space, space_qkv, space_groups, False
    )
    heads_other = swap(partner_heads, "tp", sizes)
    so_y = from_y(so_x, partner_heads)
    heads_own, proj_own, logs_own, started, normed_space = space_heads(
        clip, frames_a, frames_b, shifts, gain_space, space_qkv, space_groups, True
    )
    so_slots = (so_x, cores(so_x, heads_own), so_y, cores(so_y, heads_own))
    middle = space_mix(moves.bits, started, heads_own, heads_other, space_out, so_slots)
    packed = pack_grid(middle[:rows_a], middle[rows_a:])
    middle = exchange(packed)

    out_piece = moves.quarter(time_out, 0)
    out_piece = out_piece.reshape(PAIR, -1, PAIR).transpose(1, 0, 2).reshape(1, -1, PAIR)
    time_piece = jnp.concatenate([moves.quarter(time_qkv, 2), out_piece])
    time_x = swap(after(time_piece, heads_own), "tp", sizes)
    up_x = from_x(ffn_up, 1, heads_own)
    time_y = from_y(time_x)
    time_slots = (time_x, cores(time_x), time_y, cores(time_y))
    down_x = from_x(ffn_down, 0, time_x)
    up_y = from_y(up_x, time_x)
    down_y = from_y(down_x)
    sq_x = from_x(space_qkv, 2, down_x)
    latest, normed_time, heads_time, proj_time, logs_time = time_forward(
        unpack_grid(middle), gain_time, time_qkv, time_out, time_slots, time_groups
    )
    middle = unpack_grid(middle)
    up_slots = (up_x, cores(up_x, latest), up_y, cores(up_y, latest))
    down_slots = (down_x, cores(down_x, latest), down_y, cores(down_y, latest))
    cot = unpack_grid(cot_moved)
    out, d_latest, normed_ffn, gelu, d_hidden, d_gain_ffn = feed_forward(
        latest, cot, gain_ffn, ffn_up, ffn_down, up_slots, down_slots
    )
    out_packed = pack_frames(out)
    out_moved = exchange(out_packed)
    sq_y = from_y(sq_x, out_packed)

    def product(left_arrays, terms, chunk, y_first, micros):
        return moves.reduction(
            grad_product(moves.bits, left_arrays, terms, chunk, y_first, sizes, micros), y_first
        )

    chunk = ffn_up.shape[1] // 4
    up = product([after(normed_ffn, out_packed)], [(0, (d_hidden, 0), (d_hidden, 1), 0, 1)], chunk, False, 15)
    down = product([after(cot, up.keep)], [(0, (gelu, 0), (gelu, 1), 0, 1)], chunk, True, 15)
    gate = up.second(down.keep)
    partial_time, d_proj_own = branch_back(
        "time_back", after(d_latest, gate), proj_time, logs_time, 0, (time_qkv, time_out), time_groups
    )
    sq_slots = (sq_x, cores(sq_x, partial_time), sq_y, cores(sq_y, partial_time))
    gate = down.second(partial_time)
    d_middle, d_proj_rest, d_gain_time, _ = branch_back(
        "time_back_end", d_latest, proj_time, logs_time, 2, (time_slots,), time_groups,
        (middle, gain_time, after(partial_time, gate, out_moved)), ((0, rows),),
    )
    packed = pack_frames(d_middle)
    d_middle = exchange(packed)
    gate = up.third(packed)
    heads_time = heads_time[:, None]
    own, rest = (d_proj_own, 0), (d_proj_rest, 0)
    time_one = product([after(normed_time, gate)], [(0, own, rest, 0, 2)], PAIR, False, 10)
    out_rows = unpack_frames(after(out_moved, time_one.keep))
    out_partner = swap(out_rows, "tp", sizes)
    time_two = product(
        [normed_time, after(d_latest, time_one.keep)],
        [(0, own, rest, 2, 1), (1, (heads_time, 0), (heads_time, 1), 0, 1)],
        PAIR, True, 10,
    )
    gate = time_one.second(time_two.keep)
    heads_rest, proj_rest, logs_rest = space_rest(after(normed_space, gate), sq_slots, space_groups)
    gate = down.third(heads_rest)
    gate2 = time_two.second(heads_rest)
    d_middle = unpack_frames(d_middle)
    d_middle = after(d_middle, gate, gate2)
    partial_space, d_proj_own = branch_back(
        "space_back", d_middle, proj_own, logs_own, 0, (space_qkv, space_out), space_groups
    )
    out_a, out_b = both_clips(out_rows, after(out_partner, partial_space))
    gate = time_one.third(partial_space)
    gate2 = time_two.third(gate)
    segments = tuple((i * grid_a, grid_a) for i in range(n_frames)) + tuple(
        (rows_a + i * grid_b, grid_b) for i in range(n_frames)
    )
    d_started, d_proj_rest, d_gain_space, frame_sums = branch_back(
        "space_back_end", d_middle, proj_rest, logs_rest, 0, (sq_slots, so_slots), space_groups,
        (started, gain_space, after(partial_space, gate, gate2, out_a, out_b)), segments, True,
    )
    own, rest = (d_proj_own, 0), (d_proj_rest, 0)
    gates = [r.sum(d_started) for r in (up, down, time_one, time_two)]
    ffn, time = Pair(moves, up, down), Pair(moves, time_one, time_two)
    gates = [ffn.fourth(*gates)]
    gates += [time.fourth(*gates)]
    d_table = jnp.einsum(
        "fa,fd->ad", pick(one_hot), frame_sums[: 2 * n_frames], precision=lax.Precision.HIGHEST
    )
    small, small_other = moves.small_first(jnp.concatenate([d_table, d_gain_space, d_gain_time, d_gain_ffn]))
    started_partner = swap(d_started, "tp", sizes)
    space_two = product(
        [after(normed_space, *gates, small), d_middle],
        [(0, own, rest, 2, 1), (1, (heads_own[:, None], 0), (heads_rest[:, None], 0), 0, 1)],
        PAIR, True, 10,
    )
    small = small + after(small_other, space_two.keep)
    small_other = swap(small, "tp", sizes)
    space_one = product([after(normed_space, space_two.keep, small)], [(0, own, rest, 0, 2)], PAIR, False, 10)
    gate = space_two.second(space_one.keep)
    small = small + after(small_other, gate)
    d_frames_a, d_frames_b = both_clips(d_started, after(started_partner, gate))
    gate = space_one.second(d_frames_a, d_frames_b)
    step = 1
    while step < sizes["clip"]:
        small = small + swap(small, "clip", sizes, step)
        step *= 2
    gate = ffn.fifth(gate)
    gate = time.fifth(gate, small)
    gate = space_two.third(gate)
    gate = space_one.third(gate)
    small = moves.small_last(after(small, gate))
    space_two.sum(small), space_one.sum()
    space = Pair(moves, space_one, space_two)
    space.fourth()
    space.fifth()

    def qkv(pair):
        return jnp.stack([pair.halves(0, 0, 2), pair.halves(0, 1, 2), pair.halves(1, 0, 2)])

    return (
        out_a,
        out_b,
        d_frames_a,
        d_frames_b,
        small[:n_codes],
        small[n_codes],
        qkv(space),
        space.halves(1, 1, 2).T,
        small[n_codes + 1],
        qkv(time),
        time.halves(1, 1, 2).T,
        small[n_codes + 2],
        ffn.halves(0, 0, 1),
        ffn.halves(1, 0, 1).T,
    )


def solution(mesh):
    sizes = dict(mesh.shape)
    return jax.shard_map(
        partial(per_device, sizes),
        mesh=mesh,
        in_specs=(
            P("clip", "wide", None, None),
            P("clip", "wide", None, None),
            P("clip", "wide"),
            P("clip", "wide"),
            P(),
            P(),
            P(None, None, "tp"),
            P("tp", None),
            P(),
            P(None, None, "tp"),
            P("tp", None),
            P(),
            P(None, "tp"),
            P("tp", None),
            P("clip", "wide", None, None),
            P("clip", "wide", None, None),
        ),
        out_specs=(
            P("clip", "wide", None, None),
            P("clip", "wide", None, None),
            P("clip", "wide", None, None),
            P("clip", "wide", None, None),
            P(None, "wide"),
            P("wide"),
            P(None, "wide", "tp"),
            P("tp", "wide"),
            P("wide"),
            P(None, "wide", "tp"),
            P("tp", "wide"),
            P("wide"),
            P("wide", "tp"),
            P("tp", "wide"),
        ),
        check_vma=False,
    )
```

time: 1360 us -> 622 us (0.46)
  waiting for transfers between devices: 779 us -> 160 us
  Pallas kernels: 0 us -> 263 us
  matrix products: 198 us -> 2.58 us
  local copies, waits for them, and re-layouts: 190 us -> 35.4 us
  other arithmetic: 103 us -> 60.3 us
  starting transfers between devices: 47.6 us -> 89.7 us
  blocking collectives: 18.9 us -> 0 us
  between operations: 16.8 us -> 1.97 us
    psum x6 -> x0, waiting for transfers between devices: 400 us -> none  [the longest x2 150 us: settle(): lax.psum(partials[1].astype(jnp.bfloat16), 'tp').astype(jnp.float32)]
    pallas_call x0 -> x16, Pallas kernels: none -> 263 us  [the longest x6 80 us: grad_product(): pl.pallas_call(partial(grad_kernel, chunk, y_first, [term[0] for term in...]
    dot_general x58 -> x2, matrix products: 198 us -> 2.58 us  [the longest x1 1.53 us: per_device(): jnp.einsum('cfa,ad->cfd', one_hot, action_table.astype(F32), precision=la...]
    unnamed x19 -> x0, waiting for transfers between devices: 186 us -> none
    ppermute x0 -> x59, waiting for transfers between devices: none -> 160 us  [swap(): lax.ppermute(value, axis, [(i, i ^ step) for i in range(sizes[axis])])]
    all_to_all x8 -> x4, waiting for transfers between devices: 144 us -> 0.01 us  [exchange(): lax.all_to_all(packed, 'wide', split_axis=0, concat_axis=0, tiled=True)]
    ppermute x0 -> x59, starting transfers between devices: none -> 68.9 us  [swap(): lax.ppermute(value, axis, [(i, i ^ step) for i in range(sizes[axis])])]
    unnamed x312 -> x59, local copies, waits for them, and re-layouts: 66 us -> 4.74 us
  transfers between devices with their start and end apart: 21 -> 63, of which waited for: 21 -> 19; matrix products, arithmetic and copies ran while one was open for 16% -> 15% of each run, Pallas kernels for 0% -> 43%
where the time goes in v2:
time: 622 us; the launch traced here: 612 us
  Pallas kernels  263 us (42%)
  waiting for transfers between devices  160 us (26%)
  starting transfers between devices  89.7 us (14%)
  other arithmetic  60.3 us (10%)
  local copies, waits for them, and re-layouts  35.4 us (6%)
    ppermute x59, waiting for transfers between devices, swap(): lax.ppermute(value, axis, [(i, i ^ step) for i in range(sizes[axis])])  160 us
    pallas_call x6, Pallas kernels, grad_product(): pl.pallas_call(partial(grad_kernel, chunk, y_first, [term[0] for term in...  80 us
    pallas_call x4, Pallas kernels, branch_back(): pl.pallas_call(partial(back_kernel, groups, segments, sums, final, len(we...  77.4 us
    ppermute x59, starting transfers between devices, swap(): lax.ppermute(value, axis, [(i, i ^ step) for i in range(sizes[axis])])  68.9 us
    pallas_call x1, Pallas kernels, feed_forward(): pl.pallas_call(ffn_kernel, grid=(8,), in_specs=[whole(rows, depth), whole...  34.4 us
    pallas_call x1, Pallas kernels, time_forward(): pl.pallas_call(partial(time_kernel, groups), grid=(4,), in_specs=[whole(r...  29 us
    pallas_call x2, Pallas kernels, space_heads(): pl.pallas_call(partial(space_kernel, groups, full), grid_spec=pltpu.Prefe...  23.9 us
    all_to_all x4, starting transfers between devices, exchange(): lax.all_to_all(packed, 'wide', split_axis=0, concat_axis=0, tiled=True)  20.8 us
  transfers between devices with their start and end apart: 63, of which 19 were waited for; matrix products, arithmetic and copies ran while one was open for 15% of the time, Pallas kernels for 43%

profile of v2, /device:TPU:0, one launch (start us, length us, event | category | flops | bytes accessed | tf_op | source)
XLA Modules:
  0.0 612.1 jit_solution(7991223199811190801)
XLA Ops:
  7.7 11.8 %space_partner.1 = bf16[2,640,256]{2,1,0:T(8,128)(2,1)} custom-call(s32[1]{0:T(128)S(6)} %sub.11._, bf16[2,2,256,1024]{3,2,1,0:T(8,128)(2,1)} %fa_ref.3, bf16[2,2,64,1024]{3,2,1,0:T(8,128)(2,1)} %fb_ref.3, f32[2,4,1024]{2,1,0:T(4,128)} %fusion.43.shift_ref, f32[1,1024]{1,0:T(1,128)} %bitcast.305, bf16[3,1024,512]{2,1,0:T(8,128)(2,1)} %refs_0_.3), custom_call_target="tpu_custom_call" | custom-call | flops 48000000000 | bytes 1048576 | tf_op jit(solution)/shard_map/space_partner/pallas_call | solution.py:190
  21.6 12.0 %space_own.1 = (bf16[2,640,256]{2,1,0:T(8,128)(2,1)}, bf16[2,3,640,256]{3,2,1,0:T(8,128)(2,1)}, f32[2,8,640]{2,1,0:T(8,128)}, f32[640,1024]{1,0:T(8,128)}, bf16[640,1024]{1,0:T(8,128)(2,1)}) custom-call(s32[1]{0:T(128)} %bitcast.3._, bf16[2,2,256,1024]{3,2,1,0:T(8,128)(2,1)} %fa_ref.3, bf16[2,2,64,1024]{3,2,1,0:T(8,128)(2,1)} %fb_ref.3, ...), custom_call_target="tpu_custom_call" | custom-call | flops 48000000000 | bytes 1048576 | tf_op jit(solution)/shard_map/space_own/pallas_call | solution.py:190
  53.2 10.0 %collective-permute-done.5.q0.refs_3_ = bf16[4,1024,128]{2,1,0:T(8,128)(2,1)} collective-permute-done((bf16[4,1024,128]{2,1,0:T(8,128)(2,1)}, bf16[4,1024,128]{2,1,0:T(8,128)(2,1)}, u32[]{:S(2)}, u32[]{:S(2)}) %collective-permute-start.5) | collective-permute-done | bytes 1048608 | tf_op jit(solution)/shard_map/ppermute | solution.py:702
  70.1 17.8 %collective-permute-done.7.q2.refs_5_ = bf16[4,1024,128]{2,1,0:T(8,128)(2,1)} collective-permute-done((bf16[4,1024,128]{2,1,0:T(8,128)(2,1)}, bf16[4,1024,128]{2,1,0:T(8,128)(2,1)}, u32[]{:S(2)}, u32[]{:S(2)}) %collective-permute-start.7) | collective-permute-done | bytes 1048608 | tf_op jit(solution)/shard_map/ppermute | solution.py:702
  93.9 18.9 %collective-permute-done.13.d0 = bf16[512,1024]{1,0:T(8,128)(2,1)} collective-permute-done((bf16[512,1024]{1,0:T(8,128)(2,1)}, bf16[512,1024]{1,0:T(8,128)(2,1)}, u32[]{:S(2)}, u32[]{:S(2)}) %collective-permute-start.13) | collective-permute-done | bytes 1048608 | tf_op jit(solution)/shard_map/ppermute | solution.py:702
  120.7 29.0 %time_forward.1 = (bf16[640,1024]{1,0:T(8,128)(2,1)}, bf16[640,1024]{1,0:T(8,128)(2,1)}, bf16[4,640,256]{2,1,0:T(8,128)(2,1)}, bf16[4,3,640,256]{3,2,1,0:T(8,128)(2,1)}, f32[4,8,640]{2,1,0:T(8,128)}) custom-call(bf16[640,1024]{1,0:T(8,128)(2,1)} %bitcast.286, f32[1,1024]{1,0:T(1,128)} %bitcast.303, bf16[3,1024,512]{2,1,0:T(8,128)(2,1)} %refs_0_.2, ...), custom_call_target="tpu_custom_call" | custom-call | flops 115999997952 | bytes 1048576 | tf_op jit(solution)/shard_map/time_forward/pallas_call | solution.py:345
  157.4 34.4 %feed_forward.1 = (bf16[640,1024]{1,0:T(8,128)(2,1)}, bf16[640,1024]{1,0:T(8,128)(2,1)}, bf16[640,1024]{1,0:T(8,128)(2,1)}, bf16[8,1,640,512]{3,2,1,0:T(8,128)(2...) custom-call(bf16[640,1024]{1,0:T(8,128)(2,1)} %get-tuple-element.115.late_ref, bf16[640,1024]{1,0:T(8,128)(2,1)} %bitcast.288, ...), custom_call_target="tpu_custom_call" | custom-call | flops 135999995904 | bytes 1048576 | tf_op jit(solution)/shard_map/feed_forward/pallas_call | solution.py:456
  200.4 15.0 %grad_product.6 = (bf16[2,2,4,128,1024]{4,3,2,1,0:T(8,128)(2,1)}, bf16[2,2,4,128,1024]{4,3,2,1,0:T(8,128)(2,1)}) custom-call(s32[3]{0:T(128)} %pad_add_fusion.1.bits_ref, bf16[640,1024]{1,0:T(8,128)(2,1)} %get-tuple-element.126.refs_0_, bf16[8,1,640,512]{3,2,1,0:T(8,128)(2,1)} %get-tuple-element.127.refs_1_.refs_2_, ...), custom_call_target="tpu_custom_call" | custom-call | flops 60000002048 | bytes 1048576 | tf_op jit(solution)/shard_map/grad_product/pallas_call | solution.py:678
  215.7 16.5 %grad_product.7 = (bf16[2,2,4,128,1024]{4,3,2,1,0:T(8,128)(2,1)}, bf16[2,2,4,128,1024]{4,3,2,1,0:T(8,128)(2,1)}) custom-call(s32[3]{0:T(128)} %pad_add_fusion.1.bits_ref, bf16[640,1024]{1,0:T(8,128)(2,1)} %bitcast.289, bf16[8,1,640,512]{3,2,1,0:T(8,128)(2,1)} %get-tuple-element.131.refs_1_.refs_2_, bf16[8,1,640,512]{3,2,1,0:T(8,128)(2,1)} %get-tuple-element.131.refs_1_.refs_2_), custom_call_target="tpu_custom_call" | custom-call | flops 60000002048 | bytes 1048576 | tf_op jit(solution)/shard_map/grad_product/pallas_call | solution.py:678
  238.6 18.5 %time_back.1 = (f32[640,1024]{1,0:T(8,128)}, bf16[2,3,640,256]{3,2,1,0:T(8,128)(2,1)}) custom-call(bf16[640,1024]{1,0:T(8,128)(2,1)} %get-tuple-element.151.dy_ref.refs_1_, bf16[4,3,640,256]{3,2,1,0:T(8,128)(2,1)} %get-tuple-element.135.proj_any, f32[4,8,640]{2,1,0:T(8,128)} %get-tuple-element.136.logs_any, bf16[3,1024,512]{2,1,0:T(8,128)(2,1)} %refs_0_.2, ...), custom_call_target="tpu_custom_call" | custom-call | flops 71999995904 | bytes 1048576 | tf_op jit(solution)/shard_map/time_back/pallas_call | solution.py:575
  263.2 21.2 %time_back_end.1 = (bf16[640,1024]{1,0:T(8,128)(2,1)}, bf16[2,3,640,256]{3,2,1,0:T(8,128)(2,1)}, f32[1,1024]{1,0:T(1,128)}, f32[8,1024]{1,0:T(8,128)}) custom-call(bf16[640,1024]{1,0:T(8,128)(2,1)} %get-tuple-element.151.dy_ref.refs_1_, bf16[4,3,640,256]{3,2,1,0:T(8,128)(2,1)} %get-tuple-element.135.proj_any, f32[4,8,640]{2,1,0:T(8,128)} %get-tuple-element.136.logs_any, ...), custom_call_target="tpu_custom_call" | custom-call | flops 83999997952 | bytes 1048576 | tf_op jit(solution)/shard_map/time_back_end/pallas_call | solution.py:575
  298.9 11.1 %grad_product.8 = (bf16[2,2,4,128,512]{4,3,2,1,0:T(8,128)(2,1)}, bf16[2,2,4,128,512]{4,3,2,1,0:T(8,128)(2,1)}) custom-call(s32[3]{0:T(128)} %pad_add_fusion.1.bits_ref, bf16[640,1024]{1,0:T(8,128)(2,1)} %get-tuple-element.144.refs_0_, bf16[2,3,640,256]{3,2,1,0:T(8,128)(2,1)} %get-tuple-element.145.refs_1_.refs_2_, ...), custom_call_target="tpu_custom_call" | custom-call | flops 40000000000 | bytes 1048576 | tf_op jit(solution)/shard_map/grad_product/pallas_call | solution.py:678
  310.4 13.1 %grad_product.9 = (bf16[2,2,4,128,512]{4,3,2,1,0:T(8,128)(2,1)}, bf16[2,2,4,128,512]{4,3,2,1,0:T(8,128)(2,1)}) custom-call(s32[3]{0:T(128)} %pad_add_fusion.1.bits_ref, bf16[640,1024]{1,0:T(8,128)(2,1)} %get-tuple-element.144.refs_0_, bf16[640,1024]{1,0:T(8,128)(2,1)} %get-tuple-element.151.dy_ref.refs_1_, ...), custom_call_target="tpu_custom_call" | custom-call | flops 40000000000 | bytes 1048576 | tf_op jit(solution)/shard_map/grad_product/pallas_call | solution.py:678
  342.0 11.9 %space_rest.1 = (bf16[2,640,256]{2,1,0:T(8,128)(2,1)}, bf16[2,3,640,256]{3,2,1,0:T(8,128)(2,1)}, f32[2,8,640]{2,1,0:T(8,128)}) custom-call(bf16[640,1024]{1,0:T(8,128)(2,1)} %get-tuple-element.191.normed_ref.refs_0_, bf16[3,1024,128]{2,1,0:T(8,128)(2,1)} %collective-permute-done.23.q0.refs_3_, bf16[3,1024,128]{2,1,0:T(8,128)(2,1)} %collective-permute-done.24.q1.refs_4_, ...), custom_call_target="tpu_custom_call" | custom-call | flops 48000000000 | bytes 1048576 | tf_op jit(solution)/shard_map/space_rest/pallas_call | solution.py:267
  356.4 17.2 %space_back.1 = (f32[640,1024]{1,0:T(8,128)}, bf16[2,3,640,256]{3,2,1,0:T(8,128)(2,1)}) custom-call(bf16[640,1024]{1,0:T(8,128)(2,1)} %pad_maximum_fusion.4.dy_ref.refs_1_, bf16[2,3,640,256]{3,2,1,0:T(8,128)(2,1)} %get-tuple-element.165.proj_any, f32[2,8,640]{2,1,0:T(8,128)} %get-tuple-element.166.logs_any, bf16[3,1024,512]{2,1,0:T(8,128)(2,1)} %refs_0_.3, ...), custom_call_target="tpu_custom_call" | custom-call | flops 71999995904 | bytes 1048576 | tf_op jit(solution)/shard_map/space_back/pallas_call | solution.py:575
  378.0 11.2 %collective-permute-done.28 = bf16[2,4,128,512]{3,2,1,0:T(8,128)(2,1)} collective-permute-done((bf16[2,4,128,512]{3,2,1,0:T(8,128)(2,1)}, bf16[2,4,128,512]{3,2,1,0:T(8,128)(2,1)}, u32[]{:S(2)}, u32[]{:S(2)}) %collective-permute-start.28) | collective-permute-done | bytes 1048608 | tf_op jit(solution)/shard_map/ppermute | solution.py:702
  397.1 20.4 %space_back_end.1 = (bf16[640,1024]{1,0:T(8,128)(2,1)}, bf16[2,3,640,256]{3,2,1,0:T(8,128)(2,1)}, f32[1,1024]{1,0:T(1,128)}, f32[8,1024]{1,0:T(8,128)}) custom-call(bf16[640,1024]{1,0:T(8,128)(2,1)} %pad_maximum_fusion.4.dy_ref.refs_1_, bf16[2,3,640,256]{3,2,1,0:T(8,128)(2,1)} %get-tuple-element.169.proj_any, f32[2,8,640]{2,1,0:T(8,128)} %get-tuple-element.170.logs_any, ...), custom_call_target="tpu_custom_call" | custom-call | flops 83999997952 | bytes 1048576 | tf_op jit(solution)/shard_map/space_back_end/pallas_call | solution.py:575
  426.9 12.9 %grad_product.10 = (bf16[2,2,4,128,512]{4,3,2,1,0:T(8,128)(2,1)}, bf16[2,2,4,128,512]{4,3,2,1,0:T(8,128)(2,1)}) custom-call(s32[3]{0:T(128)} %pad_add_fusion.1.bits_ref, bf16[640,1024]{1,0:T(8,128)(2,1)} %get-tuple-element.191.normed_ref.refs_0_, bf16[640,1024]{1,0:T(8,128)(2,1)} %pad_maximum_fusion.4.dy_ref.refs_1_, ...), custom_call_target="tpu_custom_call" | custom-call | flops 40000000000 | bytes 1048576 | tf_op jit(solution)/shard_map/grad_product/pallas_call | solution.py:678
  440.4 11.3 %grad_product.11 = (bf16[2,2,4,128,512]{4,3,2,1,0:T(8,128)(2,1)}, bf16[2,2,4,128,512]{4,3,2,1,0:T(8,128)(2,1)}) custom-call(s32[3]{0:T(128)} %pad_add_fusion.1.bits_ref, bf16[640,1024]{1,0:T(8,128)(2,1)} %get-tuple-element.191.normed_ref.refs_0_, bf16[2,3,640,256]{3,2,1,0:T(8,128)(2,1)} %get-tuple-element.186.refs_2_.refs_1_, ...), custom_call_target="tpu_custom_call" | custom-call | flops 40000000000 | bytes 1048576 | tf_op jit(solution)/shard_map/grad_product/pallas_call | solution.py:678
  460.4 23.0 %collective-permute-done.30 = bf16[640,1024]{1,0:T(8,128)(2,1)S(1)} collective-permute-done((bf16[640,1024]{1,0:T(8,128)(2,1)}, bf16[640,1024]{1,0:T(8,128)(2,1)S(1)}, u32[]{:S(2)}, u32[]{:S(2)}) %collective-permute-start.30) | collective-permute-done | bytes 1310752 | tf_op jit(solution)/shard_map/ppermute | solution.py:702
  505.4 21.8 %collective-permute-done.46 = bf16[2,128,512]{2,1,0:T(8,128)(2,1)S(1)} collective-permute-done((bf16[2,128,512]{2,1,0:T(8,128)(2,1)S(1)}, bf16[2,128,512]{2,1,0:T(8,128)(2,1)S(1)}, u32[]{:S(2)}, u32[]{:S(2)}) %collective-permute-start.46) | collective-permute-done | bytes 262176 | tf_op jit(solution)/shard_map/ppermute | solution.py:702
  529.4 7.2 %collective-permute-done.57 = bf16[2,128,512]{2,1,0:T(8,128)(2,1)S(1)} collective-permute-done((bf16[2,128,512]{2,1,0:T(8,128)(2,1)S(1)}, bf16[2,128,512]{2,1,0:T(8,128)(2,1)S(1)}, u32[]{:S(2)}, u32[]{:S(2)}) %collective-permute-start.57) | collective-permute-done | bytes 262176 | tf_op jit(solution)/shard_map/ppermute | solution.py:702
  540.0 16.6 %collective-permute-done.41 = bf16[2,4,128,512]{3,2,1,0:T(8,128)(2,1)S(1)} collective-permute-done((bf16[2,4,128,512]{3,2,1,0:T(8,128)(2,1)S(1)}, bf16[2,4,128,512]{3,2,1,0:T(8,128)(2,1)S(1)}, u32[]{:S(2)}, u32[]{:S(2)}) %collective-permute-start.41) | collective-permute-done | bytes 1048608 | tf_op jit(solution)/shard_map/ppermute | solution.py:702
  593.1 9.1 %collective-permute-done.54 = bf16[2,128,512]{2,1,0:T(8,128)(2,1)S(1)} collective-permute-done((bf16[2,128,512]{2,1,0:T(8,128)(2,1)S(1)}, bf16[2,128,512]{2,1,0:T(8,128)(2,1)S(1)}, u32[]{:S(2)}, u32[]{:S(2)}) %collective-permute-start.54) | collective-permute-done | bytes 262176 | tf_op jit(solution)/shard_map/ppermute | solution.py:702
  (271 shorter events, 218.0 us)
Async XLA Ops:
  48.3 66.0 %all-to-all-start = ((bf16[8,2,40,1024]{3,2,1,0:T(8,128)(2,1)}), bf16[8,2,40,1024]{3,2,1,0:T(8,128)(2,1)S(1)}, u32[]{:S(2)}, u32[]{:S(2)}) async-start(bf16[8,2,40,1024]{3,2,1,0:T(8,128)(2,1)} %copy_bitcast_fusion), calls=%async_computation | async-start | bytes 2621440 | tf_op jit(solution)/shard_map/all_to_all | solution.py:862
  69.8 43.1 %collective-permute-start.13 = (bf16[512,1024]{1,0:T(8,128)(2,1)}, bf16[512,1024]{1,0:T(8,128)(2,1)}, u32[]{:S(2)}, u32[]{:S(2)}) collective-permute-start(bf16[512,1024]{1,0:T(8,128)(2,1)} %constant_dynamic-slice_fusion.8), channel_id=1, source_target_pairs={{0,1},{1,0},{2,3},{3,2},{4,5},{5,4},{6,7},{7,6},{8,9},{9,8},{10,11... | collective-permute-start | bytes 3145736 | tf_op jit(solution)/shard_map/ppermute | solution.py:702
  70.1 50.6 %collective-permute-start.6 = (bf16[4,1024,128]{2,1,0:T(8,128)(2,1)}, bf16[4,1024,128]{2,1,0:T(8,128)(2,1)}, u32[]{:S(2)}, u32[]{:S(2)}) collective-permute-start(bf16[4,1024,128]{2,1,0:T(8,128)(2,1)} %collective-permute-done.5.q0.refs_3_), channel_id=1, source_target_pairs={{0,2},{2,0},{4,6},{6,4},{8,10},{10,8},{12,14},{14,12},{1,3},{3,1},... | collective-permute-start | bytes 3145736 | tf_op jit(solution)/shard_map/ppermute | solution.py:702
  92.2 57.5 %collective-permute-start.11 = (bf16[1024,512]{1,0:T(8,128)(2,1)}, bf16[1024,512]{1,0:T(8,128)(2,1)}, u32[]{:S(2)}, u32[]{:S(2)}) collective-permute-start(bf16[1024,512]{1,0:T(8,128)(2,1)} %collective-permute-done.9.u0), channel_id=1, source_target_pairs={{0,16},{16,0},{1,17},{17,1},{2,18},{18,2},{3,19},{19,3},{4,20},{20... | collective-permute-start | bytes 3145736 | tf_op jit(solution)/shard_map/ppermute | solution.py:702
  112.8 36.8 %collective-permute-start.15 = (bf16[512,1024]{1,0:T(8,128)(2,1)}, bf16[512,1024]{1,0:T(8,128)(2,1)}, u32[]{:S(2)}, u32[]{:S(2)}) collective-permute-start(bf16[512,1024]{1,0:T(8,128)(2,1)} %collective-permute-done.13.d0), channel_id=1, source_target_pairs={{0,16},{16,0},{1,17},{17,1},{2,18},{18,2},{3,19},{19,3},{4,20},{20... | collective-permute-start | bytes 3145736 | tf_op jit(solution)/shard_map/ppermute | solution.py:702
  114.4 39.8 %all-to-all-start.1 = ((bf16[8,2,40,1024]{3,2,1,0:T(8,128)(2,1)}), bf16[8,2,40,1024]{3,2,1,0:T(8,128)(2,1)S(1)}, u32[]{:S(2)}, u32[]{:S(2)}) async-start(bf16[8,2,40,1024]{3,2,1,0:T(8,128)(2,1)} %copy.84), calls=%async_computation.1 | async-start | bytes 2621440 | tf_op jit(solution)/shard_map/all_to_all | solution.py:862
  152.7 47.2 %collective-permute-start.23 = (bf16[3,1024,128]{2,1,0:T(8,128)(2,1)S(1)}, bf16[3,1024,128]{2,1,0:T(8,128)(2,1)}, u32[]{:S(2)}, u32[]{:S(2)}) collective-permute-start(bf16[3,1024,128]{2,1,0:T(8,128)(2,1)S(1)} %constant_dynamic-slice_fusion.7), channel_id=1, source_target_pairs={{0,1},{1,0},{2,3},{3,2},{4,5},{5,4},{6,7},{7,6},{8,9},{9,8},{10,11... | collective-permute-start | bytes 2359304 | tf_op jit(solution)/shard_map/ppermute | solution.py:702
  194.3 68.9 %all-to-all-start.2 = ((bf16[8,2,40,1024]{3,2,1,0:T(8,128)(2,1)}), bf16[8,2,40,1024]{3,2,1,0:T(8,128)(2,1)}, u32[]{:S(2)}, u32[]{:S(2)}) async-start(bf16[8,2,40,1024]{3,2,1,0:T(8,128)(2,1)} %bitcast.266), calls=%async_computation.2 | async-start | bytes 2621440 | tf_op jit(solution)/shard_map/all_to_all | solution.py:862
  199.8 84.6 %collective-permute-start.25 = (bf16[3,1024,128]{2,1,0:T(8,128)(2,1)}, bf16[3,1024,128]{2,1,0:T(8,128)(2,1)}, u32[]{:S(2)}, u32[]{:S(2)}) collective-permute-start(bf16[3,1024,128]{2,1,0:T(8,128)(2,1)} %collective-permute-done.23.q0.refs_3_), channel_id=1, source_target_pairs={{0,16},{16,0},{1,17},{17,1},{2,18},{18,2},{3,19},{19,3},{4,20},{20... | collective-permute-start | bytes 2359304 | tf_op jit(solution)/shard_map/ppermute | solution.py:702
  237.1 55.9 %collective-permute-start.18 = (bf16[2,4,128,1024]{3,2,1,0:T(8,128)(2,1)}, bf16[2,4,128,1024]{3,2,1,0:T(8,128)(2,1)}, u32[]{:S(2)}, u32[]{:S(2)}) collective-permute-start(bf16[2,4,128,1024]{3,2,1,0:T(8,128)(2,1)} %fusion.4), channel_id=1, source_target_pairs={{0,1},{1,0},{2,3},{3,2},{4,5},{5,4},{6,7},{7,6},{8,9},{9,8},{10,11... | collective-permute-start | bytes 6291464 | tf_op jit(solution)/shard_map/ppermute | solution.py:702
  261.7 65.8 %collective-permute-start.21 = (bf16[2,4,128,1024]{3,2,1,0:T(8,128)(2,1)}, bf16[2,4,128,1024]{3,2,1,0:T(8,128)(2,1)}, u32[]{:S(2)}, u32[]{:S(2)}) collective-permute-start(bf16[2,4,128,1024]{3,2,1,0:T(8,128)(2,1)} %fusion.5), channel_id=1, source_target_pairs={{0,16},{16,0},{1,17},{17,1},{2,18},{18,2},{3,19},{19,3},{4,20},{20... | collective-permute-start | bytes 6291464 | tf_op jit(solution)/shard_map/ppermute | solution.py:702
  287.0 46.2 %all-to-all-start.3 = ((bf16[8,2,40,1024]{3,2,1,0:T(8,128)(2,1)}), bf16[8,2,40,1024]{3,2,1,0:T(8,128)(2,1)S(1)}, u32[]{:S(2)}, u32[]{:S(2)}) async-start(bf16[8,2,40,1024]{3,2,1,0:T(8,128)(2,1)} %bitcast.265), calls=%async_computation.3 | async-start | bytes 2621440 | tf_op jit(solution)/shard_map/all_to_all | solution.py:862
  292.3 49.7 %collective-permute-start.24 = (bf16[3,1024,128]{2,1,0:T(8,128)(2,1)}, bf16[3,1024,128]{2,1,0:T(8,128)(2,1)}, u32[]{:S(2)}, u32[]{:S(2)}) collective-permute-start(bf16[3,1024,128]{2,1,0:T(8,128)(2,1)} %collective-permute-done.23.q0.refs_3_), channel_id=1, source_target_pairs={{0,2},{2,0},{4,6},{6,4},{8,10},{10,8},{12,14},{14,12},{1,3},{3,1},... | collective-permute-start | bytes 2359304 | tf_op jit(solution)/shard_map/ppermute | solution.py:702
  292.9 49.1 %collective-permute-start.26 = (bf16[3,1024,128]{2,1,0:T(8,128)(2,1)}, bf16[3,1024,128]{2,1,0:T(8,128)(2,1)}, u32[]{:S(2)}, u32[]{:S(2)}) collective-permute-start(bf16[3,1024,128]{2,1,0:T(8,128)(2,1)} %collective-permute-done.25.q2.refs_5_), channel_id=1, source_target_pairs={{0,2},{2,0},{4,6},{6,4},{8,10},{10,8},{12,14},{14,12},{1,3},{3,1},... | collective-permute-start | bytes 2359304 | tf_op jit(solution)/shard_map/ppermute | solution.py:702
  327.5 93.7 %collective-permute-start.31 = (bf16[4,128,1024]{2,1,0:T(8,128)(2,1)}, bf16[4,128,1024]{2,1,0:T(8,128)(2,1)}, u32[]{:S(2)}, u32[]{:S(2)}) collective-permute-start(bf16[4,128,1024]{2,1,0:T(8,128)(2,1)} %get-tuple-element.143), channel_id=1, source_target_pairs={{0,16},{16,0},{1,17},{17,1},{2,18},{18,2},{3,19},{19,3},{4,20},{20... | collective-permute-start | bytes 3145736 | tf_op jit(solution)/shard_map/ppermute | solution.py:702
  335.0 38.6 %collective-permute-start.20 = (bf16[640,1024]{1,0:T(8,128)(2,1)S(1)}, bf16[640,1024]{1,0:T(8,128)(2,1)}, u32[]{:S(2)}, u32[]{:S(2)}) collective-permute-start(bf16[640,1024]{1,0:T(8,128)(2,1)S(1)} %copy-done.18), channel_id=1, source_target_pairs={{0,1},{1,0},{2,3},{3,2},{4,5},{5,4},{6,7},{7,6},{8,9},{9,8},{10,11... | collective-permute-start | bytes 3932168 | tf_op jit(solution)/shard_map/ppermute | solution.py:702
  338.3 50.8 %collective-permute-start.28 = (bf16[2,4,128,512]{3,2,1,0:T(8,128)(2,1)}, bf16[2,4,128,512]{3,2,1,0:T(8,128)(2,1)}, u32[]{:S(2)}, u32[]{:S(2)}) collective-permute-start(bf16[2,4,128,512]{3,2,1,0:T(8,128)(2,1)} %fusion.10), channel_id=1, source_target_pairs={{0,1},{1,0},{2,3},{3,2},{4,5},{5,4},{6,7},{7,6},{8,9},{9,8},{10,11... | collective-permute-start | bytes 3145736 | tf_op jit(solution)/shard_map/ppermute | solution.py:702
  354.0 65.5 %collective-permute-start.32 = (bf16[4,128,1024]{2,1,0:T(8,128)(2,1)}, bf16[4,128,1024]{2,1,0:T(8,128)(2,1)}, u32[]{:S(2)}, u32[]{:S(2)}) collective-permute-start(bf16[4,128,1024]{2,1,0:T(8,128)(2,1)} %get-tuple-element.161), channel_id=1, source_target_pairs={{0,1},{1,0},{2,3},{3,2},{4,5},{5,4},{6,7},{7,6},{8,9},{9,8},{10,11... | collective-permute-start | bytes 3145736 | tf_op jit(solution)/shard_map/ppermute | solution.py:702
  354.9 37.1 %collective-permute-start.29 = (bf16[2,4,128,512]{3,2,1,0:T(8,128)(2,1)}, bf16[2,4,128,512]{3,2,1,0:T(8,128)(2,1)}, u32[]{:S(2)}, u32[]{:S(2)}) collective-permute-start(bf16[2,4,128,512]{3,2,1,0:T(8,128)(2,1)} %fusion.11), channel_id=1, source_target_pairs={{0,16},{16,0},{1,17},{17,1},{2,18},{18,2},{3,19},{19,3},{4,20},{20... | collective-permute-start | bytes 3145736 | tf_op jit(solution)/shard_map/ppermute | solution.py:702
  451.7 38.2 %collective-permute-start.39 = (bf16[2,2,4,128,512]{4,3,2,1,0:T(8,128)(2,1)}, bf16[2,2,4,128,512]{4,3,2,1,0:T(8,128)(2,1)S(1)}, u32[]{:S(2)}, u32[]{:S(2)}) collective-permute-start(bf16[2,2,4,128,512]{4,3,2,1,0:T(8,128)(2,1)} %get-tuple-element.196), channel_id=1, source_target_pairs={{0,2},{2,0},{4,6},{6,4},{8,10},{10,8},{12,14},{14,12},{1,3},{3,1},... | collective-permute-start | bytes 6291464 | tf_op jit(solution)/shard_map/ppermute | solution.py:702
  454.1 37.0 %collective-permute-start.42 = (bf16[2,128,1024]{2,1,0:T(8,128)(2,1)S(1)}, bf16[2,128,1024]{2,1,0:T(8,128)(2,1)S(1)}, u32[]{:S(2)}, u32[]{:S(2)}) collective-permute-start(bf16[2,128,1024]{2,1,0:T(8,128)(2,1)S(1)} %get-tuple-element.265), channel_id=1, source_target_pairs={{0,4},{2,6},{4,0},{6,2},{8,12},{10,14},{12,8},{14,10},{1,5},{3,7},... | collective-permute-start | bytes 1572872 | tf_op jit(solution)/shard_map/ppermute | solution.py:702
  456.5 38.3 %collective-permute-start.43 = (bf16[2,128,1024]{2,1,0:T(8,128)(2,1)S(1)}, bf16[2,128,1024]{2,1,0:T(8,128)(2,1)S(1)}, u32[]{:S(2)}, u32[]{:S(2)}) collective-permute-start(bf16[2,128,1024]{2,1,0:T(8,128)(2,1)S(1)} %get-tuple-element.266), channel_id=1, source_target_pairs={{0,8},{2,10},{4,12},{6,14},{8,0},{10,2},{12,4},{14,6},{1,9},{3,11}... | collective-permute-start | bytes 1572872 | tf_op jit(solution)/shard_map/ppermute | solution.py:702
  490.0 37.2 %collective-permute-start.46 = (bf16[2,128,512]{2,1,0:T(8,128)(2,1)S(1)}, bf16[2,128,512]{2,1,0:T(8,128)(2,1)S(1)}, u32[]{:S(2)}, u32[]{:S(2)}) collective-permute-start(bf16[2,128,512]{2,1,0:T(8,128)(2,1)S(1)} %get-tuple-element.283), channel_id=1, source_target_pairs={{0,8},{2,10},{4,12},{6,14},{8,0},{10,2},{12,4},{14,6},{1,9},{3,11}... | collective-permute-start | bytes 786440 | tf_op jit(solution)/shard_map/ppermute | solution.py:702
  494.8 42.0 %collective-permute-start.40 = (bf16[2,4,128,512]{3,2,1,0:T(8,128)(2,1)S(1)}, bf16[2,4,128,512]{3,2,1,0:T(8,128)(2,1)}, u32[]{:S(2)}, u32[]{:S(2)}) collective-permute-start(bf16[2,4,128,512]{3,2,1,0:T(8,128)(2,1)S(1)} %fusion.13), channel_id=1, source_target_pairs={{0,1},{1,0},{2,3},{3,2},{4,5},{5,4},{6,7},{7,6},{8,9},{9,8},{10,11... | collective-permute-start | bytes 3145736 | tf_op jit(solution)/shard_map/ppermute | solution.py:702
  (67 other events, 1019.2 us)

commit v3 on v2

--- a/solution.py
+++ b/solution.py
@@ -39,8 +39,11 @@
     return pltpu.CompilerParams(vmem_limit_bytes=LIMIT)
 
 
-def cost(micros):
-    return pl.CostEstimate(flops=int(micros * 4e9), bytes_accessed=2**20, transcendentals=0)
+MICROS = {'space_partner': 1.2, 'space_own': 1.2, 'space_mix': 1.2, 'space_rest': 0.9985, 'time_forward': 44.8106, 'feed_forward': 4.9837, 'time_back': 11.3339, 'time_back_end': 0.852, 'space_back': 6.0811, 'space_back_end': 30.4331, 'grad_up': 12.841, 'grad_down': 0.5749, 'time_one': 0.1151, 'time_two': 0.6269, 'space_two': 0.3517, 'space_one': 1.624, 'pause0': 1.2, 'pause1': 1.2, 'pause2': 1.2, 'pause3': 1.2, 'pause4': 5.9164, 'pause5': 3.5109, 'pause6': 2.6464, 'pause7': 12.3069, 'pause8': 160.0718, 'pause9': 0.8432}
+
+
+def cost(name):
+    return pl.CostEstimate(flops=int(MICROS[name] * 1e9), bytes_accessed=2**20, transcendentals=0)
 
 
 def group_mask(kind, length):
@@ -204,7 +207,7 @@
         ),
         out_shape=[o[1] for o in outs],
         compiler_params=params(),
-        cost_estimate=cost(12),
+        cost_estimate=cost("space_own" if full else "space_partner"),
         name="space_own" if full else "space_partner",
     )(clip, frames_a, frames_b, shifts, gain, qkv)
 
@@ -280,7 +283,7 @@
         ],
         scratch_shapes=[pltpu.VMEM((2, 3, depth, BLOCK), BF), pltpu.SemaphoreType.DMA((2, 2))],
         compiler_params=params(),
-        cost_estimate=cost(12),
+        cost_estimate=cost("space_rest"),
         name="space_rest",
     )(normed, *qkv_slots)
 
@@ -312,7 +315,7 @@
         ),
         out_shape=shape_of(rows, depth),
         compiler_params=params(),
-        cost_estimate=cost(6),
+        cost_estimate=cost("space_mix"),
         name="space_mix",
     )(bits, started, own, other, weight, *out_slots)
 
@@ -367,7 +370,7 @@
             pltpu.SemaphoreType.DMA((2, 2)),
         ],
         compiler_params=params(),
-        cost_estimate=cost(29),
+        cost_estimate=cost("time_forward"),
         name="time_forward",
     )(middle, gain, qkv, out, *slots)
 
@@ -390,7 +393,7 @@
 
 
 def ffn_kernel(late_ref, cot_ref, gain_ref, up_any, down_any, u0, u1, u2, u3, d0, d1, d2, d3,
-               out_ref, d_late_ref, normed_ref, gelu_ref, d_hidden_ref, d_gain_ref, total, d_normed, wu, wd, sems):
+               out_ref, d_late_ref, normed_ref, hidden_ref, d_gain_ref, total, d_normed, wu, wd, sems):
     step = pl.program_id(0)
     rows, depth = late_ref.shape
     width = wu.shape[2]
@@ -431,9 +434,9 @@
     for chunk in row_chunks(rows, rows // 2):
         gelu, slope = gelu_parts(dot_n(normed_ref[chunk, :], wu[slot]))
         gelu = gelu.astype(BF)
-        gelu_ref[0, 0, chunk, :] = gelu
+        hidden_ref[0, 0, chunk, :] = gelu
         d_hidden = (dot_t(cot_ref[chunk, :], wd[slot]) * slope).astype(BF)
-        d_hidden_ref[0, 0, chunk, :] = d_hidden
+        hidden_ref[0, 1, chunk, :] = d_hidden
         total[chunk, :] += dot_n(gelu, wd[slot])
         d_normed[chunk, :] += dot_t(d_hidden, wu[slot])
 
@@ -452,18 +455,17 @@
 def feed_forward(latest, cot, gain, up, down, up_slots, down_slots):
     rows, depth = latest.shape
     width = up.shape[1] // 4
-    stream = pl.BlockSpec((1, 1, rows, width), lambda s: (s, 0, 0, 0))
+    stream = pl.BlockSpec((1, 2, rows, width), lambda s: (s, 0, 0, 0))
     return pl.pallas_call(
         ffn_kernel,
         grid=(8,),
         in_specs=[whole(rows, depth), whole(rows, depth), whole(1, depth)] + [any_spec()] * 10,
-        out_specs=[whole(rows, depth), whole(rows, depth), whole(rows, depth), stream, stream, whole(1, depth)],
+        out_specs=[whole(rows, depth), whole(rows, depth), whole(rows, depth), stream, whole(1, depth)],
         out_shape=[
             shape_of(rows, depth),
             shape_of(rows, depth),
             shape_of(rows, depth),
-            shape_of(8, 1, rows, width),
-            shape_of(8, 1, rows, width),
+            shape_of(8, 2, rows, width),
             shape_of(1, depth, dtype=F32),
         ],
         scratch_shapes=[
@@ -474,7 +476,7 @@
             pltpu.SemaphoreType.DMA((2, 2)),
         ],
         compiler_params=params(),
-        cost_estimate=cost(34),
+        cost_estimate=cost("feed_forward"),
         name="feed_forward",
     )(latest, cot, gain, up, down, *up_slots, *down_slots)
 
@@ -589,7 +591,7 @@
             pltpu.SemaphoreType.DMA((2, 2)),
         ],
         compiler_params=params(),
-        cost_estimate=cost(21 if final else 18),
+        cost_estimate=cost(name),
         name=name,
     )(dy, proj, logs, *others)
 
@@ -597,105 +599,114 @@
 def grad_kernel(chunk, y_first, lefts, bits_ref, *refs):
     count = len(lefts)
     n_left = max(lefts) + 1
-    left_refs, own_refs, other_refs = refs[:n_left], refs[n_left : n_left + count], refs[n_left + count : n_left + 2 * count]
-    send_ref, keep_ref, turned = refs[n_left + 2 * count :]
+    left_refs, refs = refs[: 2 * n_left], refs[2 * n_left :]
+    own_refs, other_refs = refs[: 2 * count], refs[2 * count : 4 * count]
+    keep_ref, leave_ref, turned = refs[4 * count :]
     step = pl.program_id(0)
     core_bit, z_index = bits_ref[1], bits_ref[2]
-    stacks = send_ref.shape[2]
-    cut = send_ref.shape[3]
+    _, stacks, cut, _ = keep_ref.shape
+    rows = left_refs[0].shape[0]
 
     @pl.when(step == 0)
     def _():
         for n, left_ref in enumerate(left_refs):
+            columns = slice(n % 2 * rows, (n % 2 + 1) * rows)
             for j in range(stacks):
+                place = slice(j * cut, (j + 1) * cut)
                 start = pl.multiple_of((z_index ^ j) * 2 * cut, 2 * cut)
+                if cut % 128 == 0:
+                    start = pl.multiple_of(start + core_bit * cut, cut)
+                    turned[n // 2, place, columns] = left_ref[:, pl.ds(start, cut)].T
+                    continue
                 both = left_ref[:, pl.ds(start, 2 * cut)].T
-                rows = slice(j * cut, (j + 1) * cut)
                 for core in range(2):
 
                     @pl.when(core_bit == core)
-                    def _(core=core, both=both, rows=rows, n=n):
-                        turned[n, 1, rows, :] = both[core * cut : (core + 1) * cut]
-                        turned[n, 0, rows, :] = both[(1 - core) * cut : (2 - core) * cut]
-
-    def fill(side, half, out_ref):
+                    def _(core=core, both=both, place=place, n=n, columns=columns):
+                        turned[n // 2, place, columns] = both[core * cut : (core + 1) * cut]
+
+    def fill(half, out_ref):
         matrix = 0
-        for n, own_ref, other_ref in zip(lefts, own_refs, other_refs):
-            source = own_ref if half == 0 else other_ref
-            span = source.shape[3]
-            for t in range(source.shape[1]):
-                for b in range(source.shape[0]):
-                    block = dot_n(turned[n, side], source[b, t]).astype(BF)
+        for term, n in enumerate(lefts):
+            mine_ref, partner_ref = (own_refs if half == 0 else other_refs)[2 * term : 2 * term + 2]
+            blocks, parts, _, span = mine_ref.shape
+            for t in range(parts):
+                for b in range(blocks):
+                    mine = mine_ref[b, t]
+                    if half == 0:
+                        partner = partner_ref[b, t]
+                    elif span == chunk:
+                        partner = partner_ref[1 - b, t]
+                    else:
+                        partner = partner_ref[b, t]
+                        partner = jnp.concatenate([partner[:, chunk:], partner[:, :chunk]], 1)
+                    block = dot_n(turned[n], jnp.concatenate([mine, partner], 0)).astype(BF)
                     for i in range(span // chunk):
                         index = b * (span // chunk) + i
                         if half == 1:
                             index = index ^ core_bit
                         lanes = pl.ds(pl.multiple_of((2 * matrix + index) * chunk, chunk), chunk)
                         for j in range(stacks):
-                            out_ref[0, 0, j, :, lanes] = block[
+                            out_ref[0, j, :, lanes] = block[
                                 j * cut : (j + 1) * cut, i * chunk : (i + 1) * chunk
                             ]
                 matrix += 1
 
-    for g in range(8):
+    for g in range(4):
 
         @pl.when(step == g)
         def _(g=g):
-            first, second = g // 2 % 2, g % 2
-            fill(g // 4, second if y_first else first, send_ref if g < 4 else keep_ref)
-
-
-def grad_product(bits, left_arrays, terms, chunk, y_first, sizes, micros):
-    rows, depth = left_arrays[0].shape
+            first, second = 1 - g // 2, g % 2
+            fill(second if y_first else first, leave_ref if first == 1 else keep_ref)
+
+
+def grad_product(bits, left_arrays, terms, chunk, y_first, sizes, name):
+    rows, depth = left_arrays[0][0].shape
     stacks = sizes["wide"] // 2
     cut = depth // sizes["wide"]
     columns = 2 * sum(term[4] for term in terms) * chunk
 
-    def y_flip(g):
-        return g % 4 // 2 if y_first else g % 2
-
-    def own_index(g, b):
-        flip = y_flip(g)
-        if not y_first:
-            flip = jnp.where(g % 4 // 2 == 0, flip, 1)
-        return b[0] ^ flip
-
-    def other_index(g, b):
-        flip = y_flip(g)
-        if not y_first:
-            flip = jnp.where(g % 4 // 2 == 1, flip, 0)
-        return flip
-
-    def half_spec(value, index, first_part, parts):
-        array, at = value
-        lead = 2 * chunk // array.shape[3]
-        return pl.BlockSpec(
-            (lead, parts, *array.shape[2:]),
-            lambda g, b: (2 * at + index(g, b), first_part // parts, 0, 0),
-        )
-
-    block = (1, 1, stacks, cut, columns)
+    def flip(g, half):
+        if y_first:
+            return 1 - g // 2
+        return jnp.where(1 - g // 2 == half, g % 2, 1 - half)
+
+    def half_spec(value, half, first_part, parts):
+        arrays, at = value
+        shape = arrays[0].shape
+        lead = 2 * chunk // shape[3]
+
+        def index(g, b):
+            y = flip(g, half)
+            return (2 * at + ((b[0] ^ y) if half == 0 else y), first_part // parts, 0, 0)
+
+        return [pl.BlockSpec((lead, parts, *shape[2:]), index)] * 2
+
+    block = (1, stacks, cut, columns)
     return pl.pallas_call(
         partial(grad_kernel, chunk, y_first, [term[0] for term in terms]),
         grid_spec=pltpu.PrefetchScalarGridSpec(
             num_scalar_prefetch=1,
-            grid=(8,),
-            in_specs=[whole(rows, depth)] * len(left_arrays)
-            + [half_spec(term[1], own_index, *term[3:]) for term in terms]
-            + [half_spec(term[2], other_index, *term[3:]) for term in terms],
+            grid=(4,),
+            in_specs=[whole(rows, depth)] * (2 * len(left_arrays))
+            + [spec for term in terms for spec in half_spec(term[1], 0, *term[3:])]
+            + [spec for term in terms for spec in half_spec(term[2], 1, *term[3:])],
             out_specs=[
-                pl.BlockSpec(block, lambda g, b: (jnp.minimum(g, 3) // 2, jnp.minimum(g, 3) % 2, 0, 0, 0)),
-                pl.BlockSpec(
-                    block, lambda g, b: (jnp.maximum(g - 4, 0) // 2, jnp.maximum(g - 4, 0) % 2, 0, 0, 0)
-                ),
+                pl.BlockSpec(block, lambda g, b: (jnp.maximum(g - 2, 0), 0, 0, 0)),
+                pl.BlockSpec(block, lambda g, b: (jnp.minimum(g, 1), 0, 0, 0)),
             ],
-            scratch_shapes=[pltpu.VMEM((len(left_arrays), 2, stacks * cut, rows), BF)],
+            scratch_shapes=[pltpu.VMEM((len(left_arrays), stacks * cut, 2 * rows), BF)],
         ),
-        out_shape=[shape_of(2, 2, stacks, cut, columns)] * 2,
+        out_shape=[shape_of(2, stacks, cut, columns)] * 2,
         compiler_params=params(),
-        cost_estimate=cost(micros),
+        cost_estimate=cost(name),
         name="grad_product",
-    )(bits, *left_arrays, *[term[1][0] for term in terms], *[term[2][0] for term in terms])
+    )(
+        bits,
+        *[array for pair in left_arrays for array in pair],
+        *[array for term in terms for array in term[1][0]],
+        *[array for term in terms for array in term[2][0]],
+    )
 
 
 def swap(value, axis, sizes, step=1):
@@ -704,6 +715,21 @@
 
 def after(value, *others):
     return lax.optimization_barrier((value, *others))[0]
+
+
+def pause_kernel(x_ref, o_ref):
+    o_ref[...] = x_ref[...]
+
+
+def pause(tokens, *deps):
+    token = after(jnp.zeros((8, 128), F32), *deps)
+    tokens.append(pl.pallas_call(
+        pause_kernel,
+        out_shape=shape_of(8, 128, dtype=F32),
+        cost_estimate=cost("pause%d" % len(tokens)),
+        name="pause",
+    )(token))
+    return tokens[-1]
 
 
 def wide(value):
@@ -753,23 +779,16 @@
 
 
 class Reduction:
-    def __init__(self, moves, send, keep, y_first):
+    def __init__(self, moves, keep, leaving, y_first):
         self.moves, self.sizes, self.keep = moves, moves.sizes, keep
         self.axes = ("clip", "tp") if y_first else ("tp", "clip")
-        self.got = swap(send, "wide", self.sizes)
-
-    def second(self, *deps):
-        self.leaving = (wide(self.keep[1]) + wide(self.got[1])).astype(BF)
-        if deps:
-            self.leaving = after(self.leaving, *deps)
-        self.arrived = swap(self.leaving, self.axes[0], self.sizes)
-        return self.leaving
+        self.leaving = leaving
+        self.arrived = swap(leaving, self.axes[0], self.sizes)
 
     def third(self, *deps):
-        total = wide(self.keep[0]) + wide(self.got[0]) + wide(self.arrived)
+        keep = after(self.keep, *deps) if deps else self.keep
+        total = wide(keep) + wide(self.arrived)
         self.leaving = total[1].astype(BF)
-        if deps:
-            self.leaving = after(self.leaving, *deps)
         self.mine = total[0].astype(BF)
         self.arrived = swap(self.leaving, self.axes[1], self.sizes)
         return self.leaving
@@ -911,131 +930,189 @@
     def cores(value, *deps):
         return swap(after(value, *deps) if deps else value, "wide", sizes)
 
-    so_x = from_x(space_out, 0)
-    cot_moved = exchange(pack_grid(pick(cot_a), pick(cot_b)))
+    tokens = []
+
+    def product(left_arrays, terms, chunk, y_first, name):
+        return grad_product(moves.bits, left_arrays, terms, chunk, y_first, sizes, name)
+
+    def both(value, *deps):
+        return (value, cores(value, *deps))
+
+    so_piece = moves.quarter(space_out, 0)
+    out_piece = moves.quarter(time_out, 0)
+    out_piece = out_piece.reshape(PAIR, -1, PAIR).transpose(1, 0, 2).reshape(1, -1, PAIR)
+    time_piece = jnp.concatenate([moves.quarter(time_qkv, 2), out_piece])
+    cot_packed = pack_grid(pick(cot_a), pick(cot_b))
+    so_x = swap(so_piece, "tp", sizes)
+    time_x = swap(time_piece, "tp", sizes)
+    cot_moved = exchange(cot_packed)
+    token = pause(tokens, so_piece, time_piece, cot_packed)
+    cot_moved = after(cot_moved, token)
     (partner_heads,) = space_heads(
-        1 - clip, frames_a, frames_b, shifts, gain_space, space_qkv, space_groups, False
+        after(1 - clip, token),
+        frames_a, frames_b, shifts, gain_space, space_qkv, space_groups, False,
     )
     heads_other = swap(partner_heads, "tp", sizes)
     so_y = from_y(so_x, partner_heads)
     heads_own, proj_own, logs_own, started, normed_space = space_heads(
-        clip, frames_a, frames_b, shifts, gain_space, space_qkv, space_groups, True
-    )
-    so_slots = (so_x, cores(so_x, heads_own), so_y, cores(so_y, heads_own))
+        after(clip, partner_heads), frames_a, frames_b, shifts, gain_space, space_qkv, space_groups, True
+    )
+    so_x, so_y = after(so_x, heads_own), after(so_y, heads_own)
+    so_slots = (so_x, cores(so_x), so_y, cores(so_y))
+    up_piece = moves.quarter(ffn_up, 1)
+    down_piece = moves.quarter(ffn_down, 0)
+    up_x = swap(after(up_piece, heads_other), "tp", sizes)
     middle = space_mix(moves.bits, started, heads_own, heads_other, space_out, so_slots)
     packed = pack_grid(middle[:rows_a], middle[rows_a:])
-    middle = exchange(packed)
-
-    out_piece = moves.quarter(time_out, 0)
-    out_piece = out_piece.reshape(PAIR, -1, PAIR).transpose(1, 0, 2).reshape(1, -1, PAIR)
-    time_piece = jnp.concatenate([moves.quarter(time_qkv, 2), out_piece])
-    time_x = swap(after(time_piece, heads_own), "tp", sizes)
-    up_x = from_x(ffn_up, 1, heads_own)
-    time_y = from_y(time_x)
-    time_slots = (time_x, cores(time_x), time_y, cores(time_y))
-    down_x = from_x(ffn_down, 0, time_x)
-    up_y = from_y(up_x, time_x)
-    down_y = from_y(down_x)
-    sq_x = from_x(space_qkv, 2, down_x)
+    middle_moved = exchange(after(packed, cot_moved))
+    time_x = after(time_x, packed)
+    time_y = swap(time_x, "clip", sizes)
+    time_x_core = cores(time_x)
+    token = pause(tokens, packed)
+
+    up_x = after(up_x, token)
+    up_y = swap(up_x, "clip", sizes)
+    up_x_core = cores(up_x)
+    down_x = swap(after(down_piece, up_x), "tp", sizes)
+    token = pause(tokens, up_x)
+    time_y = after(time_y, token)
+    time_slots = (time_x, time_x_core, time_y, cores(time_y))
+    down_x = after(down_x, token)
+    down_y = swap(down_x, "clip", sizes)
+    down_x_core = cores(down_x)
+    sq_x = swap(after(moves.quarter(space_qkv, 2), down_x), "tp", sizes)
+    token = pause(tokens, time_y, down_x)
+    middle = unpack_grid(after(middle_moved, token))
+    up_y = after(up_y, token)
+    up_y_core = cores(up_y)
     latest, normed_time, heads_time, proj_time, logs_time = time_forward(
-        unpack_grid(middle), gain_time, time_qkv, time_out, time_slots, time_groups
-    )
-    middle = unpack_grid(middle)
-    up_slots = (up_x, cores(up_x, latest), up_y, cores(up_y, latest))
-    down_slots = (down_x, cores(down_x, latest), down_y, cores(down_y, latest))
-    cot = unpack_grid(cot_moved)
-    out, d_latest, normed_ffn, gelu, d_hidden, d_gain_ffn = feed_forward(
+        after(middle, up_y), gain_time, time_qkv, time_out, time_slots, time_groups
+    )
+    down_y = after(down_y, latest)
+    up_slots = (up_x, up_x_core, up_y, up_y_core)
+    down_slots = (down_x, down_x_core, down_y, cores(down_y))
+    cot = unpack_grid(after(cot_moved, latest))
+    out, d_latest, normed_ffn, hidden, d_gain_ffn = feed_forward(
         latest, cot, gain_ffn, ffn_up, ffn_down, up_slots, down_slots
     )
+
     out_packed = pack_frames(out)
     out_moved = exchange(out_packed)
-    sq_y = from_y(sq_x, out_packed)
-
-    def product(left_arrays, terms, chunk, y_first, micros):
-        return moves.reduction(
-            grad_product(moves.bits, left_arrays, terms, chunk, y_first, sizes, micros), y_first
-        )
-
+    normed_time2, heads_time2 = both(normed_time, latest), both(heads_time[:, None], latest)
+    cot2, normed_ffn2, hidden2 = both(cot, latest), both(normed_ffn), both(hidden)
+    partial_time, d_proj_own = branch_back(
+        "time_back", after(d_latest, out_packed), proj_time, logs_time, 0,
+        (time_qkv, time_out), time_groups,
+    )
+    own = (both(d_proj_own), 0)
+    d_latest2 = both(d_latest, partial_time)
+    sq_x = after(sq_x, partial_time)
+    sq_y = swap(sq_x, "clip", sizes)
     chunk = ffn_up.shape[1] // 4
-    up = product([after(normed_ffn, out_packed)], [(0, (d_hidden, 0), (d_hidden, 1), 0, 1)], chunk, False, 15)
-    down = product([after(cot, up.keep)], [(0, (gelu, 0), (gelu, 1), 0, 1)], chunk, True, 15)
-    gate = up.second(down.keep)
-    partial_time, d_proj_own = branch_back(
-        "time_back", after(d_latest, gate), proj_time, logs_time, 0, (time_qkv, time_out), time_groups
-    )
-    sq_slots = (sq_x, cores(sq_x, partial_time), sq_y, cores(sq_y, partial_time))
-    gate = down.second(partial_time)
+    up = product(
+        [(after(normed_ffn2[0], partial_time), normed_ffn2[1])],
+        [(0, (hidden2, 0), (hidden2, 1), 1, 1)], chunk, False, "grad_up",
+    )
+    up = moves.reduction(up, False)
+    sq_x, sq_y = after(sq_x, up.keep), after(sq_y, up.keep, d_latest2[1])
+    sq_slots = (sq_x, cores(sq_x), sq_y, cores(sq_y))
+    down = product(
+        [(after(cot2[0], up.keep), cot2[1])], [(0, (hidden2, 0), (hidden2, 1), 0, 1)], chunk, True, "grad_down"
+    )
+    down = moves.reduction(down, True)
+    out_rows = unpack_frames(after(out_moved, down.keep))
+    out_partner = swap(out_rows, "tp", sizes)
     d_middle, d_proj_rest, d_gain_time, _ = branch_back(
         "time_back_end", d_latest, proj_time, logs_time, 2, (time_slots,), time_groups,
-        (middle, gain_time, after(partial_time, gate, out_moved)), ((0, rows),),
-    )
+        (middle, gain_time, after(partial_time, out_rows)), ((0, rows),),
+    )
+    rest = (both(d_proj_rest), 0)
     packed = pack_frames(d_middle)
     d_middle = exchange(packed)
     gate = up.third(packed)
-    heads_time = heads_time[:, None]
-    own, rest = (d_proj_own, 0), (d_proj_rest, 0)
-    time_one = product([after(normed_time, gate)], [(0, own, rest, 0, 2)], PAIR, False, 10)
-    out_rows = unpack_frames(after(out_moved, time_one.keep))
-    out_partner = swap(out_rows, "tp", sizes)
+    time_one = product(
+        [(after(normed_time, gate), normed_time2[1])], [(0, own, rest, 0, 2)], PAIR, False, "time_one"
+    )
+    time_one = moves.reduction(time_one, False)
     time_two = product(
-        [normed_time, after(d_latest, time_one.keep)],
-        [(0, own, rest, 2, 1), (1, (heads_time, 0), (heads_time, 1), 0, 1)],
-        PAIR, True, 10,
-    )
-    gate = time_one.second(time_two.keep)
-    heads_rest, proj_rest, logs_rest = space_rest(after(normed_space, gate), sq_slots, space_groups)
-    gate = down.third(heads_rest)
-    gate2 = time_two.second(heads_rest)
-    d_middle = unpack_frames(d_middle)
-    d_middle = after(d_middle, gate, gate2)
+        [(normed_time, normed_time2[1]), (after(d_latest, time_one.keep), d_latest2[1])],
+        [(0, own, rest, 2, 1), (1, (heads_time2, 0), (heads_time2, 1), 0, 1)],
+        PAIR, True, "time_two",
+    )
+    time_two = moves.reduction(time_two, True)
+    gate = down.third(time_two.keep)
+    out_a, out_b = both_clips(out_rows, after(out_partner, gate))
+    heads_rest, proj_rest, logs_rest = space_rest(
+        after(normed_space, gate, out_a, out_b), sq_slots, space_groups
+    )
+    heads_rest2 = both(heads_rest[:, None])
+    heads_own2, normed_space2 = both(heads_own[:, None], heads_rest), both(normed_space, heads_rest)
+    gate = time_one.third(heads_rest)
+    d_middle = unpack_frames(after(d_middle, gate))
+    d_middle2 = both(d_middle)
     partial_space, d_proj_own = branch_back(
         "space_back", d_middle, proj_own, logs_own, 0, (space_qkv, space_out), space_groups
     )
-    out_a, out_b = both_clips(out_rows, after(out_partner, partial_space))
-    gate = time_one.third(partial_space)
-    gate2 = time_two.third(gate)
+    own = (both(d_proj_own), 0)
+    ffn, time = Pair(moves, up, down), Pair(moves, time_one, time_two)
+    gates = [up.sum(partial_space), down.sum(partial_space)]
+    ffn.fourth()
+    gates += [time_two.third(gates[1])]
+    token = pause(tokens, *gates)
     segments = tuple((i * grid_a, grid_a) for i in range(n_frames)) + tuple(
         (rows_a + i * grid_b, grid_b) for i in range(n_frames)
     )
     d_started, d_proj_rest, d_gain_space, frame_sums = branch_back(
         "space_back_end", d_middle, proj_rest, logs_rest, 0, (sq_slots, so_slots), space_groups,
-        (started, gain_space, after(partial_space, gate, gate2, out_a, out_b)), segments, True,
-    )
-    own, rest = (d_proj_own, 0), (d_proj_rest, 0)
-    gates = [r.sum(d_started) for r in (up, down, time_one, time_two)]
-    ffn, time = Pair(moves, up, down), Pair(moves, time_one, time_two)
-    gates = [ffn.fourth(*gates)]
-    gates += [time.fourth(*gates)]
+        (started, gain_space, after(partial_space, token)), segments, True,
+    )
+    rest = (both(d_proj_rest), 0)
+    started_partner = swap(d_started, "tp", sizes)
     d_table = jnp.einsum(
         "fa,fd->ad", pick(one_hot), frame_sums[: 2 * n_frames], precision=lax.Precision.HIGHEST
     )
     small, small_other = moves.small_first(jnp.concatenate([d_table, d_gain_space, d_gain_time, d_gain_ffn]))
-    started_partner = swap(d_started, "tp", sizes)
+    gates = [time_one.sum(d_started), time_two.sum(d_started)]
+    time.fourth()
     space_two = product(
-        [after(normed_space, *gates, small), d_middle],
-        [(0, own, rest, 2, 1), (1, (heads_own[:, None], 0), (heads_rest[:, None], 0), 0, 1)],
-        PAIR, True, 10,
-    )
+        [(after(normed_space, small, *gates), normed_space2[1]), d_middle2],
+        [(0, own, rest, 2, 1), (1, (heads_own2, 0), (heads_rest2, 0), 0, 1)],
+        PAIR, True, "space_two",
+    )
+    space_two = moves.reduction(space_two, True)
     small = small + after(small_other, space_two.keep)
     small_other = swap(small, "tp", sizes)
-    space_one = product([after(normed_space, space_two.keep, small)], [(0, own, rest, 0, 2)], PAIR, False, 10)
-    gate = space_two.second(space_one.keep)
-    small = small + after(small_other, gate)
-    d_frames_a, d_frames_b = both_clips(d_started, after(started_partner, gate))
-    gate = space_one.second(d_frames_a, d_frames_b)
+    space_one = product(
+        [(after(normed_space, space_two.keep, small), normed_space2[1])], [(0, own, rest, 0, 2)], PAIR, False, "space_one"
+    )
+    space_one = moves.reduction(space_one, False)
+    token = pause(tokens, space_one.keep)
+    small = small + after(small_other, token)
+    small_other = small
     step = 1
     while step < sizes["clip"]:
-        small = small + swap(small, "clip", sizes, step)
+        small_other = swap(small, "clip", sizes, step)
+        if 2 * step < sizes["clip"]:
+            small = small + small_other
         step *= 2
-    gate = ffn.fifth(gate)
-    gate = time.fifth(gate, small)
-    gate = space_two.third(gate)
-    gate = space_one.third(gate)
-    small = moves.small_last(after(small, gate))
-    space_two.sum(small), space_one.sum()
+    d_frames_a, d_frames_b = both_clips(d_started, after(started_partner, small))
+    gate = space_two.third(d_frames_a, d_frames_b)
+    gate2 = space_one.third(gate)
+    gate3 = ffn.fifth(gate2)
+    token = pause(tokens, gate, gate2, gate3)
+    small = small + after(small_other, token)
+    gates = [space_two.sum(token), space_one.sum(token)]
     space = Pair(moves, space_one, space_two)
     space.fourth()
-    space.fifth()
+    small = moves.small_last(after(small, *gates))
+    gates += [time.fifth(gates[1])]
+    token = pause(tokens, *gates)
+    gate = space.fifth(token)
+    token = pause(tokens, gate)
+    ffn.arrived, time.arrived = after(ffn.arrived, gates[0]), after(time.arrived, token)
+    space.arrived = after(space.arrived, token)
+
+    small = small + sum(tokens)[:1, :1]
 
     def qkv(pair):
         return jnp.stack([pair.halves(0, 0, 2), pair.halves(0, 1, 2), pair.halves(1, 0, 2)])

time: 622 us -> 538 us (0.86)
  waiting for transfers between devices: 160 us -> 96.2 us
  other arithmetic: 60.3 us -> 51.1 us
    ppermute x59 -> x67, waiting for transfers between devices: 160 us -> 96.2 us  [swap(): lax.ppermute(value, axis, [(i, i ^ step) for i in range(sizes[axis])])]
    convert_element_type x6 -> x0, other arithmetic: 16.1 us -> none  [second(): self.leaving = (wide(self.keep[1]) + wide(self.got[1])).astype(BF)]
    pallas_call x6, Pallas kernels: 80 us -> 64 us  [grad_product(): pl.pallas_call(partial(grad_kernel, chunk, y_first, [term[0] for term in...]
    pallas_call x0 -> x9, Pallas kernels: none -> 11.5 us  [pause(): pl.pallas_call(pause_kernel, out_shape=shape_of(8, 128, dtype=F32), cost_...]
    ppermute x59 -> x67, starting transfers between devices: 68.9 us -> 61.4 us  [swap(): lax.ppermute(value, axis, [(i, i ^ step) for i in range(sizes[axis])])]
    another operation x8 -> x6, other arithmetic: 17.4 us -> 10.2 us
  transfers between devices with their start and end apart: 63 -> 71, of which waited for: 19 -> 19; matrix products, arithmetic and copies ran while one was open for 15% -> 15% of each run, Pallas kernels for 43% -> 42%
where the time goes in v3:
time: 538 us; the launch traced here: 529 us
  Pallas kernels  258 us (48%)
  waiting for transfers between devices  96.2 us (18%)
  starting transfers between devices  83.7 us (16%)
  other arithmetic  51.1 us (9%)
  local copies, waits for them, and re-layouts  36.9 us (7%)
    ppermute x67, waiting for transfers between devices, swap(): lax.ppermute(value, axis, [(i, i ^ step) for i in range(sizes[axis])])  96.2 us
    pallas_call x4, Pallas kernels, branch_back(): pl.pallas_call(partial(back_kernel, groups, segments, sums, final, len(we...  77.4 us
    pallas_call x6, Pallas kernels, grad_product(): pl.pallas_call(partial(grad_kernel, chunk, y_first, [term[0] for term in...  64 us
    ppermute x67, starting transfers between devices, swap(): lax.ppermute(value, axis, [(i, i ^ step) for i in range(sizes[axis])])  61.4 us
    pallas_call x1, Pallas kernels, feed_forward(): pl.pallas_call(ffn_kernel, grid=(8,), in_specs=[whole(rows, depth), whole...  34.6 us
    pallas_call x1, Pallas kernels, time_forward(): pl.pallas_call(partial(time_kernel, groups), grid=(4,), in_specs=[whole(r...  28.9 us
    pallas_call x2, Pallas kernels, space_heads(): pl.pallas_call(partial(space_kernel, groups, full), grid_spec=pltpu.Prefe...  23.9 us
    all_to_all x4, starting transfers between devices, exchange(): lax.all_to_all(packed, 'wide', split_axis=0, concat_axis=0, tiled=True)  22.3 us
  transfers between devices with their start and end apart: 71, of which 19 were waited for; matrix products, arithmetic and copies ran while one was open for 15% of the time, Pallas kernels for 42%

profile of v3, /device:TPU:0, one launch (start us, length us, event | category | flops | bytes accessed | tf_op | source)
XLA Modules:
  0.0 529.2 jit_solution(12025787879026772445)
XLA Ops:
  3.7 6.3 %all-to-all-start = ((bf16[8,2,40,1024]{3,2,1,0:T(8,128)(2,1)}), bf16[8,2,40,1024]{3,2,1,0:T(8,128)(2,1)S(1)}, u32[]{:S(2)}, u32[]{:S(2)}) async-start(bf16[8,2,40,1024]{3,2,1,0:T(8,128)(2,1)} %copy.83), calls=%async_computation | async-start | bytes 2621440 | tf_op jit(solution)/shard_map/all_to_all | solution.py:881
  18.9 11.8 %space_partner.1 = bf16[2,640,256]{2,1,0:T(8,128)(2,1)} custom-call(s32[1]{0:T(128)S(6)} %sub.11._, bf16[2,2,256,1024]{3,2,1,0:T(8,128)(2,1)} %fa_ref.3, bf16[2,2,64,1024]{3,2,1,0:T(8,128)(2,1)} %fb_ref.3, f32[2,4,1024]{2,1,0:T(4,128)} %fusion.23.shift_ref, f32[1,1024]{1,0:T(1,128)} %bitcast.265, bf16[3,1024,512]{2,1,0:T(8,128)(2,1)} %refs_0_.3), custom_call_target="tpu_custom_call" | custom-call | flops 1200000000 | bytes 1048576 | tf_op jit(solution)/shard_map/space_partner/pallas_call | solution.py:193
  34.3 12.1 %space_own.1 = (bf16[2,640,256]{2,1,0:T(8,128)(2,1)}, bf16[2,3,640,256]{3,2,1,0:T(8,128)(2,1)}, f32[2,8,640]{2,1,0:T(8,128)}, f32[640,1024]{1,0:T(8,128)}, bf16[640,1024]{1,0:T(8,128)(2,1)}) custom-call(s32[1]{0:T(128)} %bitcast.3._, bf16[2,2,256,1024]{3,2,1,0:T(8,128)(2,1)} %fa_ref.3, bf16[2,2,64,1024]{3,2,1,0:T(8,128)(2,1)} %fb_ref.3, ...), custom_call_target="tpu_custom_call" | custom-call | flops 1200000000 | bytes 1048576 | tf_op jit(solution)/shard_map/space_own/pallas_call | solution.py:193
  49.5 5.9 %space_mix.1 = bf16[640,1024]{1,0:T(8,128)(2,1)} custom-call(s32[3]{0:T(128)} %pad_add_fusion.1.bits_ref, f32[640,1024]{1,0:T(8,128)} %get-tuple-element.131.stream_ref.refs_0_, bf16[2,640,256]{2,1,0:T(8,128)(2,1)} %get-tuple-element.132.own_ref, bf16[2,640,256]{2,1,0:T(8,128)(2,1)} %copy-done.17, bf16[512,1024]{1,0:T(8,128)(2,1)} %refs_1_.3, ...), custom_call_target="tpu_custom_call" | custom-call | flops 1200000000 | bytes 1048576 | tf_op jit(solution)/shard_map/space_mix/pallas_call | solution.py:306
  76.2 16.7 %collective-permute-done.7.u0 = bf16[1024,512]{1,0:T(8,128)(2,1)} collective-permute-done((bf16[1024,512]{1,0:T(8,128)(2,1)}, bf16[1024,512]{1,0:T(8,128)(2,1)}, u32[]{:S(2)}, u32[]{:S(2)}) %collective-permute-start.7) | collective-permute-done | bytes 1048608 | tf_op jit(solution)/shard_map/ppermute | solution.py:713
  96.8 20.9 %collective-permute-done.8.d0 = bf16[512,1024]{1,0:T(8,128)(2,1)} collective-permute-done((bf16[512,1024]{1,0:T(8,128)(2,1)}, bf16[512,1024]{1,0:T(8,128)(2,1)}, u32[]{:S(2)}, u32[]{:S(2)}) %collective-permute-start.8) | collective-permute-done | bytes 1048608 | tf_op jit(solution)/shard_map/ppermute | solution.py:713
  122.2 28.9 %time_forward.1 = (bf16[640,1024]{1,0:T(8,128)(2,1)}, bf16[640,1024]{1,0:T(8,128)(2,1)}, bf16[4,640,256]{2,1,0:T(8,128)(2,1)}, bf16[4,3,640,256]{3,2,1,0:T(8,128)(2,1)}, f32[4,8,640]{2,1,0:T(8,128)}) custom-call(bf16[640,1024]{1,0:T(8,128)(2,1)} %bitcast.234, f32[1,1024]{1,0:T(1,128)} %bitcast.268, bf16[3,1024,512]{2,1,0:T(8,128)(2,1)} %refs_0_.2, ...), custom_call_target="tpu_custom_call" | custom-call | flops 44810600448 | bytes 1048576 | tf_op jit(solution)/shard_map/time_forward/pallas_call | solution.py:348
  154.9 34.6 %feed_forward.1 = (bf16[640,1024]{1,0:T(8,128)(2,1)}, bf16[640,1024]{1,0:T(8,128)(2,1)}, bf16[640,1024]{1,0:T(8,128)(2,1)}, bf16[8,2,640,512]{3,2,1,0:T(8,128)(2,1)}, f32[1,1024]{1,0:T(1,128)}) custom-call(bf16[640,1024]{1,0:T(8,128)(2,1)} %get-tuple-element.150.late_ref, bf16[640,1024]{1,0:T(8,128)(2,1)} %bitcast.229, f32[1,1024]{1,0:T(1,128)} %bitcast.270, ...), custom_call_target="tpu_custom_call" | custom-call | flops 4983699968 | bytes 1048576 | tf_op jit(solution)/shard_map/feed_forward/pallas_call | solution.py:459
  199.3 18.3 %time_back.1 = (f32[640,1024]{1,0:T(8,128)}, bf16[2,3,640,256]{3,2,1,0:T(8,128)(2,1)}) custom-call(bf16[640,1024]{1,0:T(8,128)(2,1)} %get-tuple-element.178.dy_ref.refs_2_, bf16[4,3,640,256]{3,2,1,0:T(8,128)(2,1)} %get-tuple-element.157.proj_any, f32[4,8,640]{2,1,0:T(8,128)} %get-tuple-element.158.logs_any, bf16[3,1024,512]{2,1,0:T(8,128)(2,1)} %refs_0_.2, ...), custom_call_target="tpu_custom_call" | custom-call | flops 11333900288 | bytes 1048576 | tf_op jit(solution)/shard_map/time_back/pallas_call | solution.py:577
  217.7 13.0 %grad_product.6 = (bf16[2,4,128,1024]{3,2,1,0:T(8,128)(2,1)}, bf16[2,4,128,1024]{3,2,1,0:T(8,128)(2,1)}) custom-call(s32[3]{0:T(128)} %pad_add_fusion.1.bits_ref, bf16[640,1024]{1,0:T(8,128)(2,1)} %get-tuple-element.160.refs_0_, bf16[640,1024]{1,0:T(8,128)(2,1)} %collective-permute-done.17.refs_1_, ...), custom_call_target="tpu_custom_call" | custom-call | flops 12840999936 | bytes 1048576 | tf_op jit(solution)/shard_map/grad_product/pallas_call | solution.py:686
  232.0 13.2 %grad_product.7 = (bf16[2,4,128,1024]{3,2,1,0:T(8,128)(2,1)}, bf16[2,4,128,1024]{3,2,1,0:T(8,128)(2,1)}) custom-call(s32[3]{0:T(128)} %pad_add_fusion.1.bits_ref, bf16[640,1024]{1,0:T(8,128)(2,1)} %bitcast.230, bf16[640,1024]{1,0:T(8,128)(2,1)} %collective-permute-done.19.refs_1_, bf16[8,2,640,512]{3,2,1,0:T(8,128)(2,1)} %get-tuple-element.161.refs_2_.refs_4_, ...), custom_call_target="tpu_custom_call" | custom-call | flops 574899968 | bytes 1048576 | tf_op jit(solution)/shard_map/grad_product/pallas_call | solution.py:686
  248.3 21.2 %time_back_end.1 = (bf16[640,1024]{1,0:T(8,128)(2,1)}, bf16[2,3,640,256]{3,2,1,0:T(8,128)(2,1)}, f32[1,1024]{1,0:T(1,128)}, f32[8,1024]{1,0:T(8,128)}) custom-call(bf16[640,1024]{1,0:T(8,128)(2,1)} %get-tuple-element.178.dy_ref.refs_2_, bf16[4,3,640,256]{3,2,1,0:T(8,128)(2,1)} %get-tuple-element.157.proj_any, f32[4,8,640]{2,1,0:T(8,128)} %get-tuple-element.158.logs_any, ...), custom_call_target="tpu_custom_call" | custom-call | flops 852000000 | bytes 1048576 | tf_op jit(solution)/shard_map/time_back_end/pallas_call | solution.py:577
  285.1 8.9 %grad_product.8 = (bf16[2,4,128,512]{3,2,1,0:T(8,128)(2,1)}, bf16[2,4,128,512]{3,2,1,0:T(8,128)(2,1)}) custom-call(s32[3]{0:T(128)} %pad_add_fusion.1.bits_ref, bf16[640,1024]{1,0:T(8,128)(2,1)} %get-tuple-element.173.refs_0_, bf16[640,1024]{1,0:T(8,128)(2,1)} %collective-permute-done.21.refs_1_, ...), custom_call_target="tpu_custom_call" | custom-call | flops 115100000 | bytes 1048576 | tf_op jit(solution)/shard_map/grad_product/pallas_call | solution.py:686
  294.5 9.9 %grad_product.9 = (bf16[2,4,128,512]{3,2,1,0:T(8,128)(2,1)}, bf16[2,4,128,512]{3,2,1,0:T(8,128)(2,1)}) custom-call(s32[3]{0:T(128)} %pad_add_fusion.1.bits_ref, bf16[640,1024]{1,0:T(8,128)(2,1)} %get-tuple-element.173.refs_0_, bf16[640,1024]{1,0:T(8,128)(2,1)} %collective-permute-done.21.refs_1_, bf16[640,1024]{1,0:T(8,128)(2,1)} %get-tuple-element.178.dy_ref.refs_2_, ...), custom_call_target="tpu_custom_call" | custom-call | flops 626899968 | bytes 1048576 | tf_op jit(solution)/shard_map/grad_product/pallas_call | solution.py:686
  315.9 12.2 %space_rest.1 = (bf16[2,640,256]{2,1,0:T(8,128)(2,1)}, bf16[2,3,640,256]{3,2,1,0:T(8,128)(2,1)}, f32[2,8,640]{2,1,0:T(8,128)}) custom-call(bf16[640,1024]{1,0:T(8,128)(2,1)} %get-tuple-element.220.normed_ref.refs_0_, bf16[3,1024,128]{2,1,0:T(8,128)(2,1)} %collective-permute-done.28.q0.refs_3_, bf16[3,1024,128]{2,1,0:T(8,128)(2,1)} %collective-permute-done.29.q1.refs_4_, ...), custom_call_target="tpu_custom_call" | custom-call | flops 998499968 | bytes 1048576 | tf_op jit(solution)/shard_map/space_rest/pallas_call | solution.py:270
  337.6 17.0 %space_back.1 = (f32[640,1024]{1,0:T(8,128)}, bf16[2,3,640,256]{3,2,1,0:T(8,128)(2,1)}) custom-call(bf16[640,1024]{1,0:T(8,128)(2,1)} %pad_maximum_fusion.2.dy_ref.refs_2_, bf16[2,3,640,256]{3,2,1,0:T(8,128)(2,1)} %get-tuple-element.197.proj_any, f32[2,8,640]{2,1,0:T(8,128)} %get-tuple-element.198.logs_any, bf16[3,1024,512]{2,1,0:T(8,128)(2,1)} %refs_0_.3, ...), custom_call_target="tpu_custom_call" | custom-call | flops 6081099776 | bytes 1048576 | tf_op jit(solution)/shard_map/space_back/pallas_call | solution.py:577
  364.6 20.8 %space_back_end.1 = (bf16[640,1024]{1,0:T(8,128)(2,1)}, bf16[2,3,640,256]{3,2,1,0:T(8,128)(2,1)}, f32[1,1024]{1,0:T(1,128)}, f32[8,1024]{1,0:T(8,128)}) custom-call(bf16[640,1024]{1,0:T(8,128)(2,1)} %pad_maximum_fusion.2.dy_ref.refs_2_, bf16[2,3,640,256]{3,2,1,0:T(8,128)(2,1)} %get-tuple-element.195.proj_any, f32[2,8,640]{2,1,0:T(8,128)} %get-tuple-element.196.logs_any, ...), custom_call_target="tpu_custom_call" | custom-call | flops 30433099776 | bytes 1048576 | tf_op jit(solution)/shard_map/space_back_end/pallas_call | solution.py:577
  390.7 9.8 %collective-permute-done.39 = bf16[4,128,512]{2,1,0:T(8,128)(2,1)} collective-permute-done((bf16[4,128,512]{2,1,0:T(8,128)(2,1)}, bf16[4,128,512]{2,1,0:T(8,128)(2,1)}, u32[]{:S(2)}, u32[]{:S(2)}) %collective-permute-start.39) | collective-permute-done | bytes 524320 | tf_op jit(solution)/shard_map/ppermute | solution.py:713
  409.1 9.9 %grad_product.10 = (bf16[2,4,128,512]{3,2,1,0:T(8,128)(2,1)}, bf16[2,4,128,512]{3,2,1,0:T(8,128)(2,1)}) custom-call(s32[3]{0:T(128)} %pad_add_fusion.1.bits_ref, bf16[640,1024]{1,0:T(8,128)(2,1)} %get-tuple-element.220.normed_ref.refs_0_, bf16[640,1024]{1,0:T(8,128)(2,1)} %collective-permute-done.40.refs_1_, ...), custom_call_target="tpu_custom_call" | custom-call | flops 351700000 | bytes 1048576 | tf_op jit(solution)/shard_map/grad_product/pallas_call | solution.py:686
  421.2 9.1 %grad_product.11 = (bf16[2,4,128,512]{3,2,1,0:T(8,128)(2,1)}, bf16[2,4,128,512]{3,2,1,0:T(8,128)(2,1)}) custom-call(s32[3]{0:T(128)} %pad_add_fusion.1.bits_ref, bf16[640,1024]{1,0:T(8,128)(2,1)} %get-tuple-element.220.normed_ref.refs_0_, bf16[640,1024]{1,0:T(8,128)(2,1)} %collective-permute-done.40.refs_1_, ...), custom_call_target="tpu_custom_call" | custom-call | flops 1624000000 | bytes 1048576 | tf_op jit(solution)/shard_map/grad_product/pallas_call | solution.py:686
  438.8 5.9 %collective-permute-done.48 = bf16[2,4,128,512]{3,2,1,0:T(8,128)(2,1)S(1)} collective-permute-done((bf16[2,4,128,512]{3,2,1,0:T(8,128)(2,1)}, bf16[2,4,128,512]{3,2,1,0:T(8,128)(2,1)S(1)}, u32[]{:S(2)}, u32[]{:S(2)}) %collective-permute-start.48) | collective-permute-done | bytes 1048608 | tf_op jit(solution)/shard_map/ppermute | solution.py:713
  447.7 9.3 %collective-permute-done.49 = bf16[2,4,128,512]{3,2,1,0:T(8,128)(2,1)S(1)} collective-permute-done((bf16[2,4,128,512]{3,2,1,0:T(8,128)(2,1)}, bf16[2,4,128,512]{3,2,1,0:T(8,128)(2,1)S(1)}, u32[]{:S(2)}, u32[]{:S(2)}) %collective-permute-start.49) | collective-permute-done | bytes 1048608 | tf_op jit(solution)/shard_map/ppermute | solution.py:713
  471.8 8.1 %collective-permute-done.54 = bf16[4,128,512]{2,1,0:T(8,128)(2,1)S(1)} collective-permute-done((bf16[4,128,512]{2,1,0:T(8,128)(2,1)S(1)}, bf16[4,128,512]{2,1,0:T(8,128)(2,1)S(1)}, u32[]{:S(2)}, u32[]{:S(2)}) %collective-permute-start.54) | collective-permute-done | bytes 524320 | tf_op jit(solution)/shard_map/ppermute | solution.py:713
  503.4 8.2 %collective-permute-start.56 = (f32[11,128]{1,0:T(8,128)}, f32[11,128]{1,0:T(8,128)}, u32[]{:S(2)}, u32[]{:S(2)}) collective-permute-start(f32[11,128]{1,0:T(8,128)} %bitcast.227), channel_id=1, source_target_pairs={{0,8},{2,10},{4,12},{6,14},{8,0},{10,2},{12,4},{14,6},{1,9},{3,11}... | collective-permute-start | bytes 16904 | tf_op jit(solution)/shard_map/ppermute | solution.py:713
  (323 shorter events, 195.1 us)
Async XLA Ops:
  3.7 54.2 %all-to-all-start = ((bf16[8,2,40,1024]{3,2,1,0:T(8,128)(2,1)}), bf16[8,2,40,1024]{3,2,1,0:T(8,128)(2,1)S(1)}, u32[]{:S(2)}, u32[]{:S(2)}) async-start(bf16[8,2,40,1024]{3,2,1,0:T(8,128)(2,1)} %copy.83), calls=%async_computation | async-start | bytes 2621440 | tf_op jit(solution)/shard_map/all_to_all | solution.py:881
  31.3 39.8 %collective-permute-start.5 = (bf16[4,1024,128]{2,1,0:T(8,128)(2,1)}, bf16[4,1024,128]{2,1,0:T(8,128)(2,1)}, u32[]{:S(2)}, u32[]{:S(2)}) collective-permute-start(bf16[4,1024,128]{2,1,0:T(8,128)(2,1)} %pad_maximum_fusion.3), channel_id=1, source_target_pairs={{0,1},{1,0},{2,3},{3,2},{4,5},{5,4},{6,7},{7,6},{8,9},{9,8},{10,11... | collective-permute-start | bytes 3145736 | tf_op jit(solution)/shard_map/ppermute | solution.py:713
  57.9 61.6 %all-to-all-start.1 = ((bf16[8,2,40,1024]{3,2,1,0:T(8,128)(2,1)}), bf16[8,2,40,1024]{3,2,1,0:T(8,128)(2,1)S(1)}, u32[]{:S(2)}, u32[]{:S(2)}) async-start(bf16[8,2,40,1024]{3,2,1,0:T(8,128)(2,1)} %copy_bitcast_fusion), calls=%async_computation.1 | async-start | bytes 2621440 | tf_op jit(solution)/shard_map/all_to_all | solution.py:881
  96.5 56.1 %collective-permute-start.12 = (bf16[1024,512]{1,0:T(8,128)(2,1)}, bf16[1024,512]{1,0:T(8,128)(2,1)}, u32[]{:S(2)}, u32[]{:S(2)}) collective-permute-start(bf16[1024,512]{1,0:T(8,128)(2,1)} %collective-permute-done.7.u0), channel_id=1, source_target_pairs={{0,2},{2,0},{4,6},{6,4},{8,10},{10,8},{12,14},{14,12},{1,3},{3,1},... | collective-permute-start | bytes 3145736 | tf_op jit(solution)/shard_map/ppermute | solution.py:713
  117.7 34.9 %collective-permute-start.14 = (bf16[512,1024]{1,0:T(8,128)(2,1)}, bf16[512,1024]{1,0:T(8,128)(2,1)}, u32[]{:S(2)}, u32[]{:S(2)}) collective-permute-start(bf16[512,1024]{1,0:T(8,128)(2,1)} %collective-permute-done.8.d0), channel_id=1, source_target_pairs={{0,2},{2,0},{4,6},{6,4},{8,10},{10,8},{12,14},{14,12},{1,3},{3,1},... | collective-permute-start | bytes 3145736 | tf_op jit(solution)/shard_map/ppermute | solution.py:713
  191.2 40.2 %collective-permute-start.28 = (bf16[3,1024,128]{2,1,0:T(8,128)(2,1)S(1)}, bf16[3,1024,128]{2,1,0:T(8,128)(2,1)}, u32[]{:S(2)}, u32[]{:S(2)}) collective-permute-start(bf16[3,1024,128]{2,1,0:T(8,128)(2,1)S(1)} %constant_dynamic-slice_fusion.7), channel_id=1, source_target_pairs={{0,1},{1,0},{2,3},{3,2},{4,5},{5,4},{6,7},{7,6},{8,9},{9,8},{10,11... | collective-permute-start | bytes 2359304 | tf_op jit(solution)/shard_map/ppermute | solution.py:713
  192.6 39.3 %collective-permute-start.19 = (bf16[640,1024]{1,0:T(8,128)(2,1)S(1)}, bf16[640,1024]{1,0:T(8,128)(2,1)}, u32[]{:S(2)}, u32[]{:S(2)}) collective-permute-start(bf16[640,1024]{1,0:T(8,128)(2,1)S(1)} %bitcast.231), channel_id=1, source_target_pairs={{0,2},{2,0},{4,6},{6,4},{8,10},{10,8},{12,14},{14,12},{1,3},{3,1},... | collective-permute-start | bytes 3932168 | tf_op jit(solution)/shard_map/ppermute | solution.py:713
  192.7 76.9 %collective-permute-start.21 = (bf16[640,1024]{1,0:T(8,128)(2,1)}, bf16[640,1024]{1,0:T(8,128)(2,1)}, u32[]{:S(2)}, u32[]{:S(2)}) collective-permute-start(bf16[640,1024]{1,0:T(8,128)(2,1)} %get-tuple-element.173.refs_0_), channel_id=1, source_target_pairs={{0,2},{2,0},{4,6},{6,4},{8,10},{10,8},{12,14},{14,12},{1,3},{3,1},... | collective-permute-start | bytes 3932168 | tf_op jit(solution)/shard_map/ppermute | solution.py:713
  194.4 50.8 %all-to-all-start.2 = ((bf16[8,2,40,1024]{3,2,1,0:T(8,128)(2,1)}), bf16[8,2,40,1024]{3,2,1,0:T(8,128)(2,1)S(1)}, u32[]{:S(2)}, u32[]{:S(2)}) async-start(bf16[8,2,40,1024]{3,2,1,0:T(8,128)(2,1)} %bitcast.239), calls=%async_computation.2 | async-start | bytes 2621440 | tf_op jit(solution)/shard_map/all_to_all | solution.py:881
  230.7 48.4 %collective-permute-start.22 = (bf16[2,4,128,1024]{3,2,1,0:T(8,128)(2,1)}, bf16[2,4,128,1024]{3,2,1,0:T(8,128)(2,1)}, u32[]{:S(2)}, u32[]{:S(2)}) collective-permute-start(bf16[2,4,128,1024]{3,2,1,0:T(8,128)(2,1)} %get-tuple-element.172), channel_id=1, source_target_pairs={{0,1},{1,0},{2,3},{3,2},{4,5},{5,4},{6,7},{7,6},{8,9},{9,8},{10,11... | collective-permute-start | bytes 6291464 | tf_op jit(solution)/shard_map/ppermute | solution.py:713
  231.2 38.9 %collective-permute-start.25 = (bf16[640,1024]{1,0:T(8,128)(2,1)}, bf16[640,1024]{1,0:T(8,128)(2,1)}, u32[]{:S(2)}, u32[]{:S(2)}) collective-permute-start(bf16[640,1024]{1,0:T(8,128)(2,1)} %get-tuple-element.178.dy_ref.refs_2_), channel_id=1, source_target_pairs={{0,2},{2,0},{4,6},{6,4},{8,10},{10,8},{12,14},{14,12},{1,3},{3,1},... | collective-permute-start | bytes 3932168 | tf_op jit(solution)/shard_map/ppermute | solution.py:713
  231.5 38.2 %collective-permute-start.30 = (bf16[3,1024,128]{2,1,0:T(8,128)(2,1)}, bf16[3,1024,128]{2,1,0:T(8,128)(2,1)}, u32[]{:S(2)}, u32[]{:S(2)}) collective-permute-start(bf16[3,1024,128]{2,1,0:T(8,128)(2,1)} %collective-permute-done.28.q0.refs_3_), channel_id=1, source_target_pairs={{0,16},{16,0},{1,17},{17,1},{2,18},{18,2},{3,19},{19,3},{4,20},{20... | collective-permute-start | bytes 2359304 | tf_op jit(solution)/shard_map/ppermute | solution.py:713
  245.4 59.0 %collective-permute-start.27 = (bf16[2,4,128,1024]{3,2,1,0:T(8,128)(2,1)}, bf16[2,4,128,1024]{3,2,1,0:T(8,128)(2,1)}, u32[]{:S(2)}, u32[]{:S(2)}) collective-permute-start(bf16[2,4,128,1024]{3,2,1,0:T(8,128)(2,1)} %get-tuple-element.183), channel_id=1, source_target_pairs={{0,16},{16,0},{1,17},{17,1},{2,18},{18,2},{3,19},{19,3},{4,20},{20... | collective-permute-start | bytes 6291464 | tf_op jit(solution)/shard_map/ppermute | solution.py:713
  272.7 63.4 %all-to-all-start.3 = ((bf16[8,2,40,1024]{3,2,1,0:T(8,128)(2,1)}), bf16[8,2,40,1024]{3,2,1,0:T(8,128)(2,1)S(1)}, u32[]{:S(2)}, u32[]{:S(2)}) async-start(bf16[8,2,40,1024]{3,2,1,0:T(8,128)(2,1)} %bitcast.237), calls=%async_computation.3 | async-start | bytes 2621440 | tf_op jit(solution)/shard_map/all_to_all | solution.py:881
  294.0 66.6 %collective-permute-start.33 = (bf16[4,128,1024]{2,1,0:T(8,128)(2,1)}, bf16[4,128,1024]{2,1,0:T(8,128)(2,1)}, u32[]{:S(2)}, u32[]{:S(2)}) collective-permute-start(bf16[4,128,1024]{2,1,0:T(8,128)(2,1)} %get-tuple-element.309), channel_id=1, source_target_pairs={{0,16},{16,0},{1,17},{17,1},{2,18},{18,2},{3,19},{19,3},{4,20},{20... | collective-permute-start | bytes 3145736 | tf_op jit(solution)/shard_map/ppermute | solution.py:713
  311.0 43.7 %collective-permute-start.34 = (bf16[4,128,1024]{2,1,0:T(8,128)(2,1)}, bf16[4,128,1024]{2,1,0:T(8,128)(2,1)}, u32[]{:S(2)}, u32[]{:S(2)}) collective-permute-start(bf16[4,128,1024]{2,1,0:T(8,128)(2,1)} %get-tuple-element.307), channel_id=1, source_target_pairs={{0,1},{1,0},{2,3},{3,2},{4,5},{5,4},{6,7},{7,6},{8,9},{9,8},{10,11... | collective-permute-start | bytes 3145736 | tf_op jit(solution)/shard_map/ppermute | solution.py:713
  329.5 56.3 %collective-permute-start.43 = (bf16[2,1,640,256]{3,2,1,0:T(8,128)(2,1)}, bf16[2,1,640,256]{3,2,1,0:T(8,128)(2,1)}, u32[]{:S(2)}, u32[]{:S(2)}) collective-permute-start(bf16[2,1,640,256]{3,2,1,0:T(8,128)(2,1)} %bitcast.56.refs_6_), channel_id=1, source_target_pairs={{0,2},{2,0},{4,6},{6,4},{8,10},{10,8},{12,14},{14,12},{1,3},{3,1},... | collective-permute-start | bytes 1966088 | tf_op jit(solution)/shard_map/ppermute | solution.py:713
  333.5 52.5 %collective-permute-start.45 = (bf16[2,1,640,256]{3,2,1,0:T(8,128)(2,1)}, bf16[2,1,640,256]{3,2,1,0:T(8,128)(2,1)}, u32[]{:S(2)}, u32[]{:S(2)}) collective-permute-start(bf16[2,1,640,256]{3,2,1,0:T(8,128)(2,1)} %bitcast.259), channel_id=1, source_target_pairs={{0,2},{2,0},{4,6},{6,4},{8,10},{10,8},{12,14},{14,12},{1,3},{3,1},... | collective-permute-start | bytes 1966088 | tf_op jit(solution)/shard_map/ppermute | solution.py:713
  364.4 44.6 %collective-permute-start.42 = (bf16[2,3,640,256]{3,2,1,0:T(8,128)(2,1)}, bf16[2,3,640,256]{3,2,1,0:T(8,128)(2,1)}, u32[]{:S(2)}, u32[]{:S(2)}) collective-permute-start(bf16[2,3,640,256]{3,2,1,0:T(8,128)(2,1)} %get-tuple-element.215.refs_4_.refs_2_), channel_id=1, source_target_pairs={{0,2},{2,0},{4,6},{6,4},{8,10},{10,8},{12,14},{14,12},{1,3},{3,1},... | collective-permute-start | bytes 5898248 | tf_op jit(solution)/shard_map/ppermute | solution.py:713
  405.5 54.2 %collective-permute-start.52 = (bf16[2,128,1024]{2,1,0:T(8,128)(2,1)}, bf16[2,128,1024]{2,1,0:T(8,128)(2,1)}, u32[]{:S(2)}, u32[]{:S(2)}) collective-permute-start(bf16[2,128,1024]{2,1,0:T(8,128)(2,1)} %get-tuple-element.304), channel_id=1, source_target_pairs={{0,12},{2,14},{4,8},{6,10},{8,4},{10,6},{12,0},{14,2},{1,13},{3,15... | collective-permute-start | bytes 1572872 | tf_op jit(solution)/shard_map/ppermute | solution.py:713
  409.0 57.7 %collective-permute-start.51 = (bf16[2,128,1024]{2,1,0:T(8,128)(2,1)}, bf16[2,128,1024]{2,1,0:T(8,128)(2,1)}, u32[]{:S(2)}, u32[]{:S(2)}) collective-permute-start(bf16[2,128,1024]{2,1,0:T(8,128)(2,1)} %get-tuple-element.305), channel_id=1, source_target_pairs={{0,8},{2,10},{4,12},{6,14},{8,0},{10,2},{12,4},{14,6},{1,9},{3,11}... | collective-permute-start | bytes 1572872 | tf_op jit(solution)/shard_map/ppermute | solution.py:713
  431.6 35.6 %collective-permute-start.50 = (bf16[2,128,1024]{2,1,0:T(8,128)(2,1)}, bf16[2,128,1024]{2,1,0:T(8,128)(2,1)S(1)}, u32[]{:S(2)}, u32[]{:S(2)}) collective-permute-start(bf16[2,128,1024]{2,1,0:T(8,128)(2,1)} %get-tuple-element.303), channel_id=1, source_target_pairs={{0,4},{2,6},{4,0},{6,2},{8,12},{10,14},{12,8},{14,10},{1,5},{3,7},... | collective-permute-start | bytes 1572872 | tf_op jit(solution)/shard_map/ppermute | solution.py:713
  444.7 38.9 %collective-permute-start.60 = (bf16[2,128,512]{2,1,0:T(8,128)(2,1)}, bf16[2,128,512]{2,1,0:T(8,128)(2,1)}, u32[]{:S(2)}, u32[]{:S(2)}) collective-permute-start(bf16[2,128,512]{2,1,0:T(8,128)(2,1)} %get-tuple-element.316), channel_id=1, source_target_pairs={{0,12},{2,14},{4,8},{6,10},{8,4},{10,6},{12,0},{14,2},{1,13},{3,15... | collective-permute-start | bytes 786440 | tf_op jit(solution)/shard_map/ppermute | solution.py:713
  487.6 34.8 %collective-permute-start.57 = (f32[11,128]{1,0:T(8,128)}, f32[11,128]{1,0:T(8,128)}, u32[]{:S(2)}, u32[]{:S(2)}) collective-permute-start(f32[11,128]{1,0:T(8,128)} %bitcast.226), channel_id=1, source_target_pairs={{0,12},{2,14},{4,8},{6,10},{8,4},{10,6},{12,0},{14,2},{1,13},{3,15... | collective-permute-start | bytes 16904 | tf_op jit(solution)/shard_map/ppermute | solution.py:713
  (90 other events, 1293.5 us)

commit v4 on v3

--- a/solution.py
+++ b/solution.py
@@ -10,6 +10,7 @@
 HEAD = 64
 PAIR = 2 * HEAD
 BLOCK = 2 * PAIR
+BATCH = 2**30
 BF = jnp.bfloat16
 F32 = jnp.float32
 LIMIT = 60 * 2**20
@@ -39,7 +40,7 @@
     return pltpu.CompilerParams(vmem_limit_bytes=LIMIT)
 
 
-MICROS = {'space_partner': 1.2, 'space_own': 1.2, 'space_mix': 1.2, 'space_rest': 0.9985, 'time_forward': 44.8106, 'feed_forward': 4.9837, 'time_back': 11.3339, 'time_back_end': 0.852, 'space_back': 6.0811, 'space_back_end': 30.4331, 'grad_up': 12.841, 'grad_down': 0.5749, 'time_one': 0.1151, 'time_two': 0.6269, 'space_two': 0.3517, 'space_one': 1.624, 'pause0': 1.2, 'pause1': 1.2, 'pause2': 1.2, 'pause3': 1.2, 'pause4': 5.9164, 'pause5': 3.5109, 'pause6': 2.6464, 'pause7': 12.3069, 'pause8': 160.0718, 'pause9': 0.8432}
+MICROS = {'space_partner': 8, 'space_own': 8, 'space_mix': 8, 'space_rest': 1.031, 'time_forward': 44.8106, 'feed_forward': 15.1219, 'time_back': 11.3339, 'time_back_end': 0.852, 'space_back': 6.0811, 'space_back_end': 30.4331, 'grad_up': 12.841, 'grad_down': 0.5749, 'time_one': 0.1151, 'time_two': 0.6269, 'space_two': 0.3517, 'space_one': 1.624, 'pause0': 1, 'pause1': 0.02, 'pause2': 12, 'pause3': 5.3533, 'pause4': 12, 'pause5': 5.9164, 'pause6': 3.5109, 'pause7': 2.6464, 'pause8': 12.3069, 'pause9': 160.0718, 'pause10': 0.8432, 'feed_forward_end': 15.1219}
 
 
 def cost(name):
@@ -67,28 +68,47 @@
     )
 
 
+def batches(groups):
+    result, area = [], 0
+    for group in groups:
+        size = group[1] * group[1]
+        if result and area + size <= BATCH:
+            result[-1].append(group)
+            area += size
+        else:
+            result.append([group])
+            area = size
+    return result
+
+
 def attend_block(groups, proj_ref, heads_ref, logs_ref):
     scaled = head_masks(HEAD**-0.5)
     masks = {kind: group_mask(kind, length) for _, length, kind in groups}
-    for pair in range(2):
-        cols = slice(pair * PAIR, (pair + 1) * PAIR)
-        for start, length, kind in groups:
-            rows = slice(start, start + length)
-            query, key, value = (proj_ref[i, rows, cols] for i in range(3))
-            value_t = value.T
-            outs = []
-            for h in range(2):
-                scores = dot_t(key * scaled[h], query)
-                if kind is not None:
-                    scores = jnp.where(masks[kind], scores, -1e30)
-                largest = jnp.max(scores, 0, keepdims=True)
-                shifted = jnp.exp(scores - largest)
-                total = jnp.sum(shifted, 0, keepdims=True)
-                out = dot_n(value_t[h * HEAD : (h + 1) * HEAD], shifted.astype(BF))
-                outs.append(out * (1.0 / total))
+    for batch in batches([(*group, pair) for pair in range(2) for group in groups]):
+        if True:
+            places = [slice(start, start + length) for start, length, _, _ in batch]
+            spots = [slice(group[3] * PAIR, (group[3] + 1) * PAIR) for group in batch]
+            items = [(g, h) for g in range(len(batch)) for h in range(2)]
+            scores = [
+                dot_t(proj_ref[1, places[g], spots[g]] * scaled[h], proj_ref[0, places[g], spots[g]]) for g, h in items
+            ]
+            scores = [
+                scores[n] if batch[g][2] is None else jnp.where(masks[batch[g][2]], scores[n], -1e30)
+                for n, (g, h) in enumerate(items)
+            ]
+            largest = [jnp.max(v, 0, keepdims=True) for v in scores]
+            shifted = [jnp.exp(v - m) for v, m in zip(scores, largest)]
+            totals = [jnp.sum(v, 0, keepdims=True) for v in shifted]
+            values_t = [proj_ref[2, rows, cols].T for rows, cols in zip(places, spots)]
+            outs = [
+                dot_n(values_t[g][h * HEAD : (h + 1) * HEAD], shifted[n].astype(BF)) * (1.0 / totals[n])
+                for n, (g, h) in enumerate(items)
+            ]
+            for n, (g, h) in enumerate(items):
                 if logs_ref is not None:
-                    logs_ref[2 * pair + h : 2 * pair + h + 1, rows] = largest + jnp.log(total)
-            heads_ref[rows, cols] = jnp.concatenate(outs, 0).T.astype(BF)
+                    logs_ref[2 * batch[g][3] + h : 2 * batch[g][3] + h + 1, places[g]] = largest[n] + jnp.log(totals[n])
+            for g, (rows, cols) in enumerate(zip(places, spots)):
+                heads_ref[rows, cols] = jnp.concatenate(outs[2 * g : 2 * g + 2], 0).T.astype(BF)
 
 
 def attend_back_block(groups, proj_ref, d_ref, logs_ref, o_ref):
@@ -96,32 +116,36 @@
     scaled = head_masks(scale)
     parts = head_masks(1.0)
     masks = {kind: group_mask(kind, length) for _, length, kind in groups}
-    for pair in range(2):
-        cols = slice(pair * PAIR, (pair + 1) * PAIR)
-        for start, length, kind in groups:
-            rows = slice(start, start + length)
-            query, key, value = (proj_ref[i, rows, cols] for i in range(3))
-            d_out = d_ref[rows, cols]
-            key_t = key.T
-            d_key = d_value = None
-            d_query = []
-            for h in range(2):
-                soft = jnp.exp(
-                    dot_t(key * scaled[h], query) - logs_ref[2 * pair + h : 2 * pair + h + 1, rows]
-                )
-                if kind is not None:
-                    soft = jnp.where(masks[kind], soft, 0.0)
-                d_soft = dot_t(value * parts[h], d_out)
-                row_dot = jnp.sum(soft * d_soft, 0, keepdims=True)
-                d_scores = (soft * (d_soft - row_dot)).astype(BF)
-                key_term = dot_n(d_scores, query * parts[h])
-                value_term = dot_n(soft.astype(BF), d_out * parts[h])
-                d_key = key_term if h == 0 else d_key + key_term
-                d_value = value_term if h == 0 else d_value + value_term
-                d_query.append(dot_n(key_t[h * HEAD : (h + 1) * HEAD], d_scores))
-            o_ref[0, rows, cols] = (jnp.concatenate(d_query, 0).T * scale).astype(BF)
-            o_ref[1, rows, cols] = (d_key * scale).astype(BF)
-            o_ref[2, rows, cols] = d_value.astype(BF)
+    for batch in batches([(*group, pair) for pair in range(2) for group in groups]):
+        if True:
+            places = [slice(start, start + length) for start, length, _, _ in batch]
+            spots = [slice(group[3] * PAIR, (group[3] + 1) * PAIR) for group in batch]
+            items = [(g, h) for g in range(len(batch)) for h in range(2)]
+            scores = [
+                dot_t(proj_ref[1, places[g], spots[g]] * scaled[h], proj_ref[0, places[g], spots[g]]) for g, h in items
+            ]
+            d_soft = [dot_t(proj_ref[2, places[g], spots[g]] * parts[h], d_ref[places[g], spots[g]]) for g, h in items]
+            soft = [
+                jnp.exp(scores[n] - logs_ref[2 * batch[g][3] + h : 2 * batch[g][3] + h + 1, places[g]])
+                for n, (g, h) in enumerate(items)
+            ]
+            soft = [
+                soft[n] if batch[g][2] is None else jnp.where(masks[batch[g][2]], soft[n], 0.0)
+                for n, (g, h) in enumerate(items)
+            ]
+            row_dots = [jnp.sum(p * d, 0, keepdims=True) for p, d in zip(soft, d_soft)]
+            d_scores = [(p * (d - r)).astype(BF) for p, d, r in zip(soft, d_soft, row_dots)]
+            soft = [p.astype(BF) for p in soft]
+            keys_t = [proj_ref[1, rows, cols].T for rows, cols in zip(places, spots)]
+            d_query = [
+                dot_n(keys_t[g][h * HEAD : (h + 1) * HEAD], d_scores[n]) for n, (g, h) in enumerate(items)
+            ]
+            d_key = [dot_n(d_scores[n], proj_ref[0, places[g], spots[g]] * parts[h]) for n, (g, h) in enumerate(items)]
+            d_value = [dot_n(soft[n], d_ref[places[g], spots[g]] * parts[h]) for n, (g, h) in enumerate(items)]
+            for g, (rows, cols) in enumerate(zip(places, spots)):
+                o_ref[0, rows, cols] = (jnp.concatenate(d_query[2 * g : 2 * g + 2], 0).T * scale).astype(BF)
+                o_ref[1, rows, cols] = ((d_key[2 * g] + d_key[2 * g + 1]) * scale).astype(BF)
+                o_ref[2, rows, cols] = (d_value[2 * g] + d_value[2 * g + 1]).astype(BF)
 
 
 def row_chunks(rows, size=64):
@@ -392,15 +416,23 @@
     return (scaled - mean_first - normal * mean_second) * inverse, d_normed * normal
 
 
-def ffn_kernel(late_ref, cot_ref, gain_ref, up_any, down_any, u0, u1, u2, u3, d0, d1, d2, d3,
-               out_ref, d_late_ref, normed_ref, hidden_ref, d_gain_ref, total, d_normed, wu, wd, sems):
+def ffn_kernel(final, late_ref, cot_ref, gain_ref, *refs):
+    if final:
+        normed_ref, total_in, d_normed_in, u0, u1, u2, u3, d0, d1, d2, d3 = refs[:11]
+        out_ref, d_late_ref, hidden_ref, d_gain_ref, total, d_normed, wu, wd, sems = refs[11:]
+    else:
+        up_any, down_any, normed_ref, hidden_ref, total, d_normed, wu, wd, sems = refs
     step = pl.program_id(0)
-    rows, depth = late_ref.shape
+    rows = late_ref.shape[0]
     width = wu.shape[2]
-    steps = 8
+    steps = 4
 
     @pl.when(step == 0)
     def _():
+        if final:
+            total[...] = total_in[...]
+            d_normed[...] = d_normed_in[...]
+            return
         gain = gain_ref[...]
         for chunk in row_chunks(rows):
             values = late_ref[chunk, :].astype(F32)
@@ -414,8 +446,8 @@
             @pl.when(index == s)
             def _(s=s):
                 cols = pl.ds(s * width, width)
-                up = up_any.at[:, cols] if s < 4 else (u0, u1, u2, u3)[s - 4]
-                down = down_any.at[cols, :] if s < 4 else (d0, d1, d2, d3)[s - 4]
+                up = (u0, u1, u2, u3)[s] if final else up_any.at[:, cols]
+                down = (d0, d1, d2, d3)[s] if final else down_any.at[cols, :]
                 pltpu.make_async_copy(up, wu.at[slot], sems.at[slot, 0]).start()
                 pltpu.make_async_copy(down, wd.at[slot], sems.at[slot, 1]).start()
 
@@ -440,6 +472,9 @@
         total[chunk, :] += dot_n(gelu, wd[slot])
         d_normed[chunk, :] += dot_t(d_hidden, wu[slot])
 
+    if not final:
+        return
+
     @pl.when(step == steps - 1)
     def _():
         gain = gain_ref[...]
@@ -452,33 +487,36 @@
         d_gain_ref[...] = d_gain
 
 
-def feed_forward(latest, cot, gain, up, down, up_slots, down_slots):
+def feed_forward(latest, cot, gain, weights, width, tail=None):
     rows, depth = latest.shape
-    width = up.shape[1] // 4
-    stream = pl.BlockSpec((1, 2, rows, width), lambda s: (s, 0, 0, 0))
+    stream = (pl.BlockSpec((1, 2, rows, width), lambda s: (s, 0, 0, 0)), shape_of(4, 2, rows, width))
+    plain = (whole(rows, depth), shape_of(rows, depth))
+    sums = (whole(rows, depth), shape_of(rows, depth, dtype=F32))
+    final = tail is not None
+    if final:
+        outs = [plain, plain, stream, (whole(1, depth), shape_of(1, depth, dtype=F32))]
+        scratch = [pltpu.VMEM((rows, depth), F32)] * 2
+    else:
+        outs = [plain, stream, sums, sums]
+        scratch = []
     return pl.pallas_call(
-        ffn_kernel,
-        grid=(8,),
-        in_specs=[whole(rows, depth), whole(rows, depth), whole(1, depth)] + [any_spec()] * 10,
-        out_specs=[whole(rows, depth), whole(rows, depth), whole(rows, depth), stream, whole(1, depth)],
-        out_shape=[
-            shape_of(rows, depth),
-            shape_of(rows, depth),
-            shape_of(rows, depth),
-            shape_of(8, 2, rows, width),
-            shape_of(1, depth, dtype=F32),
-        ],
-        scratch_shapes=[
-            pltpu.VMEM((rows, depth), F32),
-            pltpu.VMEM((rows, depth), F32),
+        partial(ffn_kernel, final),
+        grid=(4,),
+        in_specs=[whole(rows, depth), whole(rows, depth), whole(1, depth)]
+        + [whole(rows, depth)] * (3 if final else 0)
+        + [any_spec()] * len(weights),
+        out_specs=[o[0] for o in outs],
+        out_shape=[o[1] for o in outs],
+        scratch_shapes=scratch
+        + [
             pltpu.VMEM((2, depth, width), BF),
             pltpu.VMEM((2, width, depth), BF),
             pltpu.SemaphoreType.DMA((2, 2)),
         ],
         compiler_params=params(),
-        cost_estimate=cost("feed_forward"),
-        name="feed_forward",
-    )(latest, cot, gain, up, down, *up_slots, *down_slots)
+        cost_estimate=cost("feed_forward_end" if final else "feed_forward"),
+        name="feed_forward_end" if final else "feed_forward",
+    )(latest, cot, gain, *(tail or ()), *weights)
 
 
 def back_kernel(groups, segments, sums, final, packed, offset, dy_ref, proj_any, logs_any, *refs):
@@ -942,7 +980,7 @@
     out_piece = moves.quarter(time_out, 0)
     out_piece = out_piece.reshape(PAIR, -1, PAIR).transpose(1, 0, 2).reshape(1, -1, PAIR)
     time_piece = jnp.concatenate([moves.quarter(time_qkv, 2), out_piece])
-    cot_packed = pack_grid(pick(cot_a), pick(cot_b))
+    cot_packed = pack_grid(after(pick(cot_a), so_piece, time_piece), pick(cot_b))
     so_x = swap(so_piece, "tp", sizes)
     time_x = swap(time_piece, "tp", sizes)
     cot_moved = exchange(cot_packed)
@@ -962,7 +1000,8 @@
     up_piece = moves.quarter(ffn_up, 1)
     down_piece = moves.quarter(ffn_down, 0)
     up_x = swap(after(up_piece, heads_other), "tp", sizes)
-    middle = space_mix(moves.bits, started, heads_own, heads_other, space_out, so_slots)
+    token = pause(tokens, heads_other, up_piece, down_piece)
+    middle = space_mix(moves.bits, after(started, token), heads_own, heads_other, space_out, so_slots)
     packed = pack_grid(middle[:rows_a], middle[rows_a:])
     middle_moved = exchange(after(packed, cot_moved))
     time_x = after(time_x, packed)
@@ -983,23 +1022,24 @@
     sq_x = swap(after(moves.quarter(space_qkv, 2), down_x), "tp", sizes)
     token = pause(tokens, time_y, down_x)
     middle = unpack_grid(after(middle_moved, token))
-    up_y = after(up_y, token)
-    up_y_core = cores(up_y)
     latest, normed_time, heads_time, proj_time, logs_time = time_forward(
-        after(middle, up_y), gain_time, time_qkv, time_out, time_slots, time_groups
-    )
-    down_y = after(down_y, latest)
-    up_slots = (up_x, up_x_core, up_y, up_y_core)
+        middle, gain_time, time_qkv, time_out, time_slots, time_groups
+    )
+    cot = unpack_grid(after(cot_moved, latest))
+    width = ffn_up.shape[1] // 4
+    normed_ffn, hidden_own, total_ffn, d_sum_ffn = feed_forward(latest, cot, gain_ffn, (ffn_up, ffn_down), width)
+    up_y, down_y = after(up_y, hidden_own), after(down_y, hidden_own)
+    up_slots = (up_x, up_x_core, up_y, cores(up_y))
     down_slots = (down_x, down_x_core, down_y, cores(down_y))
-    cot = unpack_grid(after(cot_moved, latest))
-    out, d_latest, normed_ffn, hidden, d_gain_ffn = feed_forward(
-        latest, cot, gain_ffn, ffn_up, ffn_down, up_slots, down_slots
+    out, d_latest, hidden_rest, d_gain_ffn = feed_forward(
+        latest, cot, gain_ffn, (*up_slots, *down_slots), width, (normed_ffn, total_ffn, d_sum_ffn)
     )
 
     out_packed = pack_frames(out)
     out_moved = exchange(out_packed)
     normed_time2, heads_time2 = both(normed_time, latest), both(heads_time[:, None], latest)
-    cot2, normed_ffn2, hidden2 = both(cot, latest), both(normed_ffn), both(hidden)
+    cot2, normed_ffn2, hidden2 = both(cot, latest), both(normed_ffn, latest), both(hidden_own)
+    hidden_rest2 = both(hidden_rest)
     partial_time, d_proj_own = branch_back(
         "time_back", after(d_latest, out_packed), proj_time, logs_time, 0,
         (time_qkv, time_out), time_groups,
@@ -1011,13 +1051,13 @@
     chunk = ffn_up.shape[1] // 4
     up = product(
         [(after(normed_ffn2[0], partial_time), normed_ffn2[1])],
-        [(0, (hidden2, 0), (hidden2, 1), 1, 1)], chunk, False, "grad_up",
+        [(0, (hidden2, 0), (hidden_rest2, 0), 1, 1)], chunk, False, "grad_up",
     )
     up = moves.reduction(up, False)
     sq_x, sq_y = after(sq_x, up.keep), after(sq_y, up.keep, d_latest2[1])
     sq_slots = (sq_x, cores(sq_x), sq_y, cores(sq_y))
     down = product(
-        [(after(cot2[0], up.keep), cot2[1])], [(0, (hidden2, 0), (hidden2, 1), 0, 1)], chunk, True, "grad_down"
+        [(after(cot2[0], up.keep), cot2[1])], [(0, (hidden2, 0), (hidden_rest2, 0), 0, 1)], chunk, True, "grad_down"
     )
     down = moves.reduction(down, True)
     out_rows = unpack_frames(after(out_moved, down.keep))

time: 538 us -> 505 us (0.939)
  Pallas kernels: 258 us -> 224 us
    pallas_call x4, Pallas kernels: 77.4 us -> 59.1 us  [branch_back(): pl.pallas_call(partial(back_kernel, groups, segments, sums, final, len(we...]
    pallas_call x1, Pallas kernels: 28.9 us -> 16 us  [time_forward(): pl.pallas_call(partial(time_kernel, groups), grid=(4,), in_specs=[whole(r...]
    pallas_call x2, Pallas kernels: 23.9 us -> 16.4 us  [space_heads(): pl.pallas_call(partial(space_kernel, groups, full), grid_spec=pltpu.Prefe...]
    pallas_call x1 -> x2, Pallas kernels: 34.6 us -> 41.9 us  [feed_forward(): pl.pallas_call(partial(ffn_kernel, final), grid=(4,), in_specs=[whole(row...]
    ppermute x67 -> x68, starting transfers between devices: 61.4 us -> 66.8 us  [swap(): lax.ppermute(value, axis, [(i, i ^ step) for i in range(sizes[axis])])]
    pallas_call x9 -> x10, Pallas kernels: 11.5 us -> 12.9 us  [pause(): pl.pallas_call(pause_kernel, out_shape=shape_of(8, 128, dtype=F32), cost_...]
    ppermute x67 -> x68, waiting for transfers between devices: 96.2 us -> 96.2 us  [swap(): lax.ppermute(value, axis, [(i, i ^ step) for i in range(sizes[axis])])]
  transfers between devices with their start and end apart: 71 -> 72, of which waited for: 19 -> 18; matrix products, arithmetic and copies ran while one was open for 15% -> 16% of each run, Pallas kernels for 42% -> 45%
where the time goes in v4:
time: 505 us; the launch traced here: 497 us
  Pallas kernels  224 us (44%)
  waiting for transfers between devices  96.2 us (19%)
  starting transfers between devices  87.5 us (17%)
  other arithmetic  51.5 us (10%)
  local copies, waits for them, and re-layouts  35.7 us (7%)
    ppermute x68, waiting for transfers between devices, swap(): lax.ppermute(value, axis, [(i, i ^ step) for i in range(sizes[axis])])  96.2 us
    ppermute x68, starting transfers between devices, swap(): lax.ppermute(value, axis, [(i, i ^ step) for i in range(sizes[axis])])  66.8 us
    pallas_call x6, Pallas kernels, grad_product(): pl.pallas_call(partial(grad_kernel, chunk, y_first, [term[0] for term in...  63.6 us
    pallas_call x4, Pallas kernels, branch_back(): pl.pallas_call(partial(back_kernel, groups, segments, sums, final, len(we...  59.1 us
    pallas_call x2, Pallas kernels, feed_forward(): pl.pallas_call(partial(ffn_kernel, final), grid=(4,), in_specs=[whole(row...  41.9 us
    all_to_all x4, starting transfers between devices, exchange(): lax.all_to_all(packed, 'wide', split_axis=0, concat_axis=0, tiled=True)  20.8 us
    pallas_call x2, Pallas kernels, space_heads(): pl.pallas_call(partial(space_kernel, groups, full), grid_spec=pltpu.Prefe...  16.4 us
    pallas_call x1, Pallas kernels, time_forward(): pl.pallas_call(partial(time_kernel, groups), grid=(4,), in_specs=[whole(r...  16 us
  transfers between devices with their start and end apart: 72, of which 18 were waited for; matrix products, arithmetic and copies ran while one was open for 16% of the time, Pallas kernels for 45%

profile of v4, /device:TPU:0, one launch (start us, length us, event | category | flops | bytes accessed | tf_op | source)
XLA Modules:
  0.0 497.2 jit_solution(1177182504534833969)
XLA Ops:
  18.1 7.6 %space_partner.1 = bf16[2,640,256]{2,1,0:T(8,128)(2,1)} custom-call(s32[1]{0:T(128)S(6)} %sub.11._, bf16[2,2,256,1024]{3,2,1,0:T(8,128)(2,1)} %fa_ref.3, bf16[2,2,64,1024]{3,2,1,0:T(8,128)(2,1)} %fb_ref.3, f32[2,4,1024]{2,1,0:T(4,128)} %fusion.23.shift_ref, f32[1,1024]{1,0:T(1,128)} %bitcast.272, bf16[3,1024,512]{2,1,0:T(8,128)(2,1)} %refs_0_.5), custom_call_target="tpu_custom_call" | custom-call | flops 8000000000 | bytes 1048576 | tf_op jit(solution)/shard_map/space_partner/pallas_call | solution.py:217
  28.6 8.8 %space_own.1 = (bf16[2,640,256]{2,1,0:T(8,128)(2,1)}, bf16[2,3,640,256]{3,2,1,0:T(8,128)(2,1)}, f32[2,8,640]{2,1,0:T(8,128)}, f32[640,1024]{1,0:T(8,128)}, bf16[640,1024]{1,0:T(8,128)(2,1)}) custom-call(s32[1]{0:T(128)} %bitcast.3._, bf16[2,2,256,1024]{3,2,1,0:T(8,128)(2,1)} %fa_ref.3, bf16[2,2,64,1024]{3,2,1,0:T(8,128)(2,1)} %fb_ref.3, ...), custom_call_target="tpu_custom_call" | custom-call | flops 8000000000 | bytes 1048576 | tf_op jit(solution)/shard_map/space_own/pallas_call | solution.py:217
  78.3 14.8 %collective-permute-done.6.q2.refs_5_ = bf16[4,1024,128]{2,1,0:T(8,128)(2,1)} collective-permute-done((bf16[4,1024,128]{2,1,0:T(8,128)(2,1)}, bf16[4,1024,128]{2,1,0:T(8,128)(2,1)}, u32[]{:S(2)}, u32[]{:S(2)}) %collective-permute-start.6) | collective-permute-done | bytes 1048608 | tf_op jit(solution)/shard_map/ppermute | solution.py:751
  101.5 16.0 %time_forward.1 = (bf16[640,1024]{1,0:T(8,128)(2,1)}, bf16[640,1024]{1,0:T(8,128)(2,1)}, bf16[4,640,256]{2,1,0:T(8,128)(2,1)}, bf16[4,3,640,256]{3,2,1,0:T(8,128)(2,1)}, f32[4,8,640]{2,1,0:T(8,128)}) custom-call(bf16[640,1024]{1,0:T(8,128)(2,1)} %bitcast.237, f32[1,1024]{1,0:T(1,128)} %bitcast.268, bf16[3,1024,512]{2,1,0:T(8,128)(2,1)} %refs_0_.4, ...), custom_call_target="tpu_custom_call" | custom-call | flops 44810600448 | bytes 1048576 | tf_op jit(solution)/shard_map/time_forward/pallas_call | solution.py:372
  118.6 19.4 %feed_forward.1 = (bf16[640,1024]{1,0:T(8,128)(2,1)}, bf16[4,2,640,512]{3,2,1,0:T(8,128)(2,1)}, f32[640,1024]{1,0:T(8,128)}, f32[640,1024]{1,0:T(8,128)}) custom-call(bf16[640,1024]{1,0:T(8,128)(2,1)} %get-tuple-element.157.late_ref, bf16[640,1024]{1,0:T(8,128)(2,1)} %bitcast.233, f32[1,1024]{1,0:T(1,128)} %bitcast.270, bf16[1024,2048]{1,0:T(8,128)(2,1)} %refs_0_.3, ...), custom_call_target="tpu_custom_call" | custom-call | flops 15121899520 | bytes 1048576 | tf_op jit(solution)/shard_map/feed_forward/pallas_call | solution.py:502
  144.7 22.6 %feed_forward_end.1 = (bf16[640,1024]{1,0:T(8,128)(2,1)}, bf16[640,1024]{1,0:T(8,128)(2,1)}, bf16[4,2,640,512]{3,2,1,0:T(8,128)(2,1)}, f32[1,1024]{1,0:T(1,128)}) custom-call(bf16[640,1024]{1,0:T(8,128)(2,1)} %get-tuple-element.157.late_ref, bf16[640,1024]{1,0:T(8,128)(2,1)} %bitcast.234, f32[1,1024]{1,0:T(1,128)} %bitcast.271, ...), custom_call_target="tpu_custom_call" | custom-call | flops 15121899520 | bytes 1048576 | tf_op jit(solution)/shard_map/feed_forward_end/pallas_call | solution.py:502
  176.8 12.7 %time_back.1 = (f32[640,1024]{1,0:T(8,128)}, bf16[2,3,640,256]{3,2,1,0:T(8,128)(2,1)}) custom-call(bf16[640,1024]{1,0:T(8,128)(2,1)} %get-tuple-element.190.dy_ref.refs_2_, bf16[4,3,640,256]{3,2,1,0:T(8,128)(2,1)} %get-tuple-element.168.proj_any, f32[4,8,640]{2,1,0:T(8,128)} %get-tuple-element.169.logs_any, bf16[3,1024,512]{2,1,0:T(8,128)(2,1)} %refs_0_.4, ...), custom_call_target="tpu_custom_call" | custom-call | flops 11333900288 | bytes 1048576 | tf_op jit(solution)/shard_map/time_back/pallas_call | solution.py:615
  190.0 13.0 %grad_product.6 = (bf16[2,4,128,1024]{3,2,1,0:T(8,128)(2,1)}, bf16[2,4,128,1024]{3,2,1,0:T(8,128)(2,1)}) custom-call(s32[3]{0:T(128)} %pad_add_fusion.1.bits_ref, bf16[640,1024]{1,0:T(8,128)(2,1)} %get-tuple-element.172.refs_0_, bf16[640,1024]{1,0:T(8,128)(2,1)} %collective-permute-done.17.refs_1_, bf16[4,2,640,512]{3,2,1,0:T(8,128)(2,1)} %get-tuple-element.162.refs_2_, ...), custom_call_target="tpu_custom_call" | custom-call | flops 12840999936 | bytes 1048576 | tf_op jit(solution)/shard_map/grad_product/pallas_call | solution.py:724
  204.7 13.0 %grad_product.7 = (bf16[2,4,128,1024]{3,2,1,0:T(8,128)(2,1)}, bf16[2,4,128,1024]{3,2,1,0:T(8,128)(2,1)}) custom-call(s32[3]{0:T(128)} %pad_add_fusion.1.bits_ref, bf16[640,1024]{1,0:T(8,128)(2,1)} %bitcast.235, bf16[640,1024]{1,0:T(8,128)(2,1)} %collective-permute-done.20.refs_1_, bf16[4,2,640,512]{3,2,1,0:T(8,128)(2,1)} %get-tuple-element.162.refs_2_, ...), custom_call_target="tpu_custom_call" | custom-call | flops 574899968 | bytes 1048576 | tf_op jit(solution)/shard_map/grad_product/pallas_call | solution.py:724
  220.7 15.8 %time_back_end.1 = (bf16[640,1024]{1,0:T(8,128)(2,1)}, bf16[2,3,640,256]{3,2,1,0:T(8,128)(2,1)}, f32[1,1024]{1,0:T(1,128)}, f32[8,1024]{1,0:T(8,128)}) custom-call(bf16[640,1024]{1,0:T(8,128)(2,1)} %get-tuple-element.190.dy_ref.refs_2_, bf16[4,3,640,256]{3,2,1,0:T(8,128)(2,1)} %get-tuple-element.168.proj_any, f32[4,8,640]{2,1,0:T(8,128)} %get-tuple-element.169.logs_any, ...), custom_call_target="tpu_custom_call" | custom-call | flops 852000000 | bytes 1048576 | tf_op jit(solution)/shard_map/time_back_end/pallas_call | solution.py:615
  244.7 6.3 %collective-permute-done.23 = bf16[2,4,128,1024]{3,2,1,0:T(8,128)(2,1)} collective-permute-done((bf16[2,4,128,1024]{3,2,1,0:T(8,128)(2,1)}, bf16[2,4,128,1024]{3,2,1,0:T(8,128)(2,1)}, u32[]{:S(2)}, u32[]{:S(2)}) %collective-permute-start.23) | collective-permute-done | bytes 2097184 | tf_op jit(solution)/shard_map/ppermute | solution.py:751
  257.1 8.9 %grad_product.8 = (bf16[2,4,128,512]{3,2,1,0:T(8,128)(2,1)}, bf16[2,4,128,512]{3,2,1,0:T(8,128)(2,1)}) custom-call(s32[3]{0:T(128)} %pad_add_fusion.1.bits_ref, bf16[640,1024]{1,0:T(8,128)(2,1)} %get-tuple-element.185.refs_0_, bf16[640,1024]{1,0:T(8,128)(2,1)} %collective-permute-done.22.refs_1_, ...), custom_call_target="tpu_custom_call" | custom-call | flops 115100000 | bytes 1048576 | tf_op jit(solution)/shard_map/grad_product/pallas_call | solution.py:724
  266.6 10.0 %grad_product.9 = (bf16[2,4,128,512]{3,2,1,0:T(8,128)(2,1)}, bf16[2,4,128,512]{3,2,1,0:T(8,128)(2,1)}) custom-call(s32[3]{0:T(128)} %pad_add_fusion.1.bits_ref, bf16[640,1024]{1,0:T(8,128)(2,1)} %get-tuple-element.185.refs_0_, bf16[640,1024]{1,0:T(8,128)(2,1)} %collective-permute-done.22.refs_1_, bf16[640,1024]{1,0:T(8,128)(2,1)} %get-tuple-element.190.dy_ref.refs_2_, ...), custom_call_target="tpu_custom_call" | custom-call | flops 626899968 | bytes 1048576 | tf_op jit(solution)/shard_map/grad_product/pallas_call | solution.py:724
  288.4 7.7 %space_rest.1 = (bf16[2,640,256]{2,1,0:T(8,128)(2,1)}, bf16[2,3,640,256]{3,2,1,0:T(8,128)(2,1)}, f32[2,8,640]{2,1,0:T(8,128)}) custom-call(bf16[640,1024]{1,0:T(8,128)(2,1)} %get-tuple-element.232.normed_ref.refs_0_, bf16[3,1024,128]{2,1,0:T(8,128)(2,1)} %collective-permute-done.29.q0.refs_3_, bf16[3,1024,128]{2,1,0:T(8,128)(2,1)} %collective-permute-done.30.q1.refs_4_, ...), custom_call_target="tpu_custom_call" | custom-call | flops 1031000000 | bytes 1048576 | tf_op jit(solution)/shard_map/space_rest/pallas_call | solution.py:294
  297.2 8.2 %collective-permute-done.33 = bf16[2,4,128,512]{3,2,1,0:T(8,128)(2,1)} collective-permute-done((bf16[2,4,128,512]{3,2,1,0:T(8,128)(2,1)}, bf16[2,4,128,512]{3,2,1,0:T(8,128)(2,1)}, u32[]{:S(2)}, u32[]{:S(2)}) %collective-permute-start.33) | collective-permute-done | bytes 1048608 | tf_op jit(solution)/shard_map/ppermute | solution.py:751
  309.7 13.7 %space_back.1 = (f32[640,1024]{1,0:T(8,128)}, bf16[2,3,640,256]{3,2,1,0:T(8,128)(2,1)}) custom-call(bf16[640,1024]{1,0:T(8,128)(2,1)} %pad_maximum_fusion.2.dy_ref.refs_2_, bf16[2,3,640,256]{3,2,1,0:T(8,128)(2,1)} %get-tuple-element.209.proj_any, f32[2,8,640]{2,1,0:T(8,128)} %get-tuple-element.210.logs_any, bf16[3,1024,512]{2,1,0:T(8,128)(2,1)} %refs_0_.5, ...), custom_call_target="tpu_custom_call" | custom-call | flops 6081099776 | bytes 1048576 | tf_op jit(solution)/shard_map/space_back/pallas_call | solution.py:615
  336.0 16.9 %space_back_end.1 = (bf16[640,1024]{1,0:T(8,128)(2,1)}, bf16[2,3,640,256]{3,2,1,0:T(8,128)(2,1)}, f32[1,1024]{1,0:T(1,128)}, f32[8,1024]{1,0:T(8,128)}) custom-call(bf16[640,1024]{1,0:T(8,128)(2,1)} %pad_maximum_fusion.2.dy_ref.refs_2_, bf16[2,3,640,256]{3,2,1,0:T(8,128)(2,1)} %get-tuple-element.207.proj_any, f32[2,8,640]{2,1,0:T(8,128)} %get-tuple-element.208.logs_any, ...), custom_call_target="tpu_custom_call" | custom-call | flops 30433099776 | bytes 1048576 | tf_op jit(solution)/shard_map/space_back_end/pallas_call | solution.py:615
  358.0 10.1 %collective-permute-done.40 = bf16[4,128,512]{2,1,0:T(8,128)(2,1)} collective-permute-done((bf16[4,128,512]{2,1,0:T(8,128)(2,1)}, bf16[4,128,512]{2,1,0:T(8,128)(2,1)}, u32[]{:S(2)}, u32[]{:S(2)}) %collective-permute-start.40) | collective-permute-done | bytes 524320 | tf_op jit(solution)/shard_map/ppermute | solution.py:751
  377.3 9.9 %grad_product.10 = (bf16[2,4,128,512]{3,2,1,0:T(8,128)(2,1)}, bf16[2,4,128,512]{3,2,1,0:T(8,128)(2,1)}) custom-call(s32[3]{0:T(128)} %pad_add_fusion.1.bits_ref, bf16[640,1024]{1,0:T(8,128)(2,1)} %get-tuple-element.232.normed_ref.refs_0_, bf16[640,1024]{1,0:T(8,128)(2,1)} %collective-permute-done.41.refs_1_, ...), custom_call_target="tpu_custom_call" | custom-call | flops 351700000 | bytes 1048576 | tf_op jit(solution)/shard_map/grad_product/pallas_call | solution.py:724
  389.7 8.9 %grad_product.11 = (bf16[2,4,128,512]{3,2,1,0:T(8,128)(2,1)}, bf16[2,4,128,512]{3,2,1,0:T(8,128)(2,1)}) custom-call(s32[3]{0:T(128)} %pad_add_fusion.1.bits_ref, bf16[640,1024]{1,0:T(8,128)(2,1)} %get-tuple-element.232.normed_ref.refs_0_, bf16[640,1024]{1,0:T(8,128)(2,1)} %collective-permute-done.41.refs_1_, ...), custom_call_target="tpu_custom_call" | custom-call | flops 1624000000 | bytes 1048576 | tf_op jit(solution)/shard_map/grad_product/pallas_call | solution.py:724
  406.9 6.5 %collective-permute-done.49 = bf16[2,4,128,512]{3,2,1,0:T(8,128)(2,1)S(1)} collective-permute-done((bf16[2,4,128,512]{3,2,1,0:T(8,128)(2,1)}, bf16[2,4,128,512]{3,2,1,0:T(8,128)(2,1)S(1)}, u32[]{:S(2)}, u32[]{:S(2)}) %collective-permute-start.49) | collective-permute-done | bytes 1048608 | tf_op jit(solution)/shard_map/ppermute | solution.py:751
  416.3 9.1 %collective-permute-done.50 = bf16[2,4,128,512]{3,2,1,0:T(8,128)(2,1)S(1)} collective-permute-done((bf16[2,4,128,512]{3,2,1,0:T(8,128)(2,1)}, bf16[2,4,128,512]{3,2,1,0:T(8,128)(2,1)S(1)}, u32[]{:S(2)}, u32[]{:S(2)}) %collective-permute-start.50) | collective-permute-done | bytes 1048608 | tf_op jit(solution)/shard_map/ppermute | solution.py:751
  440.3 8.1 %collective-permute-done.55 = bf16[4,128,512]{2,1,0:T(8,128)(2,1)S(1)} collective-permute-done((bf16[4,128,512]{2,1,0:T(8,128)(2,1)S(1)}, bf16[4,128,512]{2,1,0:T(8,128)(2,1)S(1)}, u32[]{:S(2)}, u32[]{:S(2)}) %collective-permute-start.55) | collective-permute-done | bytes 524320 | tf_op jit(solution)/shard_map/ppermute | solution.py:751
  471.6 8.4 %collective-permute-start.57 = (f32[11,128]{1,0:T(8,128)}, f32[11,128]{1,0:T(8,128)}, u32[]{:S(2)}, u32[]{:S(2)}) collective-permute-start(f32[11,128]{1,0:T(8,128)} %bitcast.229), channel_id=1, source_target_pairs={{0,8},{2,10},{4,12},{6,14},{8,0},{10,2},{12,4},{14,6},{1,9},{3,11}... | collective-permute-start | bytes 16904 | tf_op jit(solution)/shard_map/ppermute | solution.py:751
  (329 shorter events, 219.3 us)
Async XLA Ops:
  8.4 58.4 %collective-permute-start.5 = (bf16[4,1024,128]{2,1,0:T(8,128)(2,1)}, bf16[4,1024,128]{2,1,0:T(8,128)(2,1)}, u32[]{:S(2)}, u32[]{:S(2)}) collective-permute-start(bf16[4,1024,128]{2,1,0:T(8,128)(2,1)} %pad_maximum_fusion.3), channel_id=1, source_target_pairs={{0,1},{1,0},{2,3},{3,2},{4,5},{5,4},{6,7},{7,6},{8,9},{9,8},{10,11... | collective-permute-start | bytes 3145736 | tf_op jit(solution)/shard_map/ppermute | solution.py:751
  9.9 50.6 %all-to-all-start = ((bf16[8,2,40,1024]{3,2,1,0:T(8,128)(2,1)}), bf16[8,2,40,1024]{3,2,1,0:T(8,128)(2,1)S(1)}, u32[]{:S(2)}, u32[]{:S(2)}) async-start(bf16[8,2,40,1024]{3,2,1,0:T(8,128)(2,1)} %copy.83), calls=%async_computation | async-start | bytes 2621440 | tf_op jit(solution)/shard_map/all_to_all | solution.py:919
  60.5 37.5 %all-to-all-start.1 = ((bf16[8,2,40,1024]{3,2,1,0:T(8,128)(2,1)}), bf16[8,2,40,1024]{3,2,1,0:T(8,128)(2,1)S(1)}, u32[]{:S(2)}, u32[]{:S(2)}) async-start(bf16[8,2,40,1024]{3,2,1,0:T(8,128)(2,1)} %copy_bitcast_fusion), calls=%async_computation.1 | async-start | bytes 2621440 | tf_op jit(solution)/shard_map/all_to_all | solution.py:919
  75.0 63.9 %collective-permute-start.11 = (bf16[1024,512]{1,0:T(8,128)(2,1)}, bf16[1024,512]{1,0:T(8,128)(2,1)}, u32[]{:S(2)}, u32[]{:S(2)}) collective-permute-start(bf16[1024,512]{1,0:T(8,128)(2,1)} %collective-permute-done.7.refs_3_), channel_id=1, source_target_pairs={{0,2},{2,0},{4,6},{6,4},{8,10},{10,8},{12,14},{14,12},{1,3},{3,1},... | collective-permute-start | bytes 3145736 | tf_op jit(solution)/shard_map/ppermute | solution.py:751
  75.5 62.5 %collective-permute-start.12 = (bf16[1024,512]{1,0:T(8,128)(2,1)}, bf16[1024,512]{1,0:T(8,128)(2,1)}, u32[]{:S(2)}, u32[]{:S(2)}) collective-permute-start(bf16[1024,512]{1,0:T(8,128)(2,1)} %collective-permute-done.7.refs_3_), channel_id=1, source_target_pairs={{0,16},{16,0},{1,17},{17,1},{2,18},{18,2},{3,19},{19,3},{4,20},{20... | collective-permute-start | bytes 3145736 | tf_op jit(solution)/shard_map/ppermute | solution.py:751
  96.7 42.1 %collective-permute-start.14 = (bf16[512,1024]{1,0:T(8,128)(2,1)}, bf16[512,1024]{1,0:T(8,128)(2,1)}, u32[]{:S(2)}, u32[]{:S(2)}) collective-permute-start(bf16[512,1024]{1,0:T(8,128)(2,1)} %collective-permute-done.8.refs_7_), channel_id=1, source_target_pairs={{0,2},{2,0},{4,6},{6,4},{8,10},{10,8},{12,14},{14,12},{1,3},{3,1},... | collective-permute-start | bytes 3145736 | tf_op jit(solution)/shard_map/ppermute | solution.py:751
  99.2 39.1 %collective-permute-start.15 = (bf16[512,1024]{1,0:T(8,128)(2,1)}, bf16[512,1024]{1,0:T(8,128)(2,1)S(1)}, u32[]{:S(2)}, u32[]{:S(2)}) collective-permute-start(bf16[512,1024]{1,0:T(8,128)(2,1)} %collective-permute-done.8.refs_7_), channel_id=1, source_target_pairs={{0,16},{16,0},{1,17},{17,1},{2,18},{18,2},{3,19},{19,3},{4,20},{20... | collective-permute-start | bytes 3145736 | tf_op jit(solution)/shard_map/ppermute | solution.py:751
  138.6 51.4 %collective-permute-start.18 = (bf16[4,2,640,512]{3,2,1,0:T(8,128)(2,1)}, bf16[4,2,640,512]{3,2,1,0:T(8,128)(2,1)}, u32[]{:S(2)}, u32[]{:S(2)}) collective-permute-start(bf16[4,2,640,512]{3,2,1,0:T(8,128)(2,1)} %get-tuple-element.162.refs_2_), channel_id=1, source_target_pairs={{0,2},{2,0},{4,6},{6,4},{8,10},{10,8},{12,14},{14,12},{1,3},{3,1},... | collective-permute-start | bytes 15728648 | tf_op jit(solution)/shard_map/ppermute | solution.py:751
  169.1 35.1 %collective-permute-start.29 = (bf16[3,1024,128]{2,1,0:T(8,128)(2,1)S(1)}, bf16[3,1024,128]{2,1,0:T(8,128)(2,1)}, u32[]{:S(2)}, u32[]{:S(2)}) collective-permute-start(bf16[3,1024,128]{2,1,0:T(8,128)(2,1)S(1)} %constant_dynamic-slice_fusion.7), channel_id=1, source_target_pairs={{0,1},{1,0},{2,3},{3,2},{4,5},{5,4},{6,7},{7,6},{8,9},{9,8},{10,11... | collective-permute-start | bytes 2359304 | tf_op jit(solution)/shard_map/ppermute | solution.py:751
  171.3 46.3 %all-to-all-start.2 = ((bf16[8,2,40,1024]{3,2,1,0:T(8,128)(2,1)}), bf16[8,2,40,1024]{3,2,1,0:T(8,128)(2,1)S(1)}, u32[]{:S(2)}, u32[]{:S(2)}) async-start(bf16[8,2,40,1024]{3,2,1,0:T(8,128)(2,1)} %bitcast.242), calls=%async_computation.2 | async-start | bytes 2621440 | tf_op jit(solution)/shard_map/all_to_all | solution.py:919
  189.5 47.1 %collective-permute-start.22 = (bf16[640,1024]{1,0:T(8,128)(2,1)}, bf16[640,1024]{1,0:T(8,128)(2,1)}, u32[]{:S(2)}, u32[]{:S(2)}) collective-permute-start(bf16[640,1024]{1,0:T(8,128)(2,1)} %get-tuple-element.185.refs_0_), channel_id=1, source_target_pairs={{0,2},{2,0},{4,6},{6,4},{8,10},{10,8},{12,14},{14,12},{1,3},{3,1},... | collective-permute-start | bytes 3932168 | tf_op jit(solution)/shard_map/ppermute | solution.py:751
  203.0 47.9 %collective-permute-start.23 = (bf16[2,4,128,1024]{3,2,1,0:T(8,128)(2,1)}, bf16[2,4,128,1024]{3,2,1,0:T(8,128)(2,1)}, u32[]{:S(2)}, u32[]{:S(2)}) collective-permute-start(bf16[2,4,128,1024]{3,2,1,0:T(8,128)(2,1)} %get-tuple-element.184), channel_id=1, source_target_pairs={{0,1},{1,0},{2,3},{3,2},{4,5},{5,4},{6,7},{7,6},{8,9},{9,8},{10,11... | collective-permute-start | bytes 6291464 | tf_op jit(solution)/shard_map/ppermute | solution.py:751
  217.9 58.6 %collective-permute-start.28 = (bf16[2,4,128,1024]{3,2,1,0:T(8,128)(2,1)}, bf16[2,4,128,1024]{3,2,1,0:T(8,128)(2,1)}, u32[]{:S(2)}, u32[]{:S(2)}) collective-permute-start(bf16[2,4,128,1024]{3,2,1,0:T(8,128)(2,1)} %get-tuple-element.195), channel_id=1, source_target_pairs={{0,16},{16,0},{1,17},{17,1},{2,18},{18,2},{3,19},{19,3},{4,20},{20... | collective-permute-start | bytes 6291464 | tf_op jit(solution)/shard_map/ppermute | solution.py:751
  239.8 68.5 %all-to-all-start.3 = ((bf16[8,2,40,1024]{3,2,1,0:T(8,128)(2,1)}), bf16[8,2,40,1024]{3,2,1,0:T(8,128)(2,1)S(1)}, u32[]{:S(2)}, u32[]{:S(2)}) async-start(bf16[8,2,40,1024]{3,2,1,0:T(8,128)(2,1)} %bitcast.240), calls=%async_computation.3 | async-start | bytes 2621440 | tf_op jit(solution)/shard_map/all_to_all | solution.py:919
  266.0 65.8 %collective-permute-start.34 = (bf16[4,128,1024]{2,1,0:T(8,128)(2,1)}, bf16[4,128,1024]{2,1,0:T(8,128)(2,1)}, u32[]{:S(2)}, u32[]{:S(2)}) collective-permute-start(bf16[4,128,1024]{2,1,0:T(8,128)(2,1)} %get-tuple-element.321), channel_id=1, source_target_pairs={{0,16},{16,0},{1,17},{17,1},{2,18},{18,2},{3,19},{19,3},{4,20},{20... | collective-permute-start | bytes 3145736 | tf_op jit(solution)/shard_map/ppermute | solution.py:751
  282.8 43.2 %collective-permute-start.35 = (bf16[4,128,1024]{2,1,0:T(8,128)(2,1)}, bf16[4,128,1024]{2,1,0:T(8,128)(2,1)}, u32[]{:S(2)}, u32[]{:S(2)}) collective-permute-start(bf16[4,128,1024]{2,1,0:T(8,128)(2,1)} %get-tuple-element.319), channel_id=1, source_target_pairs={{0,1},{1,0},{2,3},{3,2},{4,5},{5,4},{6,7},{7,6},{8,9},{9,8},{10,11... | collective-permute-start | bytes 3145736 | tf_op jit(solution)/shard_map/ppermute | solution.py:751
  297.2 56.3 %collective-permute-start.44 = (bf16[2,1,640,256]{3,2,1,0:T(8,128)(2,1)}, bf16[2,1,640,256]{3,2,1,0:T(8,128)(2,1)}, u32[]{:S(2)}, u32[]{:S(2)}) collective-permute-start(bf16[2,1,640,256]{3,2,1,0:T(8,128)(2,1)} %bitcast.57.refs_6_), channel_id=1, source_target_pairs={{0,2},{2,0},{4,6},{6,4},{8,10},{10,8},{12,14},{14,12},{1,3},{3,1},... | collective-permute-start | bytes 1966088 | tf_op jit(solution)/shard_map/ppermute | solution.py:751
  305.3 48.3 %collective-permute-start.46 = (bf16[2,1,640,256]{3,2,1,0:T(8,128)(2,1)}, bf16[2,1,640,256]{3,2,1,0:T(8,128)(2,1)}, u32[]{:S(2)}, u32[]{:S(2)}) collective-permute-start(bf16[2,1,640,256]{3,2,1,0:T(8,128)(2,1)} %bitcast.262), channel_id=1, source_target_pairs={{0,2},{2,0},{4,6},{6,4},{8,10},{10,8},{12,14},{14,12},{1,3},{3,1},... | collective-permute-start | bytes 1966088 | tf_op jit(solution)/shard_map/ppermute | solution.py:751
  336.0 41.3 %collective-permute-start.43 = (bf16[2,3,640,256]{3,2,1,0:T(8,128)(2,1)S(1)}, bf16[2,3,640,256]{3,2,1,0:T(8,128)(2,1)}, u32[]{:S(2)}, u32[]{:S(2)}) collective-permute-start(bf16[2,3,640,256]{3,2,1,0:T(8,128)(2,1)S(1)} %copy-done.3), channel_id=1, source_target_pairs={{0,2},{2,0},{4,6},{6,4},{8,10},{10,8},{12,14},{14,12},{1,3},{3,1},... | collective-permute-start | bytes 5898248 | tf_op jit(solution)/shard_map/ppermute | solution.py:751
  373.1 55.2 %collective-permute-start.53 = (bf16[2,128,1024]{2,1,0:T(8,128)(2,1)}, bf16[2,128,1024]{2,1,0:T(8,128)(2,1)}, u32[]{:S(2)}, u32[]{:S(2)}) collective-permute-start(bf16[2,128,1024]{2,1,0:T(8,128)(2,1)} %get-tuple-element.316), channel_id=1, source_target_pairs={{0,12},{2,14},{4,8},{6,10},{8,4},{10,6},{12,0},{14,2},{1,13},{3,15... | collective-permute-start | bytes 1572872 | tf_op jit(solution)/shard_map/ppermute | solution.py:751
  377.3 57.7 %collective-permute-start.52 = (bf16[2,128,1024]{2,1,0:T(8,128)(2,1)}, bf16[2,128,1024]{2,1,0:T(8,128)(2,1)}, u32[]{:S(2)}, u32[]{:S(2)}) collective-permute-start(bf16[2,128,1024]{2,1,0:T(8,128)(2,1)} %get-tuple-element.317), channel_id=1, source_target_pairs={{0,8},{2,10},{4,12},{6,14},{8,0},{10,2},{12,4},{14,6},{1,9},{3,11}... | collective-permute-start | bytes 1572872 | tf_op jit(solution)/shard_map/ppermute | solution.py:751
  399.9 36.0 %collective-permute-start.51 = (bf16[2,128,1024]{2,1,0:T(8,128)(2,1)}, bf16[2,128,1024]{2,1,0:T(8,128)(2,1)S(1)}, u32[]{:S(2)}, u32[]{:S(2)}) collective-permute-start(bf16[2,128,1024]{2,1,0:T(8,128)(2,1)} %get-tuple-element.315), channel_id=1, source_target_pairs={{0,4},{2,6},{4,0},{6,2},{8,12},{10,14},{12,8},{14,10},{1,5},{3,7},... | collective-permute-start | bytes 1572872 | tf_op jit(solution)/shard_map/ppermute | solution.py:751
  413.4 38.7 %collective-permute-start.61 = (bf16[2,128,512]{2,1,0:T(8,128)(2,1)}, bf16[2,128,512]{2,1,0:T(8,128)(2,1)}, u32[]{:S(2)}, u32[]{:S(2)}) collective-permute-start(bf16[2,128,512]{2,1,0:T(8,128)(2,1)} %get-tuple-element.328), channel_id=1, source_target_pairs={{0,12},{2,14},{4,8},{6,10},{8,4},{10,6},{12,0},{14,2},{1,13},{3,15... | collective-permute-start | bytes 786440 | tf_op jit(solution)/shard_map/ppermute | solution.py:751
  456.1 34.6 %collective-permute-start.58 = (f32[11,128]{1,0:T(8,128)}, f32[11,128]{1,0:T(8,128)}, u32[]{:S(2)}, u32[]{:S(2)}) collective-permute-start(f32[11,128]{1,0:T(8,128)} %bitcast.228), channel_id=1, source_target_pairs={{0,12},{2,14},{4,8},{6,10},{8,4},{10,6},{12,0},{14,2},{1,13},{3,15... | collective-permute-start | bytes 16904 | tf_op jit(solution)/shard_map/ppermute | solution.py:751
  (92 other events, 1260.4 us)

commit v5 on v4

--- a/solution.py
+++ b/solution.py
@@ -463,7 +463,7 @@
 
     pltpu.make_async_copy(wu.at[slot], wu.at[slot], sems.at[slot, 0]).wait()
     pltpu.make_async_copy(wd.at[slot], wd.at[slot], sems.at[slot, 1]).wait()
-    for chunk in row_chunks(rows, rows // 2):
+    for chunk in row_chunks(rows, rows):
         gelu, slope = gelu_parts(dot_n(normed_ref[chunk, :], wu[slot]))
         gelu = gelu.astype(BF)
         hidden_ref[0, 0, chunk, :] = gelu
@@ -1095,9 +1095,9 @@
     )
     own = (both(d_proj_own), 0)
     ffn, time = Pair(moves, up, down), Pair(moves, time_one, time_two)
-    gates = [up.sum(partial_space), down.sum(partial_space)]
+    gates = [time_two.third(partial_space)]
+    gates += [up.sum(gates[0]), down.sum(gates[0])]
     ffn.fourth()
-    gates += [time_two.third(gates[1])]
     token = pause(tokens, *gates)
     segments = tuple((i * grid_a, grid_a) for i in range(n_frames)) + tuple(
         (rows_a + i * grid_b, grid_b) for i in range(n_frames)

time: 505 us -> 501 us (level)
  no operation moved by 1% of the time
where the time goes in v5:
time: 501 us; the launch traced here: 492 us
  Pallas kernels  222 us (44%)
  waiting for transfers between devices  94 us (19%)
  starting transfers between devices  86.7 us (17%)
  other arithmetic  51.6 us (10%)
  local copies, waits for them, and re-layouts  35.7 us (7%)
    ppermute x68, waiting for transfers between devices, swap(): lax.ppermute(value, axis, [(i, i ^ step) for i in range(sizes[axis])])  93.9 us
    ppermute x68, starting transfers between devices, swap(): lax.ppermute(value, axis, [(i, i ^ step) for i in range(sizes[axis])])  65.9 us
    pallas_call x6, Pallas kernels, grad_product(): pl.pallas_call(partial(grad_kernel, chunk, y_first, [term[0] for term in...  63.6 us
    pallas_call x4, Pallas kernels, branch_back(): pl.pallas_call(partial(back_kernel, groups, segments, sums, final, len(we...  59.1 us
    pallas_call x2, Pallas kernels, feed_forward(): pl.pallas_call(partial(ffn_kernel, final), grid=(4,), in_specs=[whole(row...  39.9 us
    all_to_all x4, starting transfers between devices, exchange(): lax.all_to_all(packed, 'wide', split_axis=0, concat_axis=0, tiled=True)  20.8 us
    pallas_call x2, Pallas kernels, space_heads(): pl.pallas_call(partial(space_kernel, groups, full), grid_spec=pltpu.Prefe...  16.4 us
    pallas_call x1, Pallas kernels, time_forward(): pl.pallas_call(partial(time_kernel, groups), grid=(4,), in_specs=[whole(r...  16 us
  transfers between devices with their start and end apart: 72, of which 18 were waited for; matrix products, arithmetic and copies ran while one was open for 16% of the time, Pallas kernels for 45%

profile of v5, /device:TPU:0, one launch (start us, length us, event | category | flops | bytes accessed | tf_op | source)
XLA Modules:
  0.0 492.3 jit_solution(16994205666769274097)
XLA Ops:
  18.1 7.6 %space_partner.1 = bf16[2,640,256]{2,1,0:T(8,128)(2,1)} custom-call(s32[1]{0:T(128)S(6)} %sub.11._, bf16[2,2,256,1024]{3,2,1,0:T(8,128)(2,1)} %fa_ref.3, bf16[2,2,64,1024]{3,2,1,0:T(8,128)(2,1)} %fb_ref.3, f32[2,4,1024]{2,1,0:T(4,128)} %fusion.23.shift_ref, f32[1,1024]{1,0:T(1,128)} %bitcast.272, bf16[3,1024,512]{2,1,0:T(8,128)(2,1)} %refs_0_.5), custom_call_target="tpu_custom_call" | custom-call | flops 8000000000 | bytes 1048576 | tf_op jit(solution)/shard_map/space_partner/pallas_call | solution.py:217
  28.6 8.8 %space_own.1 = (bf16[2,640,256]{2,1,0:T(8,128)(2,1)}, bf16[2,3,640,256]{3,2,1,0:T(8,128)(2,1)}, f32[2,8,640]{2,1,0:T(8,128)}, f32[640,1024]{1,0:T(8,128)}, bf16[640,1024]{1,0:T(8,128)(2,1)}) custom-call(s32[1]{0:T(128)} %bitcast.3._, bf16[2,2,256,1024]{3,2,1,0:T(8,128)(2,1)} %fa_ref.3, bf16[2,2,64,1024]{3,2,1,0:T(8,128)(2,1)} %fb_ref.3, ...), custom_call_target="tpu_custom_call" | custom-call | flops 8000000000 | bytes 1048576 | tf_op jit(solution)/shard_map/space_own/pallas_call | solution.py:217
  78.3 14.8 %collective-permute-done.6.q2.refs_5_ = bf16[4,1024,128]{2,1,0:T(8,128)(2,1)} collective-permute-done((bf16[4,1024,128]{2,1,0:T(8,128)(2,1)}, bf16[4,1024,128]{2,1,0:T(8,128)(2,1)}, u32[]{:S(2)}, u32[]{:S(2)}) %collective-permute-start.6) | collective-permute-done | bytes 1048608 | tf_op jit(solution)/shard_map/ppermute | solution.py:751
  101.5 16.0 %time_forward.1 = (bf16[640,1024]{1,0:T(8,128)(2,1)}, bf16[640,1024]{1,0:T(8,128)(2,1)}, bf16[4,640,256]{2,1,0:T(8,128)(2,1)}, bf16[4,3,640,256]{3,2,1,0:T(8,128)(2,1)}, f32[4,8,640]{2,1,0:T(8,128)}) custom-call(bf16[640,1024]{1,0:T(8,128)(2,1)} %bitcast.237, f32[1,1024]{1,0:T(1,128)} %bitcast.268, bf16[3,1024,512]{2,1,0:T(8,128)(2,1)} %refs_0_.4, ...), custom_call_target="tpu_custom_call" | custom-call | flops 44810600448 | bytes 1048576 | tf_op jit(solution)/shard_map/time_forward/pallas_call | solution.py:372
  118.6 18.2 %feed_forward.1 = (bf16[640,1024]{1,0:T(8,128)(2,1)}, bf16[4,2,640,512]{3,2,1,0:T(8,128)(2,1)}, f32[640,1024]{1,0:T(8,128)}, f32[640,1024]{1,0:T(8,128)}) custom-call(bf16[640,1024]{1,0:T(8,128)(2,1)} %get-tuple-element.157.late_ref, bf16[640,1024]{1,0:T(8,128)(2,1)} %bitcast.233, f32[1,1024]{1,0:T(1,128)} %bitcast.270, bf16[1024,2048]{1,0:T(8,128)(2,1)} %refs_0_.3, ...), custom_call_target="tpu_custom_call" | custom-call | flops 15121899520 | bytes 1048576 | tf_op jit(solution)/shard_map/feed_forward/pallas_call | solution.py:502
  143.5 21.8 %feed_forward_end.1 = (bf16[640,1024]{1,0:T(8,128)(2,1)}, bf16[640,1024]{1,0:T(8,128)(2,1)}, bf16[4,2,640,512]{3,2,1,0:T(8,128)(2,1)}, f32[1,1024]{1,0:T(1,128)}) custom-call(bf16[640,1024]{1,0:T(8,128)(2,1)} %get-tuple-element.157.late_ref, bf16[640,1024]{1,0:T(8,128)(2,1)} %bitcast.234, f32[1,1024]{1,0:T(1,128)} %bitcast.271, ...), custom_call_target="tpu_custom_call" | custom-call | flops 15121899520 | bytes 1048576 | tf_op jit(solution)/shard_map/feed_forward_end/pallas_call | solution.py:502
  174.8 12.7 %time_back.1 = (f32[640,1024]{1,0:T(8,128)}, bf16[2,3,640,256]{3,2,1,0:T(8,128)(2,1)}) custom-call(bf16[640,1024]{1,0:T(8,128)(2,1)} %get-tuple-element.190.dy_ref.refs_2_, bf16[4,3,640,256]{3,2,1,0:T(8,128)(2,1)} %get-tuple-element.168.proj_any, f32[4,8,640]{2,1,0:T(8,128)} %get-tuple-element.169.logs_any, bf16[3,1024,512]{2,1,0:T(8,128)(2,1)} %refs_0_.4, ...), custom_call_target="tpu_custom_call" | custom-call | flops 11333900288 | bytes 1048576 | tf_op jit(solution)/shard_map/time_back/pallas_call | solution.py:615
  188.1 13.0 %grad_product.6 = (bf16[2,4,128,1024]{3,2,1,0:T(8,128)(2,1)}, bf16[2,4,128,1024]{3,2,1,0:T(8,128)(2,1)}) custom-call(s32[3]{0:T(128)} %pad_add_fusion.1.bits_ref, bf16[640,1024]{1,0:T(8,128)(2,1)} %get-tuple-element.172.refs_0_, bf16[640,1024]{1,0:T(8,128)(2,1)} %collective-permute-done.17.refs_1_, bf16[4,2,640,512]{3,2,1,0:T(8,128)(2,1)} %get-tuple-element.162.refs_2_, ...), custom_call_target="tpu_custom_call" | custom-call | flops 12840999936 | bytes 1048576 | tf_op jit(solution)/shard_map/grad_product/pallas_call | solution.py:724
  202.7 13.0 %grad_product.7 = (bf16[2,4,128,1024]{3,2,1,0:T(8,128)(2,1)}, bf16[2,4,128,1024]{3,2,1,0:T(8,128)(2,1)}) custom-call(s32[3]{0:T(128)} %pad_add_fusion.1.bits_ref, bf16[640,1024]{1,0:T(8,128)(2,1)} %bitcast.235, bf16[640,1024]{1,0:T(8,128)(2,1)} %collective-permute-done.20.refs_1_, bf16[4,2,640,512]{3,2,1,0:T(8,128)(2,1)} %get-tuple-element.162.refs_2_, ...), custom_call_target="tpu_custom_call" | custom-call | flops 574899968 | bytes 1048576 | tf_op jit(solution)/shard_map/grad_product/pallas_call | solution.py:724
  218.7 15.8 %time_back_end.1 = (bf16[640,1024]{1,0:T(8,128)(2,1)}, bf16[2,3,640,256]{3,2,1,0:T(8,128)(2,1)}, f32[1,1024]{1,0:T(1,128)}, f32[8,1024]{1,0:T(8,128)}) custom-call(bf16[640,1024]{1,0:T(8,128)(2,1)} %get-tuple-element.190.dy_ref.refs_2_, bf16[4,3,640,256]{3,2,1,0:T(8,128)(2,1)} %get-tuple-element.168.proj_any, f32[4,8,640]{2,1,0:T(8,128)} %get-tuple-element.169.logs_any, ...), custom_call_target="tpu_custom_call" | custom-call | flops 852000000 | bytes 1048576 | tf_op jit(solution)/shard_map/time_back_end/pallas_call | solution.py:615
  242.7 6.3 %collective-permute-done.23 = bf16[2,4,128,1024]{3,2,1,0:T(8,128)(2,1)} collective-permute-done((bf16[2,4,128,1024]{3,2,1,0:T(8,128)(2,1)}, bf16[2,4,128,1024]{3,2,1,0:T(8,128)(2,1)}, u32[]{:S(2)}, u32[]{:S(2)}) %collective-permute-start.23) | collective-permute-done | bytes 2097184 | tf_op jit(solution)/shard_map/ppermute | solution.py:751
  255.1 8.9 %grad_product.8 = (bf16[2,4,128,512]{3,2,1,0:T(8,128)(2,1)}, bf16[2,4,128,512]{3,2,1,0:T(8,128)(2,1)}) custom-call(s32[3]{0:T(128)} %pad_add_fusion.1.bits_ref, bf16[640,1024]{1,0:T(8,128)(2,1)} %get-tuple-element.185.refs_0_, bf16[640,1024]{1,0:T(8,128)(2,1)} %collective-permute-done.22.refs_1_, ...), custom_call_target="tpu_custom_call" | custom-call | flops 115100000 | bytes 1048576 | tf_op jit(solution)/shard_map/grad_product/pallas_call | solution.py:724
  264.7 10.0 %grad_product.9 = (bf16[2,4,128,512]{3,2,1,0:T(8,128)(2,1)}, bf16[2,4,128,512]{3,2,1,0:T(8,128)(2,1)}) custom-call(s32[3]{0:T(128)} %pad_add_fusion.1.bits_ref, bf16[640,1024]{1,0:T(8,128)(2,1)} %get-tuple-element.185.refs_0_, bf16[640,1024]{1,0:T(8,128)(2,1)} %collective-permute-done.22.refs_1_, bf16[640,1024]{1,0:T(8,128)(2,1)} %get-tuple-element.190.dy_ref.refs_2_, ...), custom_call_target="tpu_custom_call" | custom-call | flops 626899968 | bytes 1048576 | tf_op jit(solution)/shard_map/grad_product/pallas_call | solution.py:724
  286.4 7.7 %space_rest.1 = (bf16[2,640,256]{2,1,0:T(8,128)(2,1)}, bf16[2,3,640,256]{3,2,1,0:T(8,128)(2,1)}, f32[2,8,640]{2,1,0:T(8,128)}) custom-call(bf16[640,1024]{1,0:T(8,128)(2,1)} %get-tuple-element.232.normed_ref.refs_0_, bf16[3,1024,128]{2,1,0:T(8,128)(2,1)} %collective-permute-done.29.q0.refs_3_, bf16[3,1024,128]{2,1,0:T(8,128)(2,1)} %collective-permute-done.30.q1.refs_4_, ...), custom_call_target="tpu_custom_call" | custom-call | flops 1031000000 | bytes 1048576 | tf_op jit(solution)/shard_map/space_rest/pallas_call | solution.py:294
  295.2 8.1 %collective-permute-done.33 = bf16[2,4,128,512]{3,2,1,0:T(8,128)(2,1)} collective-permute-done((bf16[2,4,128,512]{3,2,1,0:T(8,128)(2,1)}, bf16[2,4,128,512]{3,2,1,0:T(8,128)(2,1)}, u32[]{:S(2)}, u32[]{:S(2)}) %collective-permute-start.33) | collective-permute-done | bytes 1048608 | tf_op jit(solution)/shard_map/ppermute | solution.py:751
  307.6 13.7 %space_back.1 = (f32[640,1024]{1,0:T(8,128)}, bf16[2,3,640,256]{3,2,1,0:T(8,128)(2,1)}) custom-call(bf16[640,1024]{1,0:T(8,128)(2,1)} %pad_maximum_fusion.2.dy_ref.refs_2_, bf16[2,3,640,256]{3,2,1,0:T(8,128)(2,1)} %get-tuple-element.209.proj_any, f32[2,8,640]{2,1,0:T(8,128)} %get-tuple-element.210.logs_any, bf16[3,1024,512]{2,1,0:T(8,128)(2,1)} %refs_0_.5, ...), custom_call_target="tpu_custom_call" | custom-call | flops 6081099776 | bytes 1048576 | tf_op jit(solution)/shard_map/space_back/pallas_call | solution.py:615
  331.5 16.9 %space_back_end.1 = (bf16[640,1024]{1,0:T(8,128)(2,1)}, bf16[2,3,640,256]{3,2,1,0:T(8,128)(2,1)}, f32[1,1024]{1,0:T(1,128)}, f32[8,1024]{1,0:T(8,128)}) custom-call(bf16[640,1024]{1,0:T(8,128)(2,1)} %pad_maximum_fusion.2.dy_ref.refs_2_, bf16[2,3,640,256]{3,2,1,0:T(8,128)(2,1)} %get-tuple-element.207.proj_any, f32[2,8,640]{2,1,0:T(8,128)} %get-tuple-element.208.logs_any, ...), custom_call_target="tpu_custom_call" | custom-call | flops 30433099776 | bytes 1048576 | tf_op jit(solution)/shard_map/space_back_end/pallas_call | solution.py:615
  353.4 9.8 %collective-permute-done.40 = bf16[4,128,512]{2,1,0:T(8,128)(2,1)} collective-permute-done((bf16[4,128,512]{2,1,0:T(8,128)(2,1)}, bf16[4,128,512]{2,1,0:T(8,128)(2,1)}, u32[]{:S(2)}, u32[]{:S(2)}) %collective-permute-start.40) | collective-permute-done | bytes 524320 | tf_op jit(solution)/shard_map/ppermute | solution.py:751
  372.3 9.9 %grad_product.10 = (bf16[2,4,128,512]{3,2,1,0:T(8,128)(2,1)}, bf16[2,4,128,512]{3,2,1,0:T(8,128)(2,1)}) custom-call(s32[3]{0:T(128)} %pad_add_fusion.1.bits_ref, bf16[640,1024]{1,0:T(8,128)(2,1)} %get-tuple-element.232.normed_ref.refs_0_, bf16[640,1024]{1,0:T(8,128)(2,1)} %collective-permute-done.41.refs_1_, ...), custom_call_target="tpu_custom_call" | custom-call | flops 351700000 | bytes 1048576 | tf_op jit(solution)/shard_map/grad_product/pallas_call | solution.py:724
  385.0 8.9 %grad_product.11 = (bf16[2,4,128,512]{3,2,1,0:T(8,128)(2,1)}, bf16[2,4,128,512]{3,2,1,0:T(8,128)(2,1)}) custom-call(s32[3]{0:T(128)} %pad_add_fusion.1.bits_ref, bf16[640,1024]{1,0:T(8,128)(2,1)} %get-tuple-element.232.normed_ref.refs_0_, bf16[640,1024]{1,0:T(8,128)(2,1)} %collective-permute-done.41.refs_1_, ...), custom_call_target="tpu_custom_call" | custom-call | flops 1624000000 | bytes 1048576 | tf_op jit(solution)/shard_map/grad_product/pallas_call | solution.py:724
  401.8 6.7 %collective-permute-done.49 = bf16[2,4,128,512]{3,2,1,0:T(8,128)(2,1)S(1)} collective-permute-done((bf16[2,4,128,512]{3,2,1,0:T(8,128)(2,1)}, bf16[2,4,128,512]{3,2,1,0:T(8,128)(2,1)S(1)}, u32[]{:S(2)}, u32[]{:S(2)}) %collective-permute-start.49) | collective-permute-done | bytes 1048608 | tf_op jit(solution)/shard_map/ppermute | solution.py:751
  411.3 9.2 %collective-permute-done.50 = bf16[2,4,128,512]{3,2,1,0:T(8,128)(2,1)S(1)} collective-permute-done((bf16[2,4,128,512]{3,2,1,0:T(8,128)(2,1)}, bf16[2,4,128,512]{3,2,1,0:T(8,128)(2,1)S(1)}, u32[]{:S(2)}, u32[]{:S(2)}) %collective-permute-start.50) | collective-permute-done | bytes 1048608 | tf_op jit(solution)/shard_map/ppermute | solution.py:751
  435.6 8.1 %collective-permute-done.55 = bf16[4,128,512]{2,1,0:T(8,128)(2,1)S(1)} collective-permute-done((bf16[4,128,512]{2,1,0:T(8,128)(2,1)S(1)}, bf16[4,128,512]{2,1,0:T(8,128)(2,1)S(1)}, u32[]{:S(2)}, u32[]{:S(2)}) %collective-permute-start.55) | collective-permute-done | bytes 524320 | tf_op jit(solution)/shard_map/ppermute | solution.py:751
  467.0 8.2 %collective-permute-start.57 = (f32[11,128]{1,0:T(8,128)}, f32[11,128]{1,0:T(8,128)}, u32[]{:S(2)}, u32[]{:S(2)}) collective-permute-start(f32[11,128]{1,0:T(8,128)} %bitcast.229), channel_id=1, source_target_pairs={{0,8},{2,10},{4,12},{6,14},{8,0},{10,2},{12,4},{14,6},{1,9},{3,11}... | collective-permute-start | bytes 16904 | tf_op jit(solution)/shard_map/ppermute | solution.py:751
  (329 shorter events, 216.7 us)
Async XLA Ops:
  8.4 58.4 %collective-permute-start.5 = (bf16[4,1024,128]{2,1,0:T(8,128)(2,1)}, bf16[4,1024,128]{2,1,0:T(8,128)(2,1)}, u32[]{:S(2)}, u32[]{:S(2)}) collective-permute-start(bf16[4,1024,128]{2,1,0:T(8,128)(2,1)} %pad_maximum_fusion.3), channel_id=1, source_target_pairs={{0,1},{1,0},{2,3},{3,2},{4,5},{5,4},{6,7},{7,6},{8,9},{9,8},{10,11... | collective-permute-start | bytes 3145736 | tf_op jit(solution)/shard_map/ppermute | solution.py:751
  9.9 50.6 %all-to-all-start = ((bf16[8,2,40,1024]{3,2,1,0:T(8,128)(2,1)}), bf16[8,2,40,1024]{3,2,1,0:T(8,128)(2,1)S(1)}, u32[]{:S(2)}, u32[]{:S(2)}) async-start(bf16[8,2,40,1024]{3,2,1,0:T(8,128)(2,1)} %copy.83), calls=%async_computation | async-start | bytes 2621440 | tf_op jit(solution)/shard_map/all_to_all | solution.py:919
  60.5 37.5 %all-to-all-start.1 = ((bf16[8,2,40,1024]{3,2,1,0:T(8,128)(2,1)}), bf16[8,2,40,1024]{3,2,1,0:T(8,128)(2,1)S(1)}, u32[]{:S(2)}, u32[]{:S(2)}) async-start(bf16[8,2,40,1024]{3,2,1,0:T(8,128)(2,1)} %copy_bitcast_fusion), calls=%async_computation.1 | async-start | bytes 2621440 | tf_op jit(solution)/shard_map/all_to_all | solution.py:919
  75.0 63.1 %collective-permute-start.11 = (bf16[1024,512]{1,0:T(8,128)(2,1)}, bf16[1024,512]{1,0:T(8,128)(2,1)}, u32[]{:S(2)}, u32[]{:S(2)}) collective-permute-start(bf16[1024,512]{1,0:T(8,128)(2,1)} %collective-permute-done.7.refs_3_), channel_id=1, source_target_pairs={{0,2},{2,0},{4,6},{6,4},{8,10},{10,8},{12,14},{14,12},{1,3},{3,1},... | collective-permute-start | bytes 3145736 | tf_op jit(solution)/shard_map/ppermute | solution.py:751
  75.5 61.3 %collective-permute-start.12 = (bf16[1024,512]{1,0:T(8,128)(2,1)}, bf16[1024,512]{1,0:T(8,128)(2,1)}, u32[]{:S(2)}, u32[]{:S(2)}) collective-permute-start(bf16[1024,512]{1,0:T(8,128)(2,1)} %collective-permute-done.7.refs_3_), channel_id=1, source_target_pairs={{0,16},{16,0},{1,17},{17,1},{2,18},{18,2},{3,19},{19,3},{4,20},{20... | collective-permute-start | bytes 3145736 | tf_op jit(solution)/shard_map/ppermute | solution.py:751
  96.7 41.4 %collective-permute-start.14 = (bf16[512,1024]{1,0:T(8,128)(2,1)}, bf16[512,1024]{1,0:T(8,128)(2,1)}, u32[]{:S(2)}, u32[]{:S(2)}) collective-permute-start(bf16[512,1024]{1,0:T(8,128)(2,1)} %collective-permute-done.8.refs_7_), channel_id=1, source_target_pairs={{0,2},{2,0},{4,6},{6,4},{8,10},{10,8},{12,14},{14,12},{1,3},{3,1},... | collective-permute-start | bytes 3145736 | tf_op jit(solution)/shard_map/ppermute | solution.py:751
  99.2 38.4 %collective-permute-start.15 = (bf16[512,1024]{1,0:T(8,128)(2,1)}, bf16[512,1024]{1,0:T(8,128)(2,1)S(1)}, u32[]{:S(2)}, u32[]{:S(2)}) collective-permute-start(bf16[512,1024]{1,0:T(8,128)(2,1)} %collective-permute-done.8.refs_7_), channel_id=1, source_target_pairs={{0,16},{16,0},{1,17},{17,1},{2,18},{18,2},{3,19},{19,3},{4,20},{20... | collective-permute-start | bytes 3145736 | tf_op jit(solution)/shard_map/ppermute | solution.py:751
  137.6 50.5 %collective-permute-start.18 = (bf16[4,2,640,512]{3,2,1,0:T(8,128)(2,1)}, bf16[4,2,640,512]{3,2,1,0:T(8,128)(2,1)}, u32[]{:S(2)}, u32[]{:S(2)}) collective-permute-start(bf16[4,2,640,512]{3,2,1,0:T(8,128)(2,1)} %get-tuple-element.162.refs_2_), channel_id=1, source_target_pairs={{0,2},{2,0},{4,6},{6,4},{8,10},{10,8},{12,14},{14,12},{1,3},{3,1},... | collective-permute-start | bytes 15728648 | tf_op jit(solution)/shard_map/ppermute | solution.py:751
  167.1 35.1 %collective-permute-start.29 = (bf16[3,1024,128]{2,1,0:T(8,128)(2,1)S(1)}, bf16[3,1024,128]{2,1,0:T(8,128)(2,1)}, u32[]{:S(2)}, u32[]{:S(2)}) collective-permute-start(bf16[3,1024,128]{2,1,0:T(8,128)(2,1)S(1)} %constant_dynamic-slice_fusion.7), channel_id=1, source_target_pairs={{0,1},{1,0},{2,3},{3,2},{4,5},{5,4},{6,7},{7,6},{8,9},{9,8},{10,11... | collective-permute-start | bytes 2359304 | tf_op jit(solution)/shard_map/ppermute | solution.py:751
  168.1 34.6 %collective-permute-start.20 = (bf16[640,1024]{1,0:T(8,128)(2,1)S(1)}, bf16[640,1024]{1,0:T(8,128)(2,1)}, u32[]{:S(2)}, u32[]{:S(2)}) collective-permute-start(bf16[640,1024]{1,0:T(8,128)(2,1)S(1)} %bitcast.236), channel_id=1, source_target_pairs={{0,2},{2,0},{4,6},{6,4},{8,10},{10,8},{12,14},{14,12},{1,3},{3,1},... | collective-permute-start | bytes 3932168 | tf_op jit(solution)/shard_map/ppermute | solution.py:751
  169.3 46.3 %all-to-all-start.2 = ((bf16[8,2,40,1024]{3,2,1,0:T(8,128)(2,1)}), bf16[8,2,40,1024]{3,2,1,0:T(8,128)(2,1)S(1)}, u32[]{:S(2)}, u32[]{:S(2)}) async-start(bf16[8,2,40,1024]{3,2,1,0:T(8,128)(2,1)} %bitcast.242), calls=%async_computation.2 | async-start | bytes 2621440 | tf_op jit(solution)/shard_map/all_to_all | solution.py:919
  187.5 47.1 %collective-permute-start.22 = (bf16[640,1024]{1,0:T(8,128)(2,1)}, bf16[640,1024]{1,0:T(8,128)(2,1)}, u32[]{:S(2)}, u32[]{:S(2)}) collective-permute-start(bf16[640,1024]{1,0:T(8,128)(2,1)} %get-tuple-element.185.refs_0_), channel_id=1, source_target_pairs={{0,2},{2,0},{4,6},{6,4},{8,10},{10,8},{12,14},{14,12},{1,3},{3,1},... | collective-permute-start | bytes 3932168 | tf_op jit(solution)/shard_map/ppermute | solution.py:751
  201.0 47.9 %collective-permute-start.23 = (bf16[2,4,128,1024]{3,2,1,0:T(8,128)(2,1)}, bf16[2,4,128,1024]{3,2,1,0:T(8,128)(2,1)}, u32[]{:S(2)}, u32[]{:S(2)}) collective-permute-start(bf16[2,4,128,1024]{3,2,1,0:T(8,128)(2,1)} %get-tuple-element.184), channel_id=1, source_target_pairs={{0,1},{1,0},{2,3},{3,2},{4,5},{5,4},{6,7},{7,6},{8,9},{9,8},{10,11... | collective-permute-start | bytes 6291464 | tf_op jit(solution)/shard_map/ppermute | solution.py:751
  216.0 58.7 %collective-permute-start.28 = (bf16[2,4,128,1024]{3,2,1,0:T(8,128)(2,1)}, bf16[2,4,128,1024]{3,2,1,0:T(8,128)(2,1)}, u32[]{:S(2)}, u32[]{:S(2)}) collective-permute-start(bf16[2,4,128,1024]{3,2,1,0:T(8,128)(2,1)} %get-tuple-element.195), channel_id=1, source_target_pairs={{0,16},{16,0},{1,17},{17,1},{2,18},{18,2},{3,19},{19,3},{4,20},{20... | collective-permute-start | bytes 6291464 | tf_op jit(solution)/shard_map/ppermute | solution.py:751
  237.8 68.4 %all-to-all-start.3 = ((bf16[8,2,40,1024]{3,2,1,0:T(8,128)(2,1)}), bf16[8,2,40,1024]{3,2,1,0:T(8,128)(2,1)S(1)}, u32[]{:S(2)}, u32[]{:S(2)}) async-start(bf16[8,2,40,1024]{3,2,1,0:T(8,128)(2,1)} %bitcast.240), calls=%async_computation.3 | async-start | bytes 2621440 | tf_op jit(solution)/shard_map/all_to_all | solution.py:919
  264.0 60.1 %collective-permute-start.35 = (bf16[4,128,1024]{2,1,0:T(8,128)(2,1)}, bf16[4,128,1024]{2,1,0:T(8,128)(2,1)}, u32[]{:S(2)}, u32[]{:S(2)}) collective-permute-start(bf16[4,128,1024]{2,1,0:T(8,128)(2,1)} %get-tuple-element.321), channel_id=1, source_target_pairs={{0,16},{16,0},{1,17},{17,1},{2,18},{18,2},{3,19},{19,3},{4,20},{20... | collective-permute-start | bytes 3145736 | tf_op jit(solution)/shard_map/ppermute | solution.py:751
  280.8 46.0 %collective-permute-start.36 = (bf16[4,128,1024]{2,1,0:T(8,128)(2,1)}, bf16[4,128,1024]{2,1,0:T(8,128)(2,1)}, u32[]{:S(2)}, u32[]{:S(2)}) collective-permute-start(bf16[4,128,1024]{2,1,0:T(8,128)(2,1)} %get-tuple-element.319), channel_id=1, source_target_pairs={{0,1},{1,0},{2,3},{3,2},{4,5},{5,4},{6,7},{7,6},{8,9},{9,8},{10,11... | collective-permute-start | bytes 3145736 | tf_op jit(solution)/shard_map/ppermute | solution.py:751
  295.2 53.3 %collective-permute-start.44 = (bf16[2,1,640,256]{3,2,1,0:T(8,128)(2,1)}, bf16[2,1,640,256]{3,2,1,0:T(8,128)(2,1)}, u32[]{:S(2)}, u32[]{:S(2)}) collective-permute-start(bf16[2,1,640,256]{3,2,1,0:T(8,128)(2,1)} %bitcast.57.refs_6_), channel_id=1, source_target_pairs={{0,2},{2,0},{4,6},{6,4},{8,10},{10,8},{12,14},{14,12},{1,3},{3,1},... | collective-permute-start | bytes 1966088 | tf_op jit(solution)/shard_map/ppermute | solution.py:751
  303.3 45.7 %collective-permute-start.46 = (bf16[2,1,640,256]{3,2,1,0:T(8,128)(2,1)}, bf16[2,1,640,256]{3,2,1,0:T(8,128)(2,1)}, u32[]{:S(2)}, u32[]{:S(2)}) collective-permute-start(bf16[2,1,640,256]{3,2,1,0:T(8,128)(2,1)} %bitcast.262), channel_id=1, source_target_pairs={{0,2},{2,0},{4,6},{6,4},{8,10},{10,8},{12,14},{14,12},{1,3},{3,1},... | collective-permute-start | bytes 1966088 | tf_op jit(solution)/shard_map/ppermute | solution.py:751
  330.9 41.4 %collective-permute-start.43 = (bf16[2,3,640,256]{3,2,1,0:T(8,128)(2,1)S(1)}, bf16[2,3,640,256]{3,2,1,0:T(8,128)(2,1)}, u32[]{:S(2)}, u32[]{:S(2)}) collective-permute-start(bf16[2,3,640,256]{3,2,1,0:T(8,128)(2,1)S(1)} %copy-done.3), channel_id=1, source_target_pairs={{0,2},{2,0},{4,6},{6,4},{8,10},{10,8},{12,14},{14,12},{1,3},{3,1},... | collective-permute-start | bytes 5898248 | tf_op jit(solution)/shard_map/ppermute | solution.py:751
  368.3 55.0 %collective-permute-start.53 = (bf16[2,128,1024]{2,1,0:T(8,128)(2,1)}, bf16[2,128,1024]{2,1,0:T(8,128)(2,1)}, u32[]{:S(2)}, u32[]{:S(2)}) collective-permute-start(bf16[2,128,1024]{2,1,0:T(8,128)(2,1)} %get-tuple-element.316), channel_id=1, source_target_pairs={{0,12},{2,14},{4,8},{6,10},{8,4},{10,6},{12,0},{14,2},{1,13},{3,15... | collective-permute-start | bytes 1572872 | tf_op jit(solution)/shard_map/ppermute | solution.py:751
  372.3 57.6 %collective-permute-start.52 = (bf16[2,128,1024]{2,1,0:T(8,128)(2,1)}, bf16[2,128,1024]{2,1,0:T(8,128)(2,1)}, u32[]{:S(2)}, u32[]{:S(2)}) collective-permute-start(bf16[2,128,1024]{2,1,0:T(8,128)(2,1)} %get-tuple-element.317), channel_id=1, source_target_pairs={{0,8},{2,10},{4,12},{6,14},{8,0},{10,2},{12,4},{14,6},{1,9},{3,11}... | collective-permute-start | bytes 1572872 | tf_op jit(solution)/shard_map/ppermute | solution.py:751
  395.2 35.6 %collective-permute-start.51 = (bf16[2,128,1024]{2,1,0:T(8,128)(2,1)}, bf16[2,128,1024]{2,1,0:T(8,128)(2,1)S(1)}, u32[]{:S(2)}, u32[]{:S(2)}) collective-permute-start(bf16[2,128,1024]{2,1,0:T(8,128)(2,1)} %get-tuple-element.315), channel_id=1, source_target_pairs={{0,4},{2,6},{4,0},{6,2},{8,12},{10,14},{12,8},{14,10},{1,5},{3,7},... | collective-permute-start | bytes 1572872 | tf_op jit(solution)/shard_map/ppermute | solution.py:751
  408.4 38.9 %collective-permute-start.61 = (bf16[2,128,512]{2,1,0:T(8,128)(2,1)}, bf16[2,128,512]{2,1,0:T(8,128)(2,1)}, u32[]{:S(2)}, u32[]{:S(2)}) collective-permute-start(bf16[2,128,512]{2,1,0:T(8,128)(2,1)} %get-tuple-element.328), channel_id=1, source_target_pairs={{0,12},{2,14},{4,8},{6,10},{8,4},{10,6},{12,0},{14,2},{1,13},{3,15... | collective-permute-start | bytes 786440 | tf_op jit(solution)/shard_map/ppermute | solution.py:751
  (92 other events, 1245.2 us)

commit v6 on v5

--- a/solution.py
+++ b/solution.py
@@ -237,6 +237,9 @@
 
 
 def stream_weights(own_qkv, own_out, qkv_slots, out_slots, wq, wo, sems, step, steps, first=0):
+    def out_at(slot, index):
+        return slot if wo.shape[0] == 2 else index
+
     def start(index, slot):
         for s in range(steps):
 
@@ -246,7 +249,7 @@
                     cols = pl.ds((s + first) * BLOCK, BLOCK)
                     pltpu.make_async_copy(own_qkv.at[:, :, cols], wq.at[slot], sems.at[slot, 0]).start()
                     if wo is not None:
-                        pltpu.make_async_copy(own_out.at[cols, :], wo.at[slot], sems.at[slot, 1]).start()
+                        pltpu.make_async_copy(own_out.at[cols, :], wo.at[out_at(slot, s)], sems.at[slot, 1]).start()
                 else:
                     for i in range(2):
                         part = 2 * (s + first - 2) + i
@@ -258,13 +261,13 @@
                             continue
                         if out_slots is not None:
                             pltpu.make_async_copy(
-                                out_slots[part], wo.at[slot, cols, :], sems.at[slot, 1]
+                                out_slots[part], wo.at[out_at(slot, s), cols, :], sems.at[slot, 1]
                             ).start()
                             continue
                         for j in range(wo.shape[2] // PAIR):
                             place = pl.ds(j * PAIR, PAIR)
                             pltpu.make_async_copy(
-                                qkv_slots[part].at[3, place, :], wo.at[slot, cols, place], sems.at[slot, 1]
+                                qkv_slots[part].at[3, place, :], wo.at[out_at(slot, s), cols, place], sems.at[slot, 1]
                             ).start()
 
     slot = step % 2
@@ -279,7 +282,7 @@
 
     pltpu.make_async_copy(wq.at[slot], wq.at[slot], sems.at[slot, 0]).wait()
     if wo is not None:
-        pltpu.make_async_copy(wo.at[slot], wo.at[slot], sems.at[slot, 1]).wait()
+        pltpu.make_async_copy(wo.at[0], wo.at[0], sems.at[slot, 1]).wait()
     return slot
 
 
@@ -345,7 +348,7 @@
 
 
 def time_kernel(groups, mid_ref, gain_ref, wq_any, wo_any, q0, q1, q2, q3,
-                late_ref, normed_ref, heads_ref, proj_ref, logs_ref, acc, wq, wo, sems):
+                late_ref, normed_ref, heads_ref, proj_ref, logs_ref, acc, wq, wo, sems, joined):
     step = pl.program_id(0)
     rows = mid_ref.shape[0]
 
@@ -360,11 +363,16 @@
     slot = stream_weights(wq_any, wo_any, (q0, q1, q2, q3), None, wq, wo, sems, step, 4)
     project_block(normed_ref, lambda i: wq[slot, i], proj_ref.at[0])
     attend_block(groups, proj_ref.at[0], heads_ref.at[0], logs_ref.at[0])
-    acc[...] += dot_n(heads_ref[0], wo[slot])
+    for s in range(4):
+
+        @pl.when(step == s)
+        def _(s=s):
+            joined[:, s * BLOCK : (s + 1) * BLOCK] = heads_ref[0]
 
     @pl.when(step == 3)
     def _():
-        late_ref[...] = acc[...].astype(BF)
+        weight = wo[...].reshape(4 * BLOCK, wo.shape[2])
+        late_ref[...] = (acc[...] + dot_n(joined[...], weight)).astype(BF)
 
 
 def time_forward(middle, gain, qkv, out, slots, groups):
@@ -390,8 +398,9 @@
         scratch_shapes=[
             pltpu.VMEM((rows, depth), F32),
             pltpu.VMEM((2, 3, depth, BLOCK), BF),
-            pltpu.VMEM((2, BLOCK, depth), BF),
+            pltpu.VMEM((4, BLOCK, depth), BF),
             pltpu.SemaphoreType.DMA((2, 2)),
+            pltpu.VMEM((rows, 4 * BLOCK), BF),
         ],
         compiler_params=params(),
         cost_estimate=cost("time_forward"),

time: 501 us -> 501 us (level)
  no operation moved by 1% of the time
where the time goes in v6:
time: 501 us; the launch traced here: 492 us
  Pallas kernels  221 us (44%)
  waiting for transfers between devices  93.5 us (19%)
  starting transfers between devices  87.5 us (17%)
  other arithmetic  51.6 us (10%)
  local copies, waits for them, and re-layouts  35.7 us (7%)
    ppermute x68, waiting for transfers between devices, swap(): lax.ppermute(value, axis, [(i, i ^ step) for i in range(sizes[axis])])  93.5 us
    ppermute x68, starting transfers between devices, swap(): lax.ppermute(value, axis, [(i, i ^ step) for i in range(sizes[axis])])  66.7 us
    pallas_call x6, Pallas kernels, grad_product(): pl.pallas_call(partial(grad_kernel, chunk, y_first, [term[0] for term in...  63.7 us
    pallas_call x4, Pallas kernels, branch_back(): pl.pallas_call(partial(back_kernel, groups, segments, sums, final, len(we...  59.1 us
    pallas_call x2, Pallas kernels, feed_forward(): pl.pallas_call(partial(ffn_kernel, final), grid=(4,), in_specs=[whole(row...  39.9 us
    all_to_all x4, starting transfers between devices, exchange(): lax.all_to_all(packed, 'wide', split_axis=0, concat_axis=0, tiled=True)  20.8 us
    pallas_call x2, Pallas kernels, space_heads(): pl.pallas_call(partial(space_kernel, groups, full), grid_spec=pltpu.Prefe...  16.4 us
    pallas_call x1, Pallas kernels, time_forward(): pl.pallas_call(partial(time_kernel, groups), grid=(4,), in_specs=[whole(r...  15.8 us
  transfers between devices with their start and end apart: 72, of which 18 were waited for; matrix products, arithmetic and copies ran while one was open for 16% of the time, Pallas kernels for 45%

profile of v6, /device:TPU:0, one launch (start us, length us, event | category | flops | bytes accessed | tf_op | source)
XLA Modules:
  0.0 492.5 jit_solution(7944762835927526958)
XLA Ops:
  18.1 7.6 %space_partner.1 = bf16[2,640,256]{2,1,0:T(8,128)(2,1)} custom-call(s32[1]{0:T(128)S(6)} %sub.11._, bf16[2,2,256,1024]{3,2,1,0:T(8,128)(2,1)} %fa_ref.3, bf16[2,2,64,1024]{3,2,1,0:T(8,128)(2,1)} %fb_ref.3, f32[2,4,1024]{2,1,0:T(4,128)} %fusion.23.shift_ref, f32[1,1024]{1,0:T(1,128)} %bitcast.272, bf16[3,1024,512]{2,1,0:T(8,128)(2,1)} %refs_0_.5), custom_call_target="tpu_custom_call" | custom-call | flops 8000000000 | bytes 1048576 | tf_op jit(solution)/shard_map/space_partner/pallas_call | solution.py:217
  28.6 8.8 %space_own.1 = (bf16[2,640,256]{2,1,0:T(8,128)(2,1)}, bf16[2,3,640,256]{3,2,1,0:T(8,128)(2,1)}, f32[2,8,640]{2,1,0:T(8,128)}, f32[640,1024]{1,0:T(8,128)}, bf16[640,1024]{1,0:T(8,128)(2,1)}) custom-call(s32[1]{0:T(128)} %bitcast.3._, bf16[2,2,256,1024]{3,2,1,0:T(8,128)(2,1)} %fa_ref.3, bf16[2,2,64,1024]{3,2,1,0:T(8,128)(2,1)} %fb_ref.3, ...), custom_call_target="tpu_custom_call" | custom-call | flops 8000000000 | bytes 1048576 | tf_op jit(solution)/shard_map/space_own/pallas_call | solution.py:217
  78.3 14.8 %collective-permute-done.6.q2.refs_5_ = bf16[4,1024,128]{2,1,0:T(8,128)(2,1)} collective-permute-done((bf16[4,1024,128]{2,1,0:T(8,128)(2,1)}, bf16[4,1024,128]{2,1,0:T(8,128)(2,1)}, u32[]{:S(2)}, u32[]{:S(2)}) %collective-permute-start.6) | collective-permute-done | bytes 1048608 | tf_op jit(solution)/shard_map/ppermute | solution.py:760
  101.5 15.8 %time_forward.1 = (bf16[640,1024]{1,0:T(8,128)(2,1)}, bf16[640,1024]{1,0:T(8,128)(2,1)}, bf16[4,640,256]{2,1,0:T(8,128)(2,1)}, bf16[4,3,640,256]{3,2,1,0:T(8,128)(2,1)}, f32[4,8,640]{2,1,0:T(8,128)}) custom-call(bf16[640,1024]{1,0:T(8,128)(2,1)} %bitcast.237, f32[1,1024]{1,0:T(1,128)} %bitcast.268, bf16[3,1024,512]{2,1,0:T(8,128)(2,1)} %refs_0_.4, ...), custom_call_target="tpu_custom_call" | custom-call | flops 44810600448 | bytes 1048576 | tf_op jit(solution)/shard_map/time_forward/pallas_call | solution.py:380
  118.5 18.2 %feed_forward.1 = (bf16[640,1024]{1,0:T(8,128)(2,1)}, bf16[4,2,640,512]{3,2,1,0:T(8,128)(2,1)}, f32[640,1024]{1,0:T(8,128)}, f32[640,1024]{1,0:T(8,128)}) custom-call(bf16[640,1024]{1,0:T(8,128)(2,1)} %get-tuple-element.157.late_ref, bf16[640,1024]{1,0:T(8,128)(2,1)} %bitcast.233, f32[1,1024]{1,0:T(1,128)} %bitcast.270, bf16[1024,2048]{1,0:T(8,128)(2,1)} %refs_0_.3, ...), custom_call_target="tpu_custom_call" | custom-call | flops 15121899520 | bytes 1048576 | tf_op jit(solution)/shard_map/feed_forward/pallas_call | solution.py:511
  143.4 21.8 %feed_forward_end.1 = (bf16[640,1024]{1,0:T(8,128)(2,1)}, bf16[640,1024]{1,0:T(8,128)(2,1)}, bf16[4,2,640,512]{3,2,1,0:T(8,128)(2,1)}, f32[1,1024]{1,0:T(1,128)}) custom-call(bf16[640,1024]{1,0:T(8,128)(2,1)} %get-tuple-element.157.late_ref, bf16[640,1024]{1,0:T(8,128)(2,1)} %bitcast.234, f32[1,1024]{1,0:T(1,128)} %bitcast.271, ...), custom_call_target="tpu_custom_call" | custom-call | flops 15121899520 | bytes 1048576 | tf_op jit(solution)/shard_map/feed_forward_end/pallas_call | solution.py:511
  174.6 12.7 %time_back.1 = (f32[640,1024]{1,0:T(8,128)}, bf16[2,3,640,256]{3,2,1,0:T(8,128)(2,1)}) custom-call(bf16[640,1024]{1,0:T(8,128)(2,1)} %get-tuple-element.190.dy_ref.refs_2_, bf16[4,3,640,256]{3,2,1,0:T(8,128)(2,1)} %get-tuple-element.168.proj_any, f32[4,8,640]{2,1,0:T(8,128)} %get-tuple-element.169.logs_any, bf16[3,1024,512]{2,1,0:T(8,128)(2,1)} %refs_0_.4, ...), custom_call_target="tpu_custom_call" | custom-call | flops 11333900288 | bytes 1048576 | tf_op jit(solution)/shard_map/time_back/pallas_call | solution.py:624
  187.9 13.0 %grad_product.6 = (bf16[2,4,128,1024]{3,2,1,0:T(8,128)(2,1)}, bf16[2,4,128,1024]{3,2,1,0:T(8,128)(2,1)}) custom-call(s32[3]{0:T(128)} %pad_add_fusion.1.bits_ref, bf16[640,1024]{1,0:T(8,128)(2,1)} %get-tuple-element.172.refs_0_, bf16[640,1024]{1,0:T(8,128)(2,1)} %collective-permute-done.17.refs_1_, bf16[4,2,640,512]{3,2,1,0:T(8,128)(2,1)} %get-tuple-element.162.refs_2_, ...), custom_call_target="tpu_custom_call" | custom-call | flops 12840999936 | bytes 1048576 | tf_op jit(solution)/shard_map/grad_product/pallas_call | solution.py:733
  202.7 13.0 %grad_product.7 = (bf16[2,4,128,1024]{3,2,1,0:T(8,128)(2,1)}, bf16[2,4,128,1024]{3,2,1,0:T(8,128)(2,1)}) custom-call(s32[3]{0:T(128)} %pad_add_fusion.1.bits_ref, bf16[640,1024]{1,0:T(8,128)(2,1)} %bitcast.235, bf16[640,1024]{1,0:T(8,128)(2,1)} %collective-permute-done.20.refs_1_, bf16[4,2,640,512]{3,2,1,0:T(8,128)(2,1)} %get-tuple-element.162.refs_2_, ...), custom_call_target="tpu_custom_call" | custom-call | flops 574899968 | bytes 1048576 | tf_op jit(solution)/shard_map/grad_product/pallas_call | solution.py:733
  218.6 15.8 %time_back_end.1 = (bf16[640,1024]{1,0:T(8,128)(2,1)}, bf16[2,3,640,256]{3,2,1,0:T(8,128)(2,1)}, f32[1,1024]{1,0:T(1,128)}, f32[8,1024]{1,0:T(8,128)}) custom-call(bf16[640,1024]{1,0:T(8,128)(2,1)} %get-tuple-element.190.dy_ref.refs_2_, bf16[4,3,640,256]{3,2,1,0:T(8,128)(2,1)} %get-tuple-element.168.proj_any, f32[4,8,640]{2,1,0:T(8,128)} %get-tuple-element.169.logs_any, ...), custom_call_target="tpu_custom_call" | custom-call | flops 852000000 | bytes 1048576 | tf_op jit(solution)/shard_map/time_back_end/pallas_call | solution.py:624
  242.5 6.3 %collective-permute-done.23 = bf16[2,4,128,1024]{3,2,1,0:T(8,128)(2,1)} collective-permute-done((bf16[2,4,128,1024]{3,2,1,0:T(8,128)(2,1)}, bf16[2,4,128,1024]{3,2,1,0:T(8,128)(2,1)}, u32[]{:S(2)}, u32[]{:S(2)}) %collective-permute-start.23) | collective-permute-done | bytes 2097184 | tf_op jit(solution)/shard_map/ppermute | solution.py:760
  255.0 8.9 %grad_product.8 = (bf16[2,4,128,512]{3,2,1,0:T(8,128)(2,1)}, bf16[2,4,128,512]{3,2,1,0:T(8,128)(2,1)}) custom-call(s32[3]{0:T(128)} %pad_add_fusion.1.bits_ref, bf16[640,1024]{1,0:T(8,128)(2,1)} %get-tuple-element.185.refs_0_, bf16[640,1024]{1,0:T(8,128)(2,1)} %collective-permute-done.22.refs_1_, ...), custom_call_target="tpu_custom_call" | custom-call | flops 115100000 | bytes 1048576 | tf_op jit(solution)/shard_map/grad_product/pallas_call | solution.py:733
  264.7 10.0 %grad_product.9 = (bf16[2,4,128,512]{3,2,1,0:T(8,128)(2,1)}, bf16[2,4,128,512]{3,2,1,0:T(8,128)(2,1)}) custom-call(s32[3]{0:T(128)} %pad_add_fusion.1.bits_ref, bf16[640,1024]{1,0:T(8,128)(2,1)} %get-tuple-element.185.refs_0_, bf16[640,1024]{1,0:T(8,128)(2,1)} %collective-permute-done.22.refs_1_, bf16[640,1024]{1,0:T(8,128)(2,1)} %get-tuple-element.190.dy_ref.refs_2_, ...), custom_call_target="tpu_custom_call" | custom-call | flops 626899968 | bytes 1048576 | tf_op jit(solution)/shard_map/grad_product/pallas_call | solution.py:733
  286.3 7.7 %space_rest.1 = (bf16[2,640,256]{2,1,0:T(8,128)(2,1)}, bf16[2,3,640,256]{3,2,1,0:T(8,128)(2,1)}, f32[2,8,640]{2,1,0:T(8,128)}) custom-call(bf16[640,1024]{1,0:T(8,128)(2,1)} %get-tuple-element.232.normed_ref.refs_0_, bf16[3,1024,128]{2,1,0:T(8,128)(2,1)} %collective-permute-done.29.q0.refs_3_, bf16[3,1024,128]{2,1,0:T(8,128)(2,1)} %collective-permute-done.30.q1.refs_4_, ...), custom_call_target="tpu_custom_call" | custom-call | flops 1031000000 | bytes 1048576 | tf_op jit(solution)/shard_map/space_rest/pallas_call | solution.py:297
  295.0 8.0 %collective-permute-done.33 = bf16[2,4,128,512]{3,2,1,0:T(8,128)(2,1)} collective-permute-done((bf16[2,4,128,512]{3,2,1,0:T(8,128)(2,1)}, bf16[2,4,128,512]{3,2,1,0:T(8,128)(2,1)}, u32[]{:S(2)}, u32[]{:S(2)}) %collective-permute-start.33) | collective-permute-done | bytes 1048608 | tf_op jit(solution)/shard_map/ppermute | solution.py:760
  307.3 13.7 %space_back.1 = (f32[640,1024]{1,0:T(8,128)}, bf16[2,3,640,256]{3,2,1,0:T(8,128)(2,1)}) custom-call(bf16[640,1024]{1,0:T(8,128)(2,1)} %pad_maximum_fusion.2.dy_ref.refs_2_, bf16[2,3,640,256]{3,2,1,0:T(8,128)(2,1)} %get-tuple-element.209.proj_any, f32[2,8,640]{2,1,0:T(8,128)} %get-tuple-element.210.logs_any, bf16[3,1024,512]{2,1,0:T(8,128)(2,1)} %refs_0_.5, ...), custom_call_target="tpu_custom_call" | custom-call | flops 6081099776 | bytes 1048576 | tf_op jit(solution)/shard_map/space_back/pallas_call | solution.py:624
  331.2 16.9 %space_back_end.1 = (bf16[640,1024]{1,0:T(8,128)(2,1)}, bf16[2,3,640,256]{3,2,1,0:T(8,128)(2,1)}, f32[1,1024]{1,0:T(1,128)}, f32[8,1024]{1,0:T(8,128)}) custom-call(bf16[640,1024]{1,0:T(8,128)(2,1)} %pad_maximum_fusion.2.dy_ref.refs_2_, bf16[2,3,640,256]{3,2,1,0:T(8,128)(2,1)} %get-tuple-element.207.proj_any, f32[2,8,640]{2,1,0:T(8,128)} %get-tuple-element.208.logs_any, ...), custom_call_target="tpu_custom_call" | custom-call | flops 30433099776 | bytes 1048576 | tf_op jit(solution)/shard_map/space_back_end/pallas_call | solution.py:624
  353.3 9.6 %collective-permute-done.40 = bf16[4,128,512]{2,1,0:T(8,128)(2,1)} collective-permute-done((bf16[4,128,512]{2,1,0:T(8,128)(2,1)}, bf16[4,128,512]{2,1,0:T(8,128)(2,1)}, u32[]{:S(2)}, u32[]{:S(2)}) %collective-permute-start.40) | collective-permute-done | bytes 524320 | tf_op jit(solution)/shard_map/ppermute | solution.py:760
  372.6 9.9 %grad_product.10 = (bf16[2,4,128,512]{3,2,1,0:T(8,128)(2,1)}, bf16[2,4,128,512]{3,2,1,0:T(8,128)(2,1)}) custom-call(s32[3]{0:T(128)} %pad_add_fusion.1.bits_ref, bf16[640,1024]{1,0:T(8,128)(2,1)} %get-tuple-element.232.normed_ref.refs_0_, bf16[640,1024]{1,0:T(8,128)(2,1)} %collective-permute-done.41.refs_1_, ...), custom_call_target="tpu_custom_call" | custom-call | flops 351700000 | bytes 1048576 | tf_op jit(solution)/shard_map/grad_product/pallas_call | solution.py:733
  384.8 8.9 %grad_product.11 = (bf16[2,4,128,512]{3,2,1,0:T(8,128)(2,1)}, bf16[2,4,128,512]{3,2,1,0:T(8,128)(2,1)}) custom-call(s32[3]{0:T(128)} %pad_add_fusion.1.bits_ref, bf16[640,1024]{1,0:T(8,128)(2,1)} %get-tuple-element.232.normed_ref.refs_0_, bf16[640,1024]{1,0:T(8,128)(2,1)} %collective-permute-done.41.refs_1_, ...), custom_call_target="tpu_custom_call" | custom-call | flops 1624000000 | bytes 1048576 | tf_op jit(solution)/shard_map/grad_product/pallas_call | solution.py:733
  402.0 6.2 %collective-permute-done.49 = bf16[2,4,128,512]{3,2,1,0:T(8,128)(2,1)S(1)} collective-permute-done((bf16[2,4,128,512]{3,2,1,0:T(8,128)(2,1)}, bf16[2,4,128,512]{3,2,1,0:T(8,128)(2,1)S(1)}, u32[]{:S(2)}, u32[]{:S(2)}) %collective-permute-start.49) | collective-permute-done | bytes 1048608 | tf_op jit(solution)/shard_map/ppermute | solution.py:760
  411.2 9.2 %collective-permute-done.50 = bf16[2,4,128,512]{3,2,1,0:T(8,128)(2,1)S(1)} collective-permute-done((bf16[2,4,128,512]{3,2,1,0:T(8,128)(2,1)}, bf16[2,4,128,512]{3,2,1,0:T(8,128)(2,1)S(1)}, u32[]{:S(2)}, u32[]{:S(2)}) %collective-permute-start.50) | collective-permute-done | bytes 1048608 | tf_op jit(solution)/shard_map/ppermute | solution.py:760
  435.4 8.1 %collective-permute-done.55 = bf16[4,128,512]{2,1,0:T(8,128)(2,1)S(1)} collective-permute-done((bf16[4,128,512]{2,1,0:T(8,128)(2,1)S(1)}, bf16[4,128,512]{2,1,0:T(8,128)(2,1)S(1)}, u32[]{:S(2)}, u32[]{:S(2)}) %collective-permute-start.55) | collective-permute-done | bytes 524320 | tf_op jit(solution)/shard_map/ppermute | solution.py:760
  466.9 8.2 %collective-permute-start.57 = (f32[11,128]{1,0:T(8,128)}, f32[11,128]{1,0:T(8,128)}, u32[]{:S(2)}, u32[]{:S(2)}) collective-permute-start(f32[11,128]{1,0:T(8,128)} %bitcast.229), channel_id=1, source_target_pairs={{0,8},{2,10},{4,12},{6,14},{8,0},{10,2},{12,4},{14,6},{1,9},{3,11}... | collective-permute-start | bytes 16904 | tf_op jit(solution)/shard_map/ppermute | solution.py:760
  (329 shorter events, 217.8 us)
Async XLA Ops:
  8.4 58.4 %collective-permute-start.5 = (bf16[4,1024,128]{2,1,0:T(8,128)(2,1)}, bf16[4,1024,128]{2,1,0:T(8,128)(2,1)}, u32[]{:S(2)}, u32[]{:S(2)}) collective-permute-start(bf16[4,1024,128]{2,1,0:T(8,128)(2,1)} %pad_maximum_fusion.3), channel_id=1, source_target_pairs={{0,1},{1,0},{2,3},{3,2},{4,5},{5,4},{6,7},{7,6},{8,9},{9,8},{10,11... | collective-permute-start | bytes 3145736 | tf_op jit(solution)/shard_map/ppermute | solution.py:760
  9.9 50.6 %all-to-all-start = ((bf16[8,2,40,1024]{3,2,1,0:T(8,128)(2,1)}), bf16[8,2,40,1024]{3,2,1,0:T(8,128)(2,1)S(1)}, u32[]{:S(2)}, u32[]{:S(2)}) async-start(bf16[8,2,40,1024]{3,2,1,0:T(8,128)(2,1)} %copy.83), calls=%async_computation | async-start | bytes 2621440 | tf_op jit(solution)/shard_map/all_to_all | solution.py:928
  60.5 37.5 %all-to-all-start.1 = ((bf16[8,2,40,1024]{3,2,1,0:T(8,128)(2,1)}), bf16[8,2,40,1024]{3,2,1,0:T(8,128)(2,1)S(1)}, u32[]{:S(2)}, u32[]{:S(2)}) async-start(bf16[8,2,40,1024]{3,2,1,0:T(8,128)(2,1)} %copy_bitcast_fusion), calls=%async_computation.1 | async-start | bytes 2621440 | tf_op jit(solution)/shard_map/all_to_all | solution.py:928
  75.0 63.1 %collective-permute-start.11 = (bf16[1024,512]{1,0:T(8,128)(2,1)}, bf16[1024,512]{1,0:T(8,128)(2,1)}, u32[]{:S(2)}, u32[]{:S(2)}) collective-permute-start(bf16[1024,512]{1,0:T(8,128)(2,1)} %collective-permute-done.7.refs_3_), channel_id=1, source_target_pairs={{0,2},{2,0},{4,6},{6,4},{8,10},{10,8},{12,14},{14,12},{1,3},{3,1},... | collective-permute-start | bytes 3145736 | tf_op jit(solution)/shard_map/ppermute | solution.py:760
  75.5 61.2 %collective-permute-start.12 = (bf16[1024,512]{1,0:T(8,128)(2,1)}, bf16[1024,512]{1,0:T(8,128)(2,1)}, u32[]{:S(2)}, u32[]{:S(2)}) collective-permute-start(bf16[1024,512]{1,0:T(8,128)(2,1)} %collective-permute-done.7.refs_3_), channel_id=1, source_target_pairs={{0,16},{16,0},{1,17},{17,1},{2,18},{18,2},{3,19},{19,3},{4,20},{20... | collective-permute-start | bytes 3145736 | tf_op jit(solution)/shard_map/ppermute | solution.py:760
  96.7 41.4 %collective-permute-start.14 = (bf16[512,1024]{1,0:T(8,128)(2,1)}, bf16[512,1024]{1,0:T(8,128)(2,1)}, u32[]{:S(2)}, u32[]{:S(2)}) collective-permute-start(bf16[512,1024]{1,0:T(8,128)(2,1)} %collective-permute-done.8.refs_7_), channel_id=1, source_target_pairs={{0,2},{2,0},{4,6},{6,4},{8,10},{10,8},{12,14},{14,12},{1,3},{3,1},... | collective-permute-start | bytes 3145736 | tf_op jit(solution)/shard_map/ppermute | solution.py:760
  99.2 38.4 %collective-permute-start.15 = (bf16[512,1024]{1,0:T(8,128)(2,1)}, bf16[512,1024]{1,0:T(8,128)(2,1)S(1)}, u32[]{:S(2)}, u32[]{:S(2)}) collective-permute-start(bf16[512,1024]{1,0:T(8,128)(2,1)} %collective-permute-done.8.refs_7_), channel_id=1, source_target_pairs={{0,16},{16,0},{1,17},{17,1},{2,18},{18,2},{3,19},{19,3},{4,20},{20... | collective-permute-start | bytes 3145736 | tf_op jit(solution)/shard_map/ppermute | solution.py:760
  137.6 50.3 %collective-permute-start.18 = (bf16[4,2,640,512]{3,2,1,0:T(8,128)(2,1)}, bf16[4,2,640,512]{3,2,1,0:T(8,128)(2,1)}, u32[]{:S(2)}, u32[]{:S(2)}) collective-permute-start(bf16[4,2,640,512]{3,2,1,0:T(8,128)(2,1)} %get-tuple-element.162.refs_2_), channel_id=1, source_target_pairs={{0,2},{2,0},{4,6},{6,4},{8,10},{10,8},{12,14},{14,12},{1,3},{3,1},... | collective-permute-start | bytes 15728648 | tf_op jit(solution)/shard_map/ppermute | solution.py:760
  166.9 35.1 %collective-permute-start.29 = (bf16[3,1024,128]{2,1,0:T(8,128)(2,1)S(1)}, bf16[3,1024,128]{2,1,0:T(8,128)(2,1)}, u32[]{:S(2)}, u32[]{:S(2)}) collective-permute-start(bf16[3,1024,128]{2,1,0:T(8,128)(2,1)S(1)} %constant_dynamic-slice_fusion.7), channel_id=1, source_target_pairs={{0,1},{1,0},{2,3},{3,2},{4,5},{5,4},{6,7},{7,6},{8,9},{9,8},{10,11... | collective-permute-start | bytes 2359304 | tf_op jit(solution)/shard_map/ppermute | solution.py:760
  169.2 46.5 %all-to-all-start.2 = ((bf16[8,2,40,1024]{3,2,1,0:T(8,128)(2,1)}), bf16[8,2,40,1024]{3,2,1,0:T(8,128)(2,1)S(1)}, u32[]{:S(2)}, u32[]{:S(2)}) async-start(bf16[8,2,40,1024]{3,2,1,0:T(8,128)(2,1)} %bitcast.242), calls=%async_computation.2 | async-start | bytes 2621440 | tf_op jit(solution)/shard_map/all_to_all | solution.py:928
  187.3 47.1 %collective-permute-start.22 = (bf16[640,1024]{1,0:T(8,128)(2,1)}, bf16[640,1024]{1,0:T(8,128)(2,1)}, u32[]{:S(2)}, u32[]{:S(2)}) collective-permute-start(bf16[640,1024]{1,0:T(8,128)(2,1)} %get-tuple-element.185.refs_0_), channel_id=1, source_target_pairs={{0,2},{2,0},{4,6},{6,4},{8,10},{10,8},{12,14},{14,12},{1,3},{3,1},... | collective-permute-start | bytes 3932168 | tf_op jit(solution)/shard_map/ppermute | solution.py:760
  200.9 47.9 %collective-permute-start.23 = (bf16[2,4,128,1024]{3,2,1,0:T(8,128)(2,1)}, bf16[2,4,128,1024]{3,2,1,0:T(8,128)(2,1)}, u32[]{:S(2)}, u32[]{:S(2)}) collective-permute-start(bf16[2,4,128,1024]{3,2,1,0:T(8,128)(2,1)} %get-tuple-element.184), channel_id=1, source_target_pairs={{0,1},{1,0},{2,3},{3,2},{4,5},{5,4},{6,7},{7,6},{8,9},{9,8},{10,11... | collective-permute-start | bytes 6291464 | tf_op jit(solution)/shard_map/ppermute | solution.py:760
  216.0 58.7 %collective-permute-start.28 = (bf16[2,4,128,1024]{3,2,1,0:T(8,128)(2,1)}, bf16[2,4,128,1024]{3,2,1,0:T(8,128)(2,1)}, u32[]{:S(2)}, u32[]{:S(2)}) collective-permute-start(bf16[2,4,128,1024]{3,2,1,0:T(8,128)(2,1)} %get-tuple-element.195), channel_id=1, source_target_pairs={{0,16},{16,0},{1,17},{17,1},{2,18},{18,2},{3,19},{19,3},{4,20},{20... | collective-permute-start | bytes 6291464 | tf_op jit(solution)/shard_map/ppermute | solution.py:760
  237.6 68.3 %all-to-all-start.3 = ((bf16[8,2,40,1024]{3,2,1,0:T(8,128)(2,1)}), bf16[8,2,40,1024]{3,2,1,0:T(8,128)(2,1)S(1)}, u32[]{:S(2)}, u32[]{:S(2)}) async-start(bf16[8,2,40,1024]{3,2,1,0:T(8,128)(2,1)} %bitcast.240), calls=%async_computation.3 | async-start | bytes 2621440 | tf_op jit(solution)/shard_map/all_to_all | solution.py:928
  263.9 59.9 %collective-permute-start.35 = (bf16[4,128,1024]{2,1,0:T(8,128)(2,1)}, bf16[4,128,1024]{2,1,0:T(8,128)(2,1)}, u32[]{:S(2)}, u32[]{:S(2)}) collective-permute-start(bf16[4,128,1024]{2,1,0:T(8,128)(2,1)} %get-tuple-element.321), channel_id=1, source_target_pairs={{0,16},{16,0},{1,17},{17,1},{2,18},{18,2},{3,19},{19,3},{4,20},{20... | collective-permute-start | bytes 3145736 | tf_op jit(solution)/shard_map/ppermute | solution.py:760
  280.5 46.0 %collective-permute-start.36 = (bf16[4,128,1024]{2,1,0:T(8,128)(2,1)}, bf16[4,128,1024]{2,1,0:T(8,128)(2,1)}, u32[]{:S(2)}, u32[]{:S(2)}) collective-permute-start(bf16[4,128,1024]{2,1,0:T(8,128)(2,1)} %get-tuple-element.319), channel_id=1, source_target_pairs={{0,1},{1,0},{2,3},{3,2},{4,5},{5,4},{6,7},{7,6},{8,9},{9,8},{10,11... | collective-permute-start | bytes 3145736 | tf_op jit(solution)/shard_map/ppermute | solution.py:760
  295.0 53.1 %collective-permute-start.44 = (bf16[2,1,640,256]{3,2,1,0:T(8,128)(2,1)}, bf16[2,1,640,256]{3,2,1,0:T(8,128)(2,1)}, u32[]{:S(2)}, u32[]{:S(2)}) collective-permute-start(bf16[2,1,640,256]{3,2,1,0:T(8,128)(2,1)} %bitcast.57.refs_6_), channel_id=1, source_target_pairs={{0,2},{2,0},{4,6},{6,4},{8,10},{10,8},{12,14},{14,12},{1,3},{3,1},... | collective-permute-start | bytes 1966088 | tf_op jit(solution)/shard_map/ppermute | solution.py:760
  303.0 45.7 %collective-permute-start.46 = (bf16[2,1,640,256]{3,2,1,0:T(8,128)(2,1)}, bf16[2,1,640,256]{3,2,1,0:T(8,128)(2,1)}, u32[]{:S(2)}, u32[]{:S(2)}) collective-permute-start(bf16[2,1,640,256]{3,2,1,0:T(8,128)(2,1)} %bitcast.262), channel_id=1, source_target_pairs={{0,2},{2,0},{4,6},{6,4},{8,10},{10,8},{12,14},{14,12},{1,3},{3,1},... | collective-permute-start | bytes 1966088 | tf_op jit(solution)/shard_map/ppermute | solution.py:760
  330.7 41.9 %collective-permute-start.43 = (bf16[2,3,640,256]{3,2,1,0:T(8,128)(2,1)S(1)}, bf16[2,3,640,256]{3,2,1,0:T(8,128)(2,1)}, u32[]{:S(2)}, u32[]{:S(2)}) collective-permute-start(bf16[2,3,640,256]{3,2,1,0:T(8,128)(2,1)S(1)} %copy-done.3), channel_id=1, source_target_pairs={{0,2},{2,0},{4,6},{6,4},{8,10},{10,8},{12,14},{14,12},{1,3},{3,1},... | collective-permute-start | bytes 5898248 | tf_op jit(solution)/shard_map/ppermute | solution.py:760
  368.1 54.9 %collective-permute-start.53 = (bf16[2,128,1024]{2,1,0:T(8,128)(2,1)}, bf16[2,128,1024]{2,1,0:T(8,128)(2,1)}, u32[]{:S(2)}, u32[]{:S(2)}) collective-permute-start(bf16[2,128,1024]{2,1,0:T(8,128)(2,1)} %get-tuple-element.316), channel_id=1, source_target_pairs={{0,12},{2,14},{4,8},{6,10},{8,4},{10,6},{12,0},{14,2},{1,13},{3,15... | collective-permute-start | bytes 1572872 | tf_op jit(solution)/shard_map/ppermute | solution.py:760
  372.5 57.7 %collective-permute-start.52 = (bf16[2,128,1024]{2,1,0:T(8,128)(2,1)}, bf16[2,128,1024]{2,1,0:T(8,128)(2,1)}, u32[]{:S(2)}, u32[]{:S(2)}) collective-permute-start(bf16[2,128,1024]{2,1,0:T(8,128)(2,1)} %get-tuple-element.317), channel_id=1, source_target_pairs={{0,8},{2,10},{4,12},{6,14},{8,0},{10,2},{12,4},{14,6},{1,9},{3,11}... | collective-permute-start | bytes 1572872 | tf_op jit(solution)/shard_map/ppermute | solution.py:760
  395.0 35.6 %collective-permute-start.51 = (bf16[2,128,1024]{2,1,0:T(8,128)(2,1)}, bf16[2,128,1024]{2,1,0:T(8,128)(2,1)S(1)}, u32[]{:S(2)}, u32[]{:S(2)}) collective-permute-start(bf16[2,128,1024]{2,1,0:T(8,128)(2,1)} %get-tuple-element.315), channel_id=1, source_target_pairs={{0,4},{2,6},{4,0},{6,2},{8,12},{10,14},{12,8},{14,10},{1,5},{3,7},... | collective-permute-start | bytes 1572872 | tf_op jit(solution)/shard_map/ppermute | solution.py:760
  408.3 38.9 %collective-permute-start.61 = (bf16[2,128,512]{2,1,0:T(8,128)(2,1)}, bf16[2,128,512]{2,1,0:T(8,128)(2,1)}, u32[]{:S(2)}, u32[]{:S(2)}) collective-permute-start(bf16[2,128,512]{2,1,0:T(8,128)(2,1)} %get-tuple-element.328), channel_id=1, source_target_pairs={{0,12},{2,14},{4,8},{6,10},{8,4},{10,6},{12,0},{14,2},{1,13},{3,15... | collective-permute-start | bytes 786440 | tf_op jit(solution)/shard_map/ppermute | solution.py:760
  451.1 34.9 %collective-permute-start.58 = (f32[11,128]{1,0:T(8,128)}, f32[11,128]{1,0:T(8,128)}, u32[]{:S(2)}, u32[]{:S(2)}) collective-permute-start(f32[11,128]{1,0:T(8,128)} %bitcast.228), channel_id=1, source_target_pairs={{0,12},{2,14},{4,8},{6,10},{8,4},{10,6},{12,0},{14,2},{1,13},{3,15... | collective-permute-start | bytes 16904 | tf_op jit(solution)/shard_map/ppermute | solution.py:760
  (92 other events, 1246.1 us)
